TPU v7x, 32 devices: a whole 2x2x4 slice. The times are simulated.
32 devices in a mesh: blk: 16 (over z, x, core), mp: 2 (over y).
Axes of the slice: x: 2, y: 2, z: 4, core: 2. Of those that a mesh axis runs over, the one named last changes fastest.
Arguments:
- features: bfloat16 [16, 2, 2, 256, 1280], P('blk', None, None, None, 'mp'), may hold values from -62 to 62
- w_query: bfloat16 [1280, 1280], P(None, 'mp'), may hold values from -2 to 2
- w_key: bfloat16 [1280, 1280], P(None, 'mp'), may hold values from -2 to 2
- w_value: bfloat16 [1280, 1280], P(None, 'mp'), may hold values from -0.15625 to 0.15625
- w_out: bfloat16 [1280, 1280], P('mp'), may hold values from -0.15625 to 0.15625
- w_head: bfloat16 [1280, 64], replicated, may hold values from -0.15625 to 0.15625
- offsets: int32 [16], P('blk'), may hold values from 0 to 255, as said below
- blend_mask: int32 [16, 64, 64], P('blk'), may hold values from 1 to 4
Outputs:
- panorama: float32 [2, 256, 256], P(None, 'blk')
Inputs may be any that keep to these rules, and one draw needn't show every extreme that they name: offsets[w] = 16 * w + s for one s shared by all windows, 0 <= s < 16.
All inputs are finite; a program needn't handle non-finite values.
Results may differ from a plain program's by a relative error of at most 0.0064.
Values may be sent and summed in bfloat16 or wider, within the bound.
No kernel may reach another device: no remote copies, remote signals or barrier semaphores. Data moves between devices by JAX's collectives and lax.ppermute only.
A program may use at most 64 MiB of HBM per device.

v0:
```python
import jax
import jax.numpy as jnp
from jax import lax
from jax.sharding import PartitionSpec as P

HEAD = 64
GRID = 16
PATCH = 4
CHAN = 4
STRIDE = 16
WINDOW = 64
OUTW = 64


guidance = 3.0


def shifted(x, axis, by):
    count = lax.axis_size(axis)
    return lax.ppermute(x, axis, [(i, (i + by) % count) for i in range(count)])


def shards(features, w_query, w_key, w_value, w_out, w_head, offsets, blend_mask):
    gathered = lax.all_gather(features, "mp", axis=4, tiled=True)
    batch_count = gathered.shape[1]
    token_count = gathered.shape[3]
    model_width = gathered.shape[4]
    sequences = batch_count * 2
    local_heads = w_query.shape[1] // HEAD
    token_plain = gathered.reshape(-1, model_width)
    token_rows = token_plain.astype(jnp.float32)
    row_mean = jnp.mean(token_rows, axis=1, keepdims=True)
    centred = token_rows - row_mean
    row_var = jnp.mean(centred * centred, axis=1, keepdims=True)
    normed = (centred * lax.rsqrt(row_var + 1e-05)).astype(jnp.bfloat16)
    queries = (
        jnp.dot(normed, w_query, preferred_element_type=jnp.float32)
        .astype(jnp.bfloat16)
        .reshape(sequences, token_count, local_heads, HEAD)
    )
    key_rows = (
        jnp.dot(normed, w_key, preferred_element_type=jnp.float32)
        .astype(jnp.bfloat16)
        .reshape(sequences, token_count, local_heads, HEAD)
    )
    value_rows = (
        jnp.dot(normed, w_value, preferred_element_type=jnp.float32)
        .astype(jnp.bfloat16)
        .reshape(sequences, token_count, local_heads, HEAD)
    )
    scores = (
        jnp.einsum("sqhd,skhd->shqk", queries, key_rows, preferred_element_type=jnp.float32)
        / HEAD**0.5
    )
    scores = scores - jnp.max(scores, axis=3, keepdims=True)
    expont = jnp.exp(scores)
    attend = (expont / jnp.sum(expont, axis=3, keepdims=True)).astype(jnp.bfloat16)
    context = jnp.einsum(
        "shqk,skhd->sqhd", attend, value_rows, preferred_element_type=jnp.float32
    ).astype(jnp.bfloat16)
    context = context.reshape(-1, local_heads * HEAD)
    partial_value = jnp.dot(context, w_out, preferred_element_type=jnp.float32)
    head_weight = w_head.astype(jnp.float32)
    head_part = jnp.dot(partial_value, head_weight, precision=lax.Precision.HIGHEST)
    tok_out = lax.psum(head_part.astype(jnp.bfloat16), "mp").astype(jnp.float32) + jnp.dot(
        token_plain, w_head, preferred_element_type=jnp.float32
    )
    tok_out = tok_out.reshape(batch_count, 2, token_count, OUTW)
    guided = tok_out[:, 0] + guidance * (tok_out[:, 1] - tok_out[:, 0])
    spread = guided.reshape(batch_count, GRID, GRID, PATCH, PATCH, CHAN).transpose(0, 2, 3, 1, 4, 5)
    spread = spread.reshape(batch_count, WINDOW, WINDOW * CHAN)
    weight = blend_mask[0].astype(jnp.float32)
    weighted = spread * jnp.repeat(weight, CHAN, axis=1)[None]
    shift_cols = offsets[0] - STRIDE * lax.axis_index("blk")
    zero_index = jnp.zeros((), jnp.int32)
    frame_num = lax.dynamic_update_slice(
        jnp.zeros((batch_count, WINDOW + STRIDE, WINDOW * CHAN), jnp.float32),
        weighted,
        (zero_index, shift_cols, zero_index),
    )
    frame_weight = lax.dynamic_update_slice(
        jnp.zeros((WINDOW + STRIDE, WINDOW), jnp.float32), weight, (shift_cols, zero_index)
    )
    piece_count = WINDOW // STRIDE + 1
    numerators = [frame_num[:, j * STRIDE : (j + 1) * STRIDE] for j in range(piece_count)]
    weight_pieces = [frame_weight[j * STRIDE : (j + 1) * STRIDE] for j in range(piece_count)]
    blended_num = numerators[0]
    blended_weight = weight_pieces[0]
    for j in range(1, piece_count):
        arrived = shifted((numerators[j], weight_pieces[j]), "blk", j)
        blended_num = blended_num + arrived[0]
        blended_weight = blended_weight + arrived[1]
    return blended_num / jnp.repeat(blended_weight, CHAN, axis=1)[None]


def solution(mesh):
    return jax.shard_map(
        shards,
        mesh=mesh,
        in_specs=(
            P("blk", None, None, None, "mp"),
            P(None, "mp"),
            P(None, "mp"),
            P(None, "mp"),
            P("mp", None),
            P(),
            P("blk"),
            P("blk", None, None),
        ),
        out_specs=P(None, "blk", None),
        check_vma=False,
    )
```

profile of v0, /device:TPU:0, one launch (start us, length us, event | category | flops | bytes accessed | tf_op | source)
XLA Modules:
  0.0 160.9 jit_solution(14204713652645674457)
XLA Ops:
  9.3 41.4 %all-gather.2.cloned.1.call-done = bf16[1,2,2,256,1280]{4,3,2,1,0:T(8,128)(2,1)} async-done(((bf16[1,2,2,256,640]{4,3,2,1,0:T(8,128)(2,1)}), bf16[1,2,2,256,1280]{4,3,2,1,0:T(8,128)(2,1)}) %all-gather.2.cloned.1.call-update) | async-done | bytes 2621456 | tf_op jit(solution)/shard_map/all_gather | solution.py:24
  50.6 2.3 %convert_reduce_fusion = f32[2,2,256]{2,1,0:T(2,128)S(1)} fusion(bf16[1,2,2,256,1280]{4,3,2,1,0:T(8,128)(2,1)} %all-gather.2.cloned.1.call-done), kind=kLoop, calls=%fused_computation.6 | loop fusion | flops 2620416 | bytes 2625536 | tf_op jit(solution)/shard_map/reduce_sum | solution.py:32
  54.7 1.5 copy-done.2
  56.2 2.2 %convolution_convert_fusion = bf16[1024,640]{1,0:T(8,128)(2,1)S(1)} fusion(bf16[1024,1280]{1,0:T(8,128)(2,1)S(1)} %multiply_convert_fusion, bf16[1280,640]{1,0:T(8,128)(2,1)S(1)} %copy-done.6), kind=kOutput, calls=%fused_computation.13 | convolution fusion | flops 1678376960 | bytes 5570560 | tf_op jit(solution)/shard_map/dot_general | solution.py:42
  58.5 1.5 copy.35
  60.0 2.9 %reshape.66 = bf16[4,256,10,64]{1,0,3,2:T(4,128)(2,1)S(1)} reshape(bf16[1024,640]{0,1:T(8,128)(2,1)} %copy.35) | data formatting | bytes 2621440 | tf_op jit(solution)/shard_map/reshape | solution.py:44
  62.9 5.6 %convolution_convert_fusion.1 = bf16[1024,640]{1,0:T(8,128)(2,1)} fusion(bf16[1024,1280]{1,0:T(8,128)(2,1)} %copy-done.2, bf16[1280,640]{1,0:T(8,128)(2,1)} %param.9), kind=kOutput, calls=%fused_computation.14 | convolution fusion | flops 1678376960 | bytes 5570560 | tf_op jit(solution)/shard_map/dot_general | solution.py:37
  68.5 3.3 %convolution_convert_fusion.2 = bf16[1024,640]{1,0:T(8,128)(2,1)} fusion(bf16[1024,1280]{1,0:T(8,128)(2,1)S(1)} %copy-done.3, bf16[1280,640]{1,0:T(8,128)(2,1)S(1)} %copy-done.7), kind=kOutput, calls=%fused_computation.15 | convolution fusion | flops 1678376960 | bytes 5570560 | tf_op jit(solution)/shard_map/dot_general | solution.py:47
  71.8 2.5 %copy.33 = bf16[1024,640]{0,1:T(8,128)(2,1)} copy(bf16[1024,640]{1,0:T(8,128)(2,1)} %convolution_convert_fusion.2) | data formatting | bytes 2621440 | tf_op jit(solution)/shard_map/convert_element_type | solution.py:48
  74.3 3.8 %reshape.64 = bf16[4,256,10,64]{1,0,3,2:T(4,128)(2,1)} reshape(bf16[1024,640]{0,1:T(8,128)(2,1)} %copy.33) | data formatting | bytes 2621440 | tf_op jit(solution)/shard_map/reshape | solution.py:49
  78.0 2.5 %copy.34 = bf16[1024,640]{0,1:T(8,128)(2,1)} copy(bf16[1024,640]{1,0:T(8,128)(2,1)} %convolution_convert_fusion.1) | data formatting | bytes 2621440 | tf_op jit(solution)/shard_map/convert_element_type | solution.py:38
  80.5 3.8 %reshape.65 = bf16[4,256,10,64]{1,0,3,2:T(4,128)(2,1)} reshape(bf16[1024,640]{0,1:T(8,128)(2,1)} %copy.34) | data formatting | bytes 2621440 | tf_op jit(solution)/shard_map/reshape | solution.py:39
  84.3 2.9 %fusion.11 = f32[4,10,256,256]{2,3,1,0:T(8,128)S(1)} fusion(bf16[4,256,10,64]{1,0,3,2:T(4,128)(2,1)S(1)} %reshape.66, bf16[4,256,10,64]{1,0,3,2:T(4,128)(2,1)} %reshape.65), kind=kOutput, calls=%fused_computation.18 | convolution fusion | flops 335544320 | bytes 13107200 | tf_op jit(solution)/shard_map/sqhd,skhd->shqk/dot_general | solution.py:52
  87.2 5.4 %fusion.23 = (f32[4,10,256]{2,1,0:T(8,128)S(1)}, f32[4,10,256,256]{2,3,1,0:T(8,128)}) fusion(f32[4,10,256,256]{2,3,1,0:T(8,128)S(1)} %fusion.11), kind=kOutput, calls=%fused_computation.39 | output fusion | flops 10486015 | bytes 21012480 | tf_op jit(solution)/shard_map/sub | solution.py:55
  92.6 4.9 %fusion.9 = bf16[4,256,10,64]{1,3,2,0:T(8,128)(2,1)S(1)} fusion(f32[4,10,256,256]{2,3,1,0:T(8,128)} %get-tuple-element.19, f32[4,10,256]{2,1,0:T(8,128)S(1)} %get-tuple-element.18, bf16[4,256,10,64]{1,0,3,2:T(4,128)(2,1)S(1)} %copy-done.4), kind=kOutput, calls=%fused_computation.16 | convolution fusion | flops 341442560 | bytes 13148160 | tf_op jit(solution)/shard_map/shqk,skhd->sqhd/dot_general | solution.py:58
  97.5 1.0 copy.40
  98.9 2.3 %fusion.24 = f32[1024,1280]{1,0:T(8,128)S(1)} fusion(bf16[1024,640]{0,1:T(8,128)(2,1)S(1)} %bitcast.57, bf16[640,1280]{1,0:T(8,128)(2,1)S(1)} %copy-done), kind=kOutput, calls=%fused_computation.40 | convolution fusion | flops 1677721600 | bytes 8192000 | tf_op jit(solution)/shard_map/dot_general | solution.py:62
  101.2 3.5 %convolution_convert_fusion.3 = bf16[1024,64]{0,1:T(8,128)(2,1)} fusion(f32[1024,1280]{1,0:T(8,128)S(1)} %fusion.24, bf16[1280,64]{0,1:T(8,128)(2,1)S(1)} %copy-done.5), kind=kOutput, calls=%fused_computation.22 | convolution fusion | flops 1006698496 | bytes 5537792 | tf_op jit(solution)/shard_map/dot_general | solution.py:64
  105.6 0.9 collective-permute-start.4
  106.6 1.5 collective-permute-start.5
  108.0 1.5 collective-permute-start.7
  109.6 16.8 %all-reduce.2.cloned.1.call-done = bf16[1024,64]{0,1:T(8,128)(2,1)} async-done(((bf16[1024,64]{0,1:T(8,128)(2,1)}), bf16[1024,64]{0,1:T(8,128)(2,1)}) %all-reduce.2.cloned.1.call-update) | async-done | bytes 131088 | tf_op jit(solution)/shard_map/psum | solution.py:65
  126.3 2.6 %convolution_add_fusion = f32[1024,64]{0,1:T(8,128)S(1)} fusion(bf16[1024,1280]{1,0:T(8,128)(2,1)} %bitcast.55, bf16[1280,64]{0,1:T(8,128)(2,1)S(1)} %copy-done.5, bf16[1024,64]{0,1:T(8,128)(2,1)} %all-reduce.2.cloned.1.call-done), kind=kOutput, calls=%fused_computation.21 | convolution fusion | flops 167903232 | bytes 3178496 | tf_op jit(solution)/shard_map/dot_general | solution.py:65
  129.5 1.3 squeeze.11
  130.8 1.3 squeeze.12
  132.1 1.7 %add_bitcast_fusion = f32[2,16,4,16,4,4]{1,3,5,4,2,0:T(8,128)S(1)} fusion(f32[2,16,16,4,4,4]{2,1,5,4,3,0:T(8,128)} %squeeze.11, f32[2,16,16,4,4,4]{2,1,5,4,3,0:T(8,128)} %squeeze.12), kind=kLoop, calls=%fused_computation.23 | loop fusion | flops 98304 | bytes 393216 | tf_op jit(solution)/shard_map/transpose | solution.py:70
  133.8 4.7 %copy.43 = f32[2,16,4,16,4,4]{2,1,5,4,3,0:T(8,128)} copy(f32[2,16,4,16,4,4]{1,3,5,4,2,0:T(8,128)S(1)} %add_bitcast_fusion) | data formatting | bytes 262144 | tf_op jit(solution)/shard_map/transpose | solution.py:70
  138.6 3.6 %reshape.69 = f32[2,64,256]{1,2,0:T(8,128)S(1)} reshape(f32[2,16,4,16,4,4]{2,1,5,4,3,0:T(8,128)} %copy.43) | data formatting | bytes 262144 | tf_op jit(solution)/shard_map/reshape | solution.py:71
  142.9 1.5 collective-permute-start.3
  144.5 2.3 %collective-permute-start.2 = (f32[2,16,256]{2,1,0:T(8,128)S(1)}, f32[2,16,256]{2,1,0:T(8,128)S(1)}, u32[]{:S(2)}, u32[]{:S(2)}) collective-permute-start(f32[2,16,256]{2,1,0:T(8,128)S(1)} %get-tuple-element.9), channel_id=1, source_target_pairs={{0,6},{2,8},{4,10},{6,12},{8,14},{10,16},{12,18},{14,20},{16,22},{... | collective-permute-start | bytes 98312 | tf_op jit(solution)/shard_map/ppermute | solution.py:20
  146.8 1.5 collective-permute-start.1
  149.6 3.8 %collective-permute-done.1 = f32[2,16,256]{2,1,0:T(8,128)S(1)} collective-permute-done((f32[2,16,256]{2,1,0:T(8,128)S(1)}, f32[2,16,256]{2,1,0:T(8,128)S(1)}, u32[]{:S(2)}, u32[]{:S(2)}) %collective-permute-start.1) | collective-permute-done | bytes 32800 | tf_op jit(solution)/shard_map/ppermute | solution.py:20
  (60 shorter events, 8.2 us)
Async XLA Ops:
  6.5 92.3 %copy-start = (bf16[640,1280]{1,0:T(8,128)(2,1)S(1)}, bf16[640,1280]{1,0:T(8,128)(2,1)}, u32[]{:S(2)}) copy-start(bf16[640,1280]{1,0:T(8,128)(2,1)} %param.12) | copy-start | bytes 4915204
  6.5 44.1 %all-gather.2.cloned.1.call-start = ((), (), s32[]{:S(2)}) async-start(), calls=%async_computation | async-start | bytes 3932160 | tf_op jit(solution)/shard_map/all_gather | solution.py:24
  7.3 119.1 %all-reduce.2.cloned.1.call-start = ((), (), s32[]{:S(2)}) async-start(), calls=%async_computation.1 | async-start | bytes 262144 | tf_op jit(solution)/shard_map/psum | solution.py:65
  50.6 2.5 %copy-start.1 = (bf16[1,2,2,256,1280]{4,3,2,1,0:T(8,128)(2,1)S(1)}, bf16[1,2,2,256,1280]{4,3,2,1,0:T(8,128)(2,1)}, u32[]{:S(2)}) copy-start(bf16[1,2,2,256,1280]{4,3,2,1,0:T(8,128)(2,1)} %all-gather.2.cloned.1.call-done) | copy-start | bytes 7864324
  54.0 2.2 %copy-start.6 = (bf16[1280,640]{1,0:T(8,128)(2,1)S(1)}, bf16[1280,640]{1,0:T(8,128)(2,1)}, u32[]{:S(2)}) copy-start(bf16[1280,640]{1,0:T(8,128)(2,1)} %param.10) | copy-start | bytes 4915204
  54.7 1.5 copy-start.2
  62.8 5.6 %copy-start.3 = (bf16[1024,1280]{1,0:T(8,128)(2,1)S(1)}, bf16[1024,1280]{1,0:T(8,128)(2,1)}, u32[]{:S(2)}) copy-start(bf16[1024,1280]{1,0:T(8,128)(2,1)} %copy-done.2) | copy-start | bytes 7864324
  62.9 5.6 %copy-start.7 = (bf16[1280,640]{1,0:T(8,128)(2,1)S(1)}, bf16[1280,640]{1,0:T(8,128)(2,1)}, u32[]{:S(2)}) copy-start(bf16[1280,640]{1,0:T(8,128)(2,1)} %param.11) | copy-start | bytes 4915204
  87.2 5.5 %copy-start.4 = (bf16[4,256,10,64]{1,0,3,2:T(4,128)(2,1)S(1)}, bf16[4,256,10,64]{1,0,3,2:T(4,128)(2,1)}, u32[]{:S(2)}) copy-start(bf16[4,256,10,64]{1,0,3,2:T(4,128)(2,1)} %reshape.64) | copy-start | bytes 3932164
  98.9 2.3 %copy-start.5 = (bf16[1280,64]{0,1:T(8,128)(2,1)S(1)}, bf16[1280,64]{0,1:T(8,128)(2,1)}, u32[]{:S(2)}) copy-start(bf16[1280,64]{0,1:T(8,128)(2,1)} %param.13) | copy-start | bytes 491524
  104.8 38.1 %collective-permute-start.6 = (f32[16,64]{1,0:T(8,128)S(1)}, f32[16,64]{1,0:T(8,128)S(1)}, u32[]{:S(2)}, u32[]{:S(2)}) collective-permute-start(f32[16,64]{1,0:T(8,128)S(1)} %copy.59), channel_id=1, source_target_pairs={{0,6},{2,8},{4,10},{6,12},{8,14},{10,16},{12,18},{14,20},{16,22},{... | collective-permute-start | bytes 12296 | tf_op jit(solution)/shard_map/ppermute | solution.py:20
  105.6 38.8 %collective-permute-start.4 = (f32[16,64]{1,0:T(8,128)S(1)}, f32[16,64]{1,0:T(8,128)S(1)}, u32[]{:S(2)}, u32[]{:S(2)}) collective-permute-start(f32[16,64]{1,0:T(8,128)S(1)} %copy.57), channel_id=1, source_target_pairs={{0,2},{2,4},{4,6},{6,8},{8,10},{10,12},{12,14},{14,16},{16,18},{18... | collective-permute-start | bytes 12296 | tf_op jit(solution)/shard_map/ppermute | solution.py:20
  106.6 40.2 %collective-permute-start.5 = (f32[16,64]{1,0:T(8,128)S(1)}, f32[16,64]{1,0:T(8,128)S(1)}, u32[]{:S(2)}, u32[]{:S(2)}) collective-permute-start(f32[16,64]{1,0:T(8,128)S(1)} %copy.58), channel_id=1, source_target_pairs={{0,4},{2,6},{4,8},{6,10},{8,12},{10,14},{12,16},{14,18},{16,20},{1... | collective-permute-start | bytes 12296 | tf_op jit(solution)/shard_map/ppermute | solution.py:20
  108.0 40.3 %collective-permute-start.7 = (f32[16,64]{0,1:T(8,128)S(1)}, f32[16,64]{0,1:T(8,128)S(1)}, u32[]{:S(2)}, u32[]{:S(2)}) collective-permute-start(f32[16,64]{0,1:T(8,128)S(1)} %get-tuple-element.11), channel_id=1, source_target_pairs={{0,8},{2,10},{4,12},{6,14},{8,16},{10,18},{12,20},{14,22},{16,24},... | collective-permute-start | bytes 12296 | tf_op jit(solution)/shard_map/ppermute | solution.py:20
  142.8 6.1 %collective-permute-start = (f32[2,16,256]{2,1,0:T(8,128)S(1)}, f32[2,16,256]{2,1,0:T(8,128)S(1)}, u32[]{:S(2)}, u32[]{:S(2)}) collective-permute-start(f32[2,16,256]{2,1,0:T(8,128)S(1)} %get-tuple-element.7), channel_id=1, source_target_pairs={{0,2},{2,4},{4,6},{6,8},{8,10},{10,12},{12,14},{14,16},{16,18},{18... | collective-permute-start | bytes 98312 | tf_op jit(solution)/shard_map/ppermute | solution.py:20
  142.9 6.0 %collective-permute-start.3 = (f32[2,16,256]{2,1,0:T(8,128)S(1)}, f32[2,16,256]{2,1,0:T(8,128)S(1)}, u32[]{:S(2)}, u32[]{:S(2)}) collective-permute-start(f32[2,16,256]{2,1,0:T(8,128)S(1)} %get-tuple-element.8), channel_id=1, source_target_pairs={{0,8},{2,10},{4,12},{6,14},{8,16},{10,18},{12,20},{14,22},{16,24},... | collective-permute-start | bytes 98312 | tf_op jit(solution)/shard_map/ppermute | solution.py:20
  144.5 5.1 %collective-permute-start.2 = (f32[2,16,256]{2,1,0:T(8,128)S(1)}, f32[2,16,256]{2,1,0:T(8,128)S(1)}, u32[]{:S(2)}, u32[]{:S(2)}) collective-permute-start(f32[2,16,256]{2,1,0:T(8,128)S(1)} %get-tuple-element.9), channel_id=1, source_target_pairs={{0,6},{2,8},{4,10},{6,12},{8,14},{10,16},{12,18},{14,20},{16,22},{... | collective-permute-start | bytes 98312 | tf_op jit(solution)/shard_map/ppermute | solution.py:20
  146.8 6.6 %collective-permute-start.1 = (f32[2,16,256]{2,1,0:T(8,128)S(1)}, f32[2,16,256]{2,1,0:T(8,128)S(1)}, u32[]{:S(2)}, u32[]{:S(2)}) collective-permute-start(f32[2,16,256]{2,1,0:T(8,128)S(1)} %get-tuple-element.10), channel_id=1, source_target_pairs={{0,4},{2,6},{4,8},{6,10},{8,12},{10,14},{12,16},{14,18},{16,20},{1... | collective-permute-start | bytes 98312 | tf_op jit(solution)/shard_map/ppermute | solution.py:20
Sparse Core Ops, SparseCore 0:
  8.9 41.7 all-gather.1
  104.8 21.5 all-reduce.1
where the time goes:
time: 161 us
  waiting for transfers between devices  63.8 us (40%)
  local copies, waits for them, and re-layouts  33 us (20%)
  matrix products  27.3 us (17%)
  between operations  14.4 us (9%)
  other arithmetic  12.4 us (8%)
  starting transfers between devices  9.98 us (6%)
    all_gather x1, waiting for transfers between devices, shards(): gathered = lax.all_gather(features, 'mp', axis=4, tiled=True)  41.4 us
    psum x1, waiting for transfers between devices, shards(): lax.psum(head_part.astype(jnp.bfloat16), 'mp').astype(jnp.float32)  16.8 us
    ppermute x8, starting transfers between devices, shifted(): return lax.ppermute(x, axis, [(i, (i + by) % count) for i in range(count)])  9.94 us
    dot_general x1, matrix products, shards(): jnp.dot(normed, w_query, preferred_element_type=jnp.float32)  5.62 us
    sub x1, other arithmetic, shards(): scores = scores - jnp.max(scores, axis=3, keepdims=True)  5.44 us
    ppermute x8, waiting for transfers between devices, shifted(): return lax.ppermute(x, axis, [(i, (i + by) % count) for i in range(count)])  4.95 us
    dot_general x1, matrix products, shards(): jnp.einsum('shqk,skhd->sqhd', attend, value_rows, preferred_element_type=...  4.91 us
    transpose x1, local copies, waits for them, and re-layouts, shards(): guided.reshape(batch_count, GRID, GRID, PATCH, PATCH, CHAN)  4.74 us
  transfers between devices with their start and end apart: 10, of which 5 were waited for; matrix products, arithmetic and copies ran while one was open for 11% of the time, Pallas kernels for 0%

commit v1 on v0

v1 whole, which is shorter than its diff:
```python
import functools
import math

import jax
import jax.numpy as jnp
from jax import lax
from jax.experimental import pallas as pl
from jax.experimental.pallas import tpu as pltpu
from jax.sharding import PartitionSpec as P

HEAD = 64
GRID = 16
PATCH = 4
CHAN = 4
STRIDE = 16
WINDOW = 64
OUTW = 64

guidance = 3.0

F32 = jnp.float32
BF16 = jnp.bfloat16
LAT = WINDOW * CHAN
PIECES = WINDOW // STRIDE + 1
FRAME = PIECES * STRIDE
PAIR = 2 * HEAD
LANES = 128
HALVES = LAT // LANES
NT = (((1,), (1,)), ((), ()))


def dot(a, b):
    return jnp.dot(a, b, preferred_element_type=F32)


def split2(x):
    high = x.astype(BF16)
    return high, (x - high.astype(F32)).astype(BF16)


def iota(shape, axis):
    return lax.broadcasted_iota(jnp.int32, shape, axis)


def prepare(
    place,
    features,
    w_query,
    w_key,
    w_value,
    w_out,
    w_head,
    mask,
    own_acc,
    own_mean,
    own_square,
    column_sum,
    far_weights,
    out_weights,
    direct,
    spread_map,
    mask_tile,
    mask_keep,
    mask_send,
    mask_frame,
):
    half = features.shape[-1]
    width = w_query.shape[1]
    sequences = own_acc.shape[0]
    tokens = own_acc.shape[1]
    side = place[0]
    shift = place[1]
    near = pl.ds(pl.multiple_of(side * half, 128), half)
    far = pl.ds(pl.multiple_of((1 - side) * half, 128), half)
    repeat_map = (iota((WINDOW, LAT), 1) // CHAN == iota((WINDOW, LAT), 0)).astype(BF16)
    wide = dot(mask[0].astype(F32).astype(BF16), repeat_map)
    for h in range(HALVES):
        lanes = slice(h * LANES, (h + 1) * LANES)
        mask_frame[h, :WINDOW] = wide[:, lanes]
        mask_frame[h, WINDOW:] = jnp.zeros((FRAME - WINDOW, LANES), F32)
        for a in range(PATCH):
            places = slice(a * LAT + h * LANES, a * LAT + (h + 1) * LANES)
            mask_tile[:, places] = mask_frame[h, pl.ds(a, GRID, stride=PATCH), :]
        rolled = pltpu.roll(mask_frame[h], shift, 0)
        for t in range(PIECES):
            piece = rolled[t * STRIDE : (t + 1) * STRIDE]
            (mask_send if t % 2 else mask_keep)[t // 2, :, lanes] = piece
    part = OUTW // PATCH
    rows, columns = iota((2 * OUTW, PATCH * LAT), 0) % OUTW, iota((2 * OUTW, PATCH * LAT), 1)
    spread_map[...] = (
        (rows // part == columns // LAT) & (rows % part == columns % part)
    ).astype(BF16)
    ones = jnp.ones((8, w_query.shape[0]), BF16)
    for j, w in enumerate((w_query, w_key, w_value)):
        column_sum[:, j * width : (j + 1) * width] = dot(ones, w[...])
        far_weights[:, j * width : (j + 1) * width] = w[far, :]
    high, low = split2(dot(w_out[...], w_head[...]))
    out_weights[:half] = high
    out_weights[half:] = low
    for s in range(sequences):
        x = features[0, s // 2, s % 2]
        xf = x.astype(F32)
        mean = jnp.mean(xf, axis=1, keepdims=True)
        centred = xf - mean
        own_mean[s] = mean
        own_square[s] = jnp.sum(centred * centred, axis=1, keepdims=True)
        direct[s] = dot(x, w_head[near, :])
        for j, w in enumerate((w_query, w_key, w_value)):
            own_acc[s, :, j * width : (j + 1) * width] = dot(x, w[near, :])


def attend(
    s,
    last,
    place,
    arrived,
    own_acc,
    own_mean,
    own_square,
    column_sum,
    far_weights,
    out_weights,
    direct,
    *rest,
):
    if s % 2 == 0:
        guided_out, q_even, q_odd, keys, values, context = rest
    else:
        spread_map, mask_tile, guided_in = rest[:3]
        rest = rest[3:]
        if last:
            before = rest[: 2 * (s // 2)]
            rest = rest[2 * (s // 2) :]
        keep, send, frame, q_even, q_odd, keys, values, context = rest
    half = arrived.shape[-1]
    width = far_weights.shape[1] // 3
    tokens = arrived.shape[-2]
    x = arrived[...]
    xf = x.astype(F32)
    far_mean = jnp.mean(xf, axis=1, keepdims=True)
    centred = xf - far_mean
    far_square = jnp.sum(centred * centred, axis=1, keepdims=True)
    near_mean = own_mean[s]
    gap = near_mean - far_mean
    mean = 0.5 * (near_mean + far_mean)
    var = (own_square[s] + far_square + gap * gap * (0.5 * half)) / (2.0 * half)
    scale = lax.rsqrt(var + 1e-05)
    offset = mean * scale

    def project(j):
        columns = slice(j * width, (j + 1) * width)
        total = own_acc[s, :, columns] + dot(x, far_weights[:, columns])
        return total, column_sum[0:1, columns]

    factor = math.log2(math.e) / HEAD**0.5
    total, sums = project(0)
    queries = total * (scale * factor) - (offset * factor) * sums
    even = iota((1, width), 1) % PAIR < HEAD
    q_even[...] = jnp.where(even, queries, 0.0).astype(BF16)
    q_odd[...] = jnp.where(even, 0.0, queries).astype(BF16)
    total, sums = project(1)
    keys[...] = (total * scale - offset * sums).astype(BF16)
    total, sums = project(2)
    values[...] = (total * scale - offset * sums).astype(BF16)
    first = iota((1, PAIR), 1) < HEAD
    ones = jnp.ones((tokens, PAIR), BF16)
    none = jnp.zeros((tokens, PAIR), BF16)
    ones_even = jnp.where(first, ones, none)
    ones_odd = jnp.where(first, none, ones)
    for p in range(width // PAIR):
        columns = slice(p * PAIR, (p + 1) * PAIR)
        k = keys[:, columns]
        v = values[:, columns]
        probs = []
        for q in (q_even, q_odd):
            scores = lax.dot_general(q[:, columns], k, NT, preferred_element_type=F32)
            top = jnp.max(scores, axis=1, keepdims=True)
            probs.append(jnp.exp2(scores - top).astype(BF16))
        stacked = jnp.concatenate(
            [
                jnp.concatenate([jnp.where(first, v, none), ones_even], axis=1),
                jnp.concatenate([jnp.where(first, none, v), ones_odd], axis=1),
            ],
            axis=0,
        )
        both = dot(jnp.concatenate(probs, axis=1), stacked)
        context[:, columns] = (both[:, :PAIR] / both[:, PAIR:]).astype(BF16)
    ctx = context[...]
    out = dot(ctx, out_weights[:width]) + dot(ctx, out_weights[width:]) + direct[s]
    if s % 2 == 0:
        guided_out[...] = (1.0 - guidance) * out
        return
    guided = guidance * out + guided_in[...]
    tiled = dot(jnp.concatenate(split2(guided), axis=1), spread_map[...])
    lane_row = iota((1, PATCH * LAT), 1) % LAT // (LAT // GRID)
    spread = tiled[:GRID]
    for r in range(1, GRID):
        spread = jnp.where(lane_row == r, tiled[r * GRID : (r + 1) * GRID], spread)
    spread = spread * mask_tile[...]
    shift = place[1]
    slot = s // 2 if last else 0
    if last:
        for b in range(slot):
            keep[b] = before[2 * b][0]
            send[b] = before[2 * b + 1][0]
    for h in range(HALVES):
        lanes = slice(h * LANES, (h + 1) * LANES)
        for a in range(PATCH):
            places = slice(a * LAT + h * LANES, a * LAT + (h + 1) * LANES)
            frame[h, pl.ds(a, GRID, stride=PATCH), :] = spread[:, places]
        frame[h, WINDOW:] = jnp.zeros((FRAME - WINDOW, LANES), F32)
        rolled = pltpu.roll(frame[h], shift, 0)
        for t in range(PIECES):
            piece = rolled[t * STRIDE : (t + 1) * STRIDE]
            (send if t % 2 else keep)[slot, t // 2, :, lanes] = piece


def in_vmem(shape, dtype):
    return pltpu.VMEM(shape, dtype)


def call(kernel, name, args, outs, scratch, flops, limit):
    specs = [pl.BlockSpec(memory_space=pltpu.SMEM)]
    specs += [pl.BlockSpec(memory_space=pltpu.VMEM)] * (len(args) - 1)
    return pl.pallas_call(
        kernel,
        out_shape=[in_vmem(shape, dtype) for shape, dtype in outs],
        in_specs=specs,
        out_specs=[pl.BlockSpec(memory_space=pltpu.VMEM)] * len(outs),
        scratch_shapes=scratch,
        compiler_params=pltpu.CompilerParams(vmem_limit_bytes=limit),
        cost_estimate=pl.CostEstimate(flops=flops, bytes_accessed=4 << 20, transcendentals=0),
        name=name,
    )(*args)


def blend(keep, send, parity, count):
    def moved(x, by):
        return lax.ppermute(x, "blk", [(i, (i + by) % count) for i in range(count)])

    got = lax.ppermute(send, "blk", [(i, i ^ 1) for i in range(count)])
    odd = parity == 1
    zero = jnp.zeros_like(got[:, 0])
    near = keep[:, 0] + jnp.where(odd, got[:, 0], zero)
    next_chip = keep[:, 1] + jnp.where(odd, got[:, 1], got[:, 0])
    second_chip = keep[:, 2] + jnp.where(odd, zero, got[:, 1])
    next_chip = moved(next_chip, 2)
    second_chip = moved(second_chip, 4)
    return near + next_chip + second_chip


def shards(features, w_query, w_key, w_value, w_out, w_head, offsets, blend_mask):
    batch_count, passes, tokens, half = features.shape[1:]
    width = w_query.shape[1]
    sequences = batch_count * passes
    count = lax.axis_size("blk")
    block = lax.axis_index("blk")
    side = lax.axis_index("mp")
    swap = [(0, 1), (1, 0)]
    arrived = [
        lax.ppermute(features[0, s // 2, s % 2], "mp", swap) for s in range(sequences)
    ]
    shift = offsets[0] - STRIDE * block
    place = jnp.stack([side, shift]).astype(jnp.int32)
    keeps = PIECES // 2 + 1
    sends = PIECES // 2
    outs = [
        ((sequences, tokens, 3 * width), F32),
        ((sequences, tokens, 1), F32),
        ((sequences, tokens, 1), F32),
        ((8, 3 * width), F32),
        ((half, 3 * width), BF16),
        ((2 * half, OUTW), BF16),
        ((sequences, tokens, OUTW), F32),
        ((2 * OUTW, PATCH * LAT), BF16),
        ((GRID, PATCH * LAT), F32),
        ((keeps, STRIDE, LAT), F32),
        ((sends, STRIDE, LAT), F32),
    ]
    *shared, spread_map, mask_tile, mask_keep, mask_send = call(
        prepare,
        "prepare",
        (place, features, w_query, w_key, w_value, w_out, w_head, blend_mask),
        outs,
        [pltpu.VMEM((HALVES, FRAME, LANES), F32)],
        2 * sequences * tokens * half * 3 * width,
        48 << 20,
    )
    parity = block % 2
    weight_total = blend(mask_keep[None], mask_send[None], parity, count)
    work = [pltpu.VMEM((tokens, width), BF16)] * 5
    flops = 2 * tokens * (half * 3 * width + 2 * tokens * width)
    pieces = []
    for b in range(batch_count):
        last = b == batch_count - 1
        (guided,) = call(
            functools.partial(attend, 2 * b, False),
            f"attend_{b}_0",
            (place, arrived[2 * b], *shared),
            [((tokens, OUTW), F32)],
            work,
            flops,
            24 << 20,
        )
        planes = b + 1 if last else 1
        pieces += call(
            functools.partial(attend, 2 * b + 1, last),
            f"attend_{b}_1",
            (place, arrived[2 * b + 1], *shared, spread_map, mask_tile, guided)
            + (tuple(pieces) if last else ()),
            [
                ((planes, keeps, STRIDE, LAT), F32),
                ((planes, sends, STRIDE, LAT), F32),
            ],
            [pltpu.VMEM((HALVES, FRAME, LANES), F32)] + work,
            flops,
            24 << 20,
        )
    part = blend(pieces[-2], pieces[-1], parity, count)
    total = part + lax.ppermute(part, "mp", swap)
    return total / weight_total


def solution(mesh):
    return jax.shard_map(
        shards,
        mesh=mesh,
        in_specs=(
            P("blk", None, None, None, "mp"),
            P(None, "mp"),
            P(None, "mp"),
            P(None, "mp"),
            P("mp", None),
            P(),
            P("blk"),
            P("blk", None, None),
        ),
        out_specs=P(None, "blk", None),
        check_vma=False,
    )
```

time: 161 us -> 50.7 us (0.31)
  waiting for transfers between devices: 63.8 us -> 10.8 us
  local copies, waits for them, and re-layouts: 33 us -> 2.32 us
  matrix products: 27.3 us -> 0 us
  Pallas kernels: 0 us -> 21.3 us
  between operations: 14.4 us -> 0.75 us
  other arithmetic: 12.4 us -> 1.32 us
  starting transfers between devices: 9.98 us -> 14.1 us
    all_gather x1 -> x0, waiting for transfers between devices: 41.4 us -> none  [shards(): gathered = lax.all_gather(features, 'mp', axis=4, tiled=True)]
    dot_general x8 -> x0, matrix products: 27.3 us -> none  [the longest x1 5.62 us: shards(): jnp.dot(normed, w_query, preferred_element_type=jnp.float32)]
    pallas_call x0 -> x5, Pallas kernels: none -> 21.3 us  [call(): pl.pallas_call(kernel, out_shape=[in_vmem(shape, dtype) for shape, dtype...]
    psum x1 -> x0, waiting for transfers between devices: 16.8 us -> none  [shards(): lax.psum(head_part.astype(jnp.bfloat16), 'mp').astype(jnp.float32)]
    reshape x5 -> x0, local copies, waits for them, and re-layouts: 14.3 us -> none  [the longest x1 3.78 us: shards(): value_rows = jnp.dot(normed, w_value, preferred_element_type=jnp.float32)...]
    convert_element_type x5 -> x0, local copies, waits for them, and re-layouts: 7.57 us -> none  [the longest x1 2.49 us: shards(): queries = jnp.dot(normed, w_query, preferred_element_type=jnp.float32).as...]
    ppermute x8 -> x11, waiting for transfers between devices: 4.95 us -> 10.8 us  [the longest x4 6.6 us: shards(): lax.ppermute(features[0, s // 2, s % 2], 'mp', swap)]
    sub x1 -> x0, other arithmetic: 5.44 us -> none  [shards(): scores = scores - jnp.max(scores, axis=3, keepdims=True)]
  transfers between devices with their start and end apart: 10 -> 11, of which waited for: 5 -> 6; matrix products, arithmetic and copies ran while one was open for 11% -> 3% of each run, Pallas kernels for 0% -> 36%
where the time goes in v1:
time: 50.7 us; the launch traced here: 50.6 us
  Pallas kernels  21.3 us (42%)
  starting transfers between devices  14.1 us (28%)
  waiting for transfers between devices  10.8 us (21%)
  local copies, waits for them, and re-layouts  2.32 us (5%)
  other arithmetic  1.32 us (3%)
  between operations  0.75 us (1%)
    pallas_call x5, Pallas kernels, call(): pl.pallas_call(kernel, out_shape=[in_vmem(shape, dtype) for shape, dtype...  21.3 us
    ppermute x4, starting transfers between devices, moved(): return lax.ppermute(x, 'blk', [(i, (i + by) % count) for i in range(count)])  6.8 us
    ppermute x4, waiting for transfers between devices, shards(): lax.ppermute(features[0, s // 2, s % 2], 'mp', swap)  6.6 us
    ppermute x4, starting transfers between devices, shards(): lax.ppermute(features[0, s // 2, s % 2], 'mp', swap)  5.16 us
    ppermute x4, waiting for transfers between devices, moved(): return lax.ppermute(x, 'blk', [(i, (i + by) % count) for i in range(count)])  3.32 us
    ppermute x1, starting transfers between devices, shards(): total = part + lax.ppermute(part, 'mp', swap)  1.54 us
    squeeze x1, local copies, waits for them, and re-layouts, shards(): features[0, s // 2, s % 2]  1.42 us
  transfers between devices with their start and end apart: 11, of which 6 were waited for; matrix products, arithmetic and copies ran while one was open for 3% of the time, Pallas kernels for 36%

profile of v1, /device:TPU:0, one launch (start us, length us, event | category | flops | bytes accessed | tf_op | source)
XLA Modules:
  0.0 50.6 jit_solution(6682565245340195056)
XLA Ops:
  0.0 1.4 %slice_bitcast_fusion = (bf16[256,640]{1,0:T(8,128)(2,1)S(1)}, bf16[256,640]{1,0:T(8,128)(2,1)S(1)}, bf16[256,640]{1,0:T(8,128)(2,1)S(1)}, bf16[256,640]{1,0:T(8,128)(2,1)S(1)}) fusion(bf16[1,2,2,256,640]{4,3,2,1,0:T(8,128)(2,1)} %features.1), kind=kLoop, calls=%fused_computation | loop fusion | bytes 2621440 | tf_op jit(solution)/shard_map/squeeze | solution.py:261
  1.4 3.1 %collective-permute-start.3 = (bf16[256,640]{1,0:T(8,128)(2,1)S(1)}, bf16[256,640]{1,0:T(8,128)(2,1)S(1)}, u32[]{:S(2)}, u32[]{:S(2)}) collective-permute-start(bf16[256,640]{1,0:T(8,128)(2,1)S(1)} %get-tuple-element.35), channel_id=1, source_target_pairs={{0,1},{1,0},{2,3},{3,2},{4,5},{5,4},{6,7},{7,6},{8,9},{9,8},{10,11... | collective-permute-start | bytes 983048 | tf_op jit(solution)/shard_map/ppermute | solution.py:261
  4.5 0.1 collective-permute-start.2
  4.6 1.9 %collective-permute-start.1 = (bf16[256,640]{1,0:T(8,128)(2,1)S(1)}, bf16[256,640]{1,0:T(8,128)(2,1)S(1)}, u32[]{:S(2)}, u32[]{:S(2)}) collective-permute-start(bf16[256,640]{1,0:T(8,128)(2,1)S(1)} %get-tuple-element.36), channel_id=1, source_target_pairs={{0,1},{1,0},{2,3},{3,2},{4,5},{5,4},{6,7},{7,6},{8,9},{9,8},{10,11... | collective-permute-start | bytes 983048 | tf_op jit(solution)/shard_map/ppermute | solution.py:261
  6.5 0.1 collective-permute-start
  7.2 0.7 %pad_add_fusion.place = s32[2]{0:T(128)} fusion(s32[1]{0:T(128)} %bitcast.2, s32[1]{0:T(128)} %bitcast), kind=kLoop, calls=%fused_computation.25 | loop fusion | flops 2 | bytes 16 | tf_op jit(solution)/shard_map/stack | solution.py:264
  7.9 0.0 copy-done.1
  7.9 0.9 %copy.9.w_head = bf16[1280,64]{1,0:T(8,128)(2,1)} copy(bf16[1280,64]{0,1:T(8,128)(2,1)S(1)} %copy-done.1) | data formatting | bytes 327680 | tf_op args[5]
  8.8 8.7 %prepare.1 = (f32[4,256,1920]{2,1,0:T(8,128)S(1)}, f32[4,256,1]{2,1,0:T(8,128)S(1)}, f32[4,256,1]{2,1,0:T(8,128)S(1)}, f32[8,1920]{1,0:T(8,128)S(1)}, bf16[640,1...) custom-call(s32[2]{0:T(128)} %pad_add_fusion.place, ...), custom_call_target="tpu_custom_call" | custom-call | flops 2516582400 | bytes 4194304 | tf_op jit(solution)/shard_map/prepare/pallas_call | solution.py:225
  17.5 0.0 collective-permute-done.3.arrived
  17.6 2.9 %attend_0_0.1.rest_2_ = f32[256,64]{1,0:T(8,128)S(1)} custom-call(s32[2]{0:T(128)S(1)} %copy-done, bf16[256,640]{1,0:T(8,128)(2,1)S(1)} %collective-permute-done.3.arrived, f32[4,256,1920]{2,1,0:T(8,128)S(1)} %get-tuple-element.20.own_acc, f32[4,256,1]{2,1,0:T(8,128)S(1)} %get-tuple-element.21.own_mean, f32[4,256,1]{2,1,0:T(8,128)S(1)} %get-tuple-element.22.own_square, ...), custom_call_target="tpu_custom_call" | custom-call | flops 796917760 | bytes 4194304 | tf_op jit(solution)/shard_map/attend_0_0/pallas_call | solution.py:225
  20.5 6.6 %collective-permute-done.1.arrived = bf16[256,640]{1,0:T(8,128)(2,1)S(1)} collective-permute-done((bf16[256,640]{1,0:T(8,128)(2,1)S(1)}, bf16[256,640]{1,0:T(8,128)(2,1)S(1)}, u32[]{:S(2)}, u32[]{:S(2)}) %collective-permute-start.1) | collective-permute-done | bytes 327712 | tf_op jit(solution)/shard_map/ppermute | solution.py:261
  27.1 2.9 %attend_1_0.1.rest_2_ = f32[256,64]{1,0:T(8,128)S(1)} custom-call(s32[2]{0:T(128)S(1)} %copy-done, bf16[256,640]{1,0:T(8,128)(2,1)S(1)} %collective-permute-done.1.arrived, f32[4,256,1920]{2,1,0:T(8,128)S(1)} %get-tuple-element.20.own_acc, f32[4,256,1]{2,1,0:T(8,128)S(1)} %get-tuple-element.21.own_mean, f32[4,256,1]{2,1,0:T(8,128)S(1)} %get-tuple-element.22.own_square, ...), custom_call_target="tpu_custom_call" | custom-call | flops 796917760 | bytes 4194304 | tf_op jit(solution)/shard_map/attend_1_0/pallas_call | solution.py:225
  30.0 0.0 collective-permute-done.2.arrived
  30.1 3.4 %attend_0_1.1 = (f32[1,3,16,256]{3,2,1,0:T(8,128)S(1)}, f32[1,2,16,256]{3,2,1,0:T(8,128)S(1)}) custom-call(s32[2]{0:T(128)S(1)} %copy-done, bf16[256,640]{1,0:T(8,128)(2,1)S(1)} %collective-permute-done.2.arrived, f32[4,256,1920]{2,1,0:T(8,128)S(1)} %get-tuple-element.20.own_acc, f32[4,256,1]{2,1,0:T(8,128)S(1)} %get-tuple-element.21.own_mean, ...), custom_call_target="tpu_custom_call" | custom-call | flops 796917760 | bytes 4194304 | tf_op jit(solution)/shard_map/attend_0_1/pallas_call | solution.py:225
  33.5 0.0 collective-permute-done.arrived
  33.5 3.3 %attend_1_1.1 = (f32[2,3,16,256]{3,2,1,0:T(8,128)S(1)}, f32[2,2,16,256]{3,2,1,0:T(8,128)S(1)}) custom-call(s32[2]{0:T(128)S(1)} %copy-done, bf16[256,640]{1,0:T(8,128)(2,1)S(1)} %collective-permute-done.arrived, f32[4,256,1920]{2,1,0:T(8,128)S(1)} %get-tuple-element.20.own_acc, f32[4,256,1]{2,1,0:T(8,128)S(1)} %get-tuple-element.21.own_mean, ...), custom_call_target="tpu_custom_call" | custom-call | flops 796917760 | bytes 4194304 | tf_op jit(solution)/shard_map/attend_1_1/pallas_call | solution.py:225
  36.8 0.1 collective-permute-start.4
  36.8 0.5 collective-permute-start.8
  37.3 0.7 %collective-permute-done.4 = f32[2,2,16,256]{3,2,1,0:T(8,128)S(1)} collective-permute-done((f32[2,2,16,256]{3,2,1,0:T(8,128)S(1)}, f32[2,2,16,256]{3,2,1,0:T(8,128)S(1)}, u32[]{:S(2)}, u32[]{:S(2)}) %collective-permute-start.4) | collective-permute-done | bytes 65568 | tf_op jit(solution)/shard_map/ppermute | solution.py:241
  38.1 2.0 %collective-permute-start.5 = (f32[2,16,256]{2,1,0:T(8,128)S(1)}, f32[2,16,256]{2,1,0:T(8,128)S(1)}, u32[]{:S(2)}, u32[]{:S(2)}) collective-permute-start(f32[2,16,256]{2,1,0:T(8,128)S(1)} %fusion), channel_id=1, source_target_pairs={{0,4},{2,6},{4,8},{6,10},{8,12},{10,14},{12,16},{14,18},{16,20},{1... | collective-permute-start | bytes 98312 | tf_op jit(solution)/shard_map/ppermute | solution.py:239
  40.2 1.6 %collective-permute-start.6 = (f32[2,16,256]{2,1,0:T(8,128)S(1)}, f32[2,16,256]{2,1,0:T(8,128)S(1)}, u32[]{:S(2)}, u32[]{:S(2)}) collective-permute-start(f32[2,16,256]{2,1,0:T(8,128)S(1)} %fusion.5), channel_id=1, source_target_pairs={{0,8},{2,10},{4,12},{6,14},{8,16},{10,18},{12,20},{14,22},{16,24},... | collective-permute-start | bytes 98312 | tf_op jit(solution)/shard_map/ppermute | solution.py:239
  41.7 0.0 collective-permute-done.8
  41.7 1.6 %collective-permute-start.10 = (f32[1,16,256]{2,1,0:T(8,128)S(1)}, f32[1,16,256]{2,1,0:T(8,128)S(1)}, u32[]{:S(2)}, u32[]{:S(2)}) collective-permute-start(f32[1,16,256]{2,1,0:T(8,128)S(1)} %get-tuple-element.40), channel_id=1, source_target_pairs={{0,8},{2,10},{4,12},{6,14},{8,16},{10,18},{12,20},{14,22},{16,24},... | collective-permute-start | bytes 49160 | tf_op jit(solution)/shard_map/ppermute | solution.py:239
  43.4 1.6 %collective-permute-start.9 = (f32[1,16,256]{2,1,0:T(8,128)S(1)}, f32[1,16,256]{2,1,0:T(8,128)S(1)}, u32[]{:S(2)}, u32[]{:S(2)}) collective-permute-start(f32[1,16,256]{2,1,0:T(8,128)S(1)} %get-tuple-element.39), channel_id=1, source_target_pairs={{0,4},{2,6},{4,8},{6,10},{8,12},{10,14},{12,16},{14,18},{16,20},{1... | collective-permute-start | bytes 49160 | tf_op jit(solution)/shard_map/ppermute | solution.py:239
  44.9 0.1 collective-permute-done.5
  45.1 0.9 %collective-permute-done.6 = f32[2,16,256]{2,1,0:T(8,128)S(1)} collective-permute-done((f32[2,16,256]{2,1,0:T(8,128)S(1)}, f32[2,16,256]{2,1,0:T(8,128)S(1)}, u32[]{:S(2)}, u32[]{:S(2)}) %collective-permute-start.6) | collective-permute-done | bytes 32800 | tf_op jit(solution)/shard_map/ppermute | solution.py:239
  46.0 1.5 %collective-permute-start.7 = (f32[2,16,256]{2,1,0:T(8,128)S(1)}, f32[2,16,256]{2,1,0:T(8,128)S(1)}, u32[]{:S(2)}, u32[]{:S(2)}) collective-permute-start(f32[2,16,256]{2,1,0:T(8,128)S(1)} %fusion.3), channel_id=1, source_target_pairs={{0,1},{1,0},{2,3},{3,2},{4,5},{5,4},{6,7},{7,6},{8,9},{9,8},{10,11... | collective-permute-start | bytes 98312 | tf_op jit(solution)/shard_map/ppermute | solution.py:320
  47.5 0.0 collective-permute-done.10
  47.5 2.3 %collective-permute-done.9 = f32[1,16,256]{2,1,0:T(8,128)S(1)} collective-permute-done((f32[1,16,256]{2,1,0:T(8,128)S(1)}, f32[1,16,256]{2,1,0:T(8,128)S(1)}, u32[]{:S(2)}, u32[]{:S(2)}) %collective-permute-start.9) | collective-permute-done | bytes 16416 | tf_op jit(solution)/shard_map/ppermute | solution.py:239
  49.8 0.2 collective-permute-done.7
  50.0 0.6 %add_divide_fusion = f32[2,16,256]{2,1,0:T(8,128)} fusion(f32[2,16,256]{2,1,0:T(8,128)S(1)} %fusion.3, f32[2,16,256]{2,1,0:T(8,128)S(1)} %collective-permute-done.7, f32[16,256]{1,0:T(8,128)S(1)} %fusion.11), kind=kLoop, calls=%fused_computation.15 | loop fusion | flops 16384 | bytes 114688 | tf_op jit(solution)/shard_map/div | solution.py:321
  (8 shorter events, 0.0 us)
Async XLA Ops:
  0.0 7.9 %copy-start.1 = (bf16[1280,64]{0,1:T(8,128)(2,1)S(1)}, bf16[1280,64]{0,1:T(8,128)(2,1)}, u32[]{:S(2)}) copy-start(bf16[1280,64]{0,1:T(8,128)(2,1)} %param.13) | copy-start | bytes 491524
  1.4 16.1 %collective-permute-start.3 = (bf16[256,640]{1,0:T(8,128)(2,1)S(1)}, bf16[256,640]{1,0:T(8,128)(2,1)S(1)}, u32[]{:S(2)}, u32[]{:S(2)}) collective-permute-start(bf16[256,640]{1,0:T(8,128)(2,1)S(1)} %get-tuple-element.35), channel_id=1, source_target_pairs={{0,1},{1,0},{2,3},{3,2},{4,5},{5,4},{6,7},{7,6},{8,9},{9,8},{10,11... | collective-permute-start | bytes 983048 | tf_op jit(solution)/shard_map/ppermute | solution.py:261
  4.5 25.6 %collective-permute-start.2 = (bf16[256,640]{1,0:T(8,128)(2,1)S(1)}, bf16[256,640]{1,0:T(8,128)(2,1)S(1)}, u32[]{:S(2)}, u32[]{:S(2)}) collective-permute-start(bf16[256,640]{1,0:T(8,128)(2,1)S(1)} %get-tuple-element.38), channel_id=1, source_target_pairs={{0,1},{1,0},{2,3},{3,2},{4,5},{5,4},{6,7},{7,6},{8,9},{9,8},{10,11... | collective-permute-start | bytes 983048 | tf_op jit(solution)/shard_map/ppermute | solution.py:261
  4.6 22.5 %collective-permute-start.1 = (bf16[256,640]{1,0:T(8,128)(2,1)S(1)}, bf16[256,640]{1,0:T(8,128)(2,1)S(1)}, u32[]{:S(2)}, u32[]{:S(2)}) collective-permute-start(bf16[256,640]{1,0:T(8,128)(2,1)S(1)} %get-tuple-element.36), channel_id=1, source_target_pairs={{0,1},{1,0},{2,3},{3,2},{4,5},{5,4},{6,7},{7,6},{8,9},{9,8},{10,11... | collective-permute-start | bytes 983048 | tf_op jit(solution)/shard_map/ppermute | solution.py:261
  6.5 27.0 %collective-permute-start = (bf16[256,640]{1,0:T(8,128)(2,1)S(1)}, bf16[256,640]{1,0:T(8,128)(2,1)S(1)}, u32[]{:S(2)}, u32[]{:S(2)}) collective-permute-start(bf16[256,640]{1,0:T(8,128)(2,1)S(1)} %get-tuple-element.37), channel_id=1, source_target_pairs={{0,1},{1,0},{2,3},{3,2},{4,5},{5,4},{6,7},{7,6},{8,9},{9,8},{10,11... | collective-permute-start | bytes 983048 | tf_op jit(solution)/shard_map/ppermute | solution.py:261
  8.8 8.7 %copy-start = (s32[2]{0:T(128)S(1)}, s32[2]{0:T(128)}, u32[]{:S(2)}) copy-start(s32[2]{0:T(128)} %pad_add_fusion.place) | copy-start | bytes 28
  36.8 1.3 %collective-permute-start.4 = (f32[2,2,16,256]{3,2,1,0:T(8,128)S(1)}, f32[2,2,16,256]{3,2,1,0:T(8,128)S(1)}, u32[]{:S(2)}, u32[]{:S(2)}) collective-permute-start(f32[2,2,16,256]{3,2,1,0:T(8,128)S(1)} %get-tuple-element.32), channel_id=1, source_target_pairs={{0,2},{2,0},{4,6},{6,4},{8,10},{10,8},{12,14},{14,12},{16,18},{18,... | collective-permute-start | bytes 196616 | tf_op jit(solution)/shard_map/ppermute | solution.py:241
  36.8 4.9 %collective-permute-start.8 = (f32[1,2,16,256]{3,2,1,0:T(8,128)S(1)}, f32[1,2,16,256]{3,2,1,0:T(8,128)S(1)}, u32[]{:S(2)}, u32[]{:S(2)}) collective-permute-start(f32[1,2,16,256]{3,2,1,0:T(8,128)S(1)} %bitcast.58), channel_id=1, source_target_pairs={{0,2},{2,0},{4,6},{6,4},{8,10},{10,8},{12,14},{14,12},{16,18},{18,... | collective-permute-start | bytes 98312 | tf_op jit(solution)/shard_map/ppermute | solution.py:241
  38.1 7.0 %collective-permute-start.5 = (f32[2,16,256]{2,1,0:T(8,128)S(1)}, f32[2,16,256]{2,1,0:T(8,128)S(1)}, u32[]{:S(2)}, u32[]{:S(2)}) collective-permute-start(f32[2,16,256]{2,1,0:T(8,128)S(1)} %fusion), channel_id=1, source_target_pairs={{0,4},{2,6},{4,8},{6,10},{8,12},{10,14},{12,16},{14,18},{16,20},{1... | collective-permute-start | bytes 98312 | tf_op jit(solution)/shard_map/ppermute | solution.py:239
  40.2 5.8 %collective-permute-start.6 = (f32[2,16,256]{2,1,0:T(8,128)S(1)}, f32[2,16,256]{2,1,0:T(8,128)S(1)}, u32[]{:S(2)}, u32[]{:S(2)}) collective-permute-start(f32[2,16,256]{2,1,0:T(8,128)S(1)} %fusion.5), channel_id=1, source_target_pairs={{0,8},{2,10},{4,12},{6,14},{8,16},{10,18},{12,20},{14,22},{16,24},... | collective-permute-start | bytes 98312 | tf_op jit(solution)/shard_map/ppermute | solution.py:239
  41.7 5.8 %collective-permute-start.10 = (f32[1,16,256]{2,1,0:T(8,128)S(1)}, f32[1,16,256]{2,1,0:T(8,128)S(1)}, u32[]{:S(2)}, u32[]{:S(2)}) collective-permute-start(f32[1,16,256]{2,1,0:T(8,128)S(1)} %get-tuple-element.40), channel_id=1, source_target_pairs={{0,8},{2,10},{4,12},{6,14},{8,16},{10,18},{12,20},{14,22},{16,24},... | collective-permute-start | bytes 49160 | tf_op jit(solution)/shard_map/ppermute | solution.py:239
  43.4 6.4 %collective-permute-start.9 = (f32[1,16,256]{2,1,0:T(8,128)S(1)}, f32[1,16,256]{2,1,0:T(8,128)S(1)}, u32[]{:S(2)}, u32[]{:S(2)}) collective-permute-start(f32[1,16,256]{2,1,0:T(8,128)S(1)} %get-tuple-element.39), channel_id=1, source_target_pairs={{0,4},{2,6},{4,8},{6,10},{8,12},{10,14},{12,16},{14,18},{16,20},{1... | collective-permute-start | bytes 49160 | tf_op jit(solution)/shard_map/ppermute | solution.py:239
  46.0 4.0 %collective-permute-start.7 = (f32[2,16,256]{2,1,0:T(8,128)S(1)}, f32[2,16,256]{2,1,0:T(8,128)S(1)}, u32[]{:S(2)}, u32[]{:S(2)}) collective-permute-start(f32[2,16,256]{2,1,0:T(8,128)S(1)} %fusion.3), channel_id=1, source_target_pairs={{0,1},{1,0},{2,3},{3,2},{4,5},{5,4},{6,7},{7,6},{8,9},{9,8},{10,11... | collective-permute-start | bytes 98312 | tf_op jit(solution)/shard_map/ppermute | solution.py:320

commit v2 on v0

v2 whole, which is shorter than its diff:
```python
import functools
import math

import jax
import jax.numpy as jnp
from jax import lax
from jax.experimental import pallas as pl
from jax.experimental.pallas import tpu as pltpu
from jax.sharding import PartitionSpec as P


HEAD = 64
GRID = 16
PATCH = 4
CHAN = 4
STRIDE = 16
WINDOW = 64
OUTW = 64

guidance = 3.0


F32 = jnp.float32
BF16 = jnp.bfloat16
LAT = WINDOW * CHAN
LANES = 128
HALVES = LAT // LANES
BLOCK = 2 * STRIDE
BLOCKS = -(-(WINDOW + BLOCK - 1) // BLOCK)
FRAME = BLOCKS * BLOCK
PACKED = BLOCK * WINDOW // LAT
PAIR = 2 * HEAD
TRIPLE = 3 * PAIR
TAIL = 128
LAST_COLUMNS = 256


def dot(a, b):
    return jnp.dot(a, b, preferred_element_type=F32)


def dot_nt(a, b):
    return lax.dot_general(a, b, (((1,), (1,)), ((), ())), preferred_element_type=F32)


def moments(x):
    mean = jnp.mean(x, axis=1, keepdims=True)
    centred = x - mean
    return mean, jnp.sum(centred * centred, axis=1, keepdims=True)


def merged(a, b, a_count, b_count):
    count = a_count + b_count
    gap = b[0] - a[0]
    mean = a[0] + gap * (b_count / count)
    return mean, a[1] + b[1] + gap * gap * (a_count * b_count / count)


def split2(x):
    high = x.astype(BF16)
    return high, (x - high.astype(F32)).astype(BF16)


def iota(shape, axis):
    return lax.broadcasted_iota(jnp.int32, shape, axis)


def repeat_map():
    return (iota((WINDOW, LAT), 1) // CHAN == iota((WINDOW, LAT), 0)).astype(BF16)


def column_groups(columns):
    pairs = columns // TRIPLE
    starts = [2 * TRIPLE * g for g in range(-(-pairs // 2))]
    return list(zip(starts, starts[1:] + [columns]))


def to_frame(frame, shift):
    frame[WINDOW:] = jnp.zeros((FRAME - WINDOW, LANES), F32)
    by = shift + STRIDE * (lax.axis_index("blk") % 2)
    return pltpu.roll(frame[...], by, 0)


def window_shift(offsets):
    return offsets[0] - STRIDE * lax.axis_index("blk")


def prepare(
    offsets,
    features,
    w_query,
    w_key,
    w_value,
    w_out,
    w_head,
    mask,
    own_acc,
    own_mean,
    own_square,
    own_tail,
    near_sum,
    far_weights,
    out_weights,
    spread_map,
    mask_tile,
    mask_blocks,
    frame,
    held,
    near_weights,
    out_rows,
    sem,
):
    half = features.shape[-1]
    width = w_query.shape[1]
    sequences, _, columns = own_acc.shape
    passes = features.shape[2]
    pairs = width // PAIR
    side = lax.axis_index("mp")
    near = pl.ds(pl.multiple_of(side * half, LANES), half)
    far = pl.ds(pl.multiple_of((1 - side) * half, LANES), half)
    loads = [(features.at[0], held)]
    for p in range(pairs):
        for j, w in enumerate((w_query, w_key, w_value)):
            source = pl.ds(p * PAIR, PAIR)
            place = pl.ds(p * TRIPLE + j * PAIR, PAIR)
            loads.append((w.at[near, source], near_weights.at[:, place]))
    loads.append((w_out, out_rows))
    for p in range(pairs):
        for j, w in enumerate((w_query, w_key, w_value)):
            source = pl.ds(p * PAIR, PAIR)
            place = pl.ds(p * TRIPLE + j * PAIR, PAIR)
            loads.append((w.at[far, source], far_weights.at[pl.ds(TAIL, half), place]))
    loads = [pltpu.make_async_copy(a, b, sem.at[i]) for i, (a, b) in enumerate(loads)]
    for load in loads:
        load.start()
    shift = window_shift(offsets)
    plain = mask[0].astype(F32)
    wide = dot(plain.astype(BF16), repeat_map())
    for h in range(HALVES):
        lanes = slice(h * LANES, (h + 1) * LANES)
        frame[:WINDOW] = wide[:, lanes]
        for a in range(PATCH):
            places = slice(a * LAT + h * LANES, a * LAT + (h + 1) * LANES)
            mask_tile[:, places] = frame[pl.ds(a, GRID, stride=PATCH), :]
    frame[:WINDOW, :WINDOW] = 0.5 * plain
    frame[:WINDOW, WINDOW:] = jnp.zeros((WINDOW, LANES - WINDOW), F32)
    rolled = to_frame(frame, shift)
    for t in range(BLOCKS):
        for k in range(LAT // WINDOW):
            rows = slice(t * BLOCK + k * PACKED, t * BLOCK + (k + 1) * PACKED)
            mask_blocks[t, :, k * WINDOW : (k + 1) * WINDOW] = rolled[rows, :WINDOW]
    part = OUTW // PATCH
    rows, places = iota(spread_map.shape, 0) % OUTW, iota(spread_map.shape, 1)
    spread_map[...] = ((rows // part == places // LAT) & (rows % part == places % part)).astype(BF16)
    near_weights[:, 3 * width : 3 * width + OUTW] = w_head[:, near].T
    near_weights[:, 3 * width + OUTW :] = jnp.zeros((half, columns - 3 * width - OUTW), BF16)
    far_weights[TAIL:, 3 * width :] = jnp.zeros((half, columns - 3 * width), BF16)
    loads[0].wait()
    main = half - TAIL
    ones = jnp.ones((8, main), BF16)
    for s in range(sequences):
        x = held[s // passes, s % passes]
        own_mean[s], own_square[s] = moments(x.astype(F32))
        own_tail[s] = x[:, main:]
    done = 1
    for first, last in column_groups(columns):
        count = 3 * ((min(last, 3 * width) - first) // TRIPLE)
        for load in loads[done : done + count]:
            load.wait()
        done += count
        w = near_weights[:main, first:last]
        for s in range(sequences):
            own_acc[s, :, first:last] = dot(held[s // passes, s % passes, :, :main], w)
        near_sum[:, first:last] = dot(ones, w)
    far_weights[:TAIL] = near_weights[main:]
    loads[done].wait()
    high, low = split2(dot_nt(out_rows[...], w_head[...]))
    out_weights[:, :OUTW] = high
    out_weights[:, OUTW:] = low
    for load in loads[done + 1 :]:
        load.wait()


def cut(windows, features, *refs):
    outs, sem = refs[:-1], refs[-1]
    passes = features.shape[2]
    loads = [
        pltpu.make_async_copy(
            features.at[0, s // passes, s % passes, :, pl.ds(start, stop - start)],
            out,
            sem.at[i],
        )
        for i, ((s, start, stop), out) in enumerate(zip(windows, outs))
    ]
    for load in loads:
        load.start()
    for load in loads:
        load.wait()


def halves(x):
    odd = lax.axis_index("blk") % 2 == 1
    own, other = [], []
    for b in range(x.shape[0] // BLOCK):
        low = x[b * BLOCK : b * BLOCK + STRIDE]
        high = x[b * BLOCK + STRIDE : (b + 1) * BLOCK]
        own.append(jnp.where(odd, high, low))
        other.append(jnp.where(odd, low, high))
    weights = x[-PACKED:]
    return jnp.concatenate(own + [weights], axis=0), jnp.concatenate(other + [weights], axis=0)


def sum_chip(own, got, here, next_chip, second_chip):
    here[...] = halves(own[0] + got[0])[0]
    next_chip[...] = own[1] + got[1]
    second_chip[...] = own[2] + got[2]


def sum_far(here, across, first, second, mine, other):
    kept, passed = halves(first[...] + second[...])
    mine[...] = here[...] + across[...] + kept
    other[...] = passed


def finish(mine, got, out):
    odd = lax.axis_index("blk") % 2 == 1
    total = mine[...] + got[...]
    packed = total[-PACKED:]
    packed = jnp.where(odd, packed[:, LAT // 2 :], packed[:, : LAT // 2])
    weights = [packed[:, k * WINDOW : (k + 1) * WINDOW] for k in range(STRIDE // PACKED)]
    weights = dot(jnp.concatenate(weights, axis=0).astype(BF16), repeat_map())
    for b in range(out.shape[0]):
        out[b] = total[b * STRIDE : (b + 1) * STRIDE] / weights


def extend(
    s,
    arrived,
    own_acc,
    own_mean,
    own_square,
    own_tail,
    far_weights,
    token,
    acc,
    mean,
    square,
):
    del token
    x = arrived[...]
    near = own_mean[s], own_square[s]
    half = far_weights.shape[0] - TAIL
    mean[0], square[0] = merged(near, moments(x.astype(F32)), half, x.shape[1])
    x = jnp.concatenate([own_tail[s], x], axis=1)
    for first, last in column_groups(own_acc.shape[2]):
        w = far_weights[: x.shape[1], first:last]
        acc[0, :, first:last] = own_acc[s, :, first:last] + dot(x, w)


def attend(
    s,
    near_count,
    width,
    offsets,
    arrived,
    own_acc,
    own_mean,
    own_square,
    own_tail,
    sums_in,
    far_weights,
    out_weights,
    *rest,
):
    first_pass = s % 2 == 0
    if first_pass:
        _, guided_out = rest[:2]
        sums_out = rest[2:]
    else:
        spread_map, mask_tile, guided_in = rest[:3]
        before = rest[3:-2]
        blocks, frame = rest[-2:]
    tokens, far_count = arrived.shape
    columns = own_acc.shape[2]
    half = far_weights.shape[0] - TAIL
    slab = s if own_acc.shape[0] > 1 else 0
    x = arrived[...]
    near = own_mean[slab], own_square[slab]
    mean, square = merged(near, moments(x.astype(F32)), near_count, far_count)
    scale = lax.rsqrt(square / (near_count + far_count) + 1e-05)
    offset = mean * scale
    if near_count == half:
        x = jnp.concatenate([own_tail[s], x], axis=1)
    rows = slice(TAIL + half - x.shape[1], TAIL + half)
    start = s == 0
    if start:
        x = jnp.concatenate([x, jnp.ones((16, x.shape[1]), BF16)], axis=0)
    factor = math.log2(math.e) / HEAD**0.5
    query_scale, query_offset = scale * factor, offset * factor
    first_head = iota((1, PAIR), 1) < HEAD
    ones = jnp.ones((tokens, PAIR), BF16)
    none = jnp.zeros((tokens, PAIR), BF16)
    ones_even = jnp.where(first_head, ones, none)
    ones_odd = jnp.where(first_head, none, ones)
    out = None
    for first, last in column_groups(columns):
        total = dot(x, far_weights[rows, first:last])
        sums = sums_in[0:8, first:last]
        if start:
            sums = sums + total[tokens : tokens + 8]
            sums_out[0][:, first:last] = sums
            total = total[:tokens]
        total = total + own_acc[slab, :, first:last]
        sums = sums[0:1]
        contexts = []
        for p in range((min(last, 3 * width) - first) // TRIPLE):

            def part(j, by, less):
                places = slice(p * TRIPLE + j * PAIR, p * TRIPLE + (j + 1) * PAIR)
                return total[:, places] * by - less * sums[:, places]

            query = part(0, query_scale, query_offset)
            k = part(1, scale, offset).astype(BF16)
            v = part(2, scale, offset).astype(BF16)
            probs = []
            for q in (jnp.where(first_head, query, 0.0), jnp.where(first_head, 0.0, query)):
                scores = dot_nt(q.astype(BF16), k)
                top = jnp.max(scores, axis=1, keepdims=True)
                probs.append(jnp.exp2(scores - top).astype(BF16))
            stacked = jnp.concatenate(
                [
                    jnp.concatenate([jnp.where(first_head, v, none), ones_even], axis=1),
                    jnp.concatenate([jnp.where(first_head, none, v), ones_odd], axis=1),
                ],
                axis=0,
            )
            both = dot(jnp.concatenate(probs, axis=1), stacked)
            contexts.append((both[:, :PAIR] / both[:, PAIR:]).astype(BF16))
        here = slice(first // 3, first // 3 + len(contexts) * PAIR)
        more = dot(jnp.concatenate(contexts, axis=1), out_weights[here])
        out = more if out is None else out + more
        if last > 3 * width:
            out = out + total[:, 3 * width - first :]
    if first_pass:
        guided_out[...] = (1.0 - guidance) * out
        return
    guided = guidance * out + guided_in[...]
    tiled = dot(jnp.concatenate(split2(guided), axis=1), spread_map[...])
    lane_row = iota((1, PATCH * LAT), 1) % LAT // (LAT // GRID)
    spread = tiled[:GRID]
    for r in range(1, GRID):
        spread = jnp.where(lane_row == r, tiled[r * GRID : (r + 1) * GRID], spread)
    spread = spread * mask_tile[...]
    shift = window_shift(offsets)
    for h in range(HALVES):
        lanes = slice(h * LANES, (h + 1) * LANES)
        for a in range(PATCH):
            places = slice(a * LAT + h * LANES, a * LAT + (h + 1) * LANES)
            frame[pl.ds(a, GRID, stride=PATCH), :] = spread[:, places]
        rolled = to_frame(frame, shift)
        at = sum(x.shape[1] for x in before[:-1])
        for t in range(BLOCKS):
            blocks[t, at : at + BLOCK, lanes] = rolled[t * BLOCK : (t + 1) * BLOCK]
    at = 0
    for i, x in enumerate(before):
        if i == len(before) - 1:
            at += BLOCK
        blocks[:, at : at + x.shape[1]] = x[...]
        at += x.shape[1]


def call(kernel, args, outs, scratch=(), flops=0, limit=1 << 20, smem=0):
    specs, values = [], []
    for i, x in enumerate(args):
        space = pltpu.SMEM if i < smem else pltpu.VMEM
        if isinstance(x, tuple):
            x, space = x
            x = pltpu.with_memory_space_constraint(x, space)
        specs.append(pl.BlockSpec(memory_space=space))
        values.append(x)
    return pl.pallas_call(
        kernel,
        out_shape=[pltpu.VMEM(shape, dtype) for shape, dtype in outs],
        in_specs=specs,
        out_specs=[pl.BlockSpec(memory_space=pltpu.VMEM)] * len(outs),
        scratch_shapes=list(scratch),
        compiler_params=pltpu.CompilerParams(vmem_limit_bytes=limit),
        cost_estimate=pl.CostEstimate(flops=flops, bytes_accessed=1 << 20, transcendentals=0),
    )(*values)


def partner(x):
    count = lax.axis_size("blk")
    return lax.ppermute(x, "blk", [(i, i ^ 1) for i in range(count)])


def across(x):
    return lax.ppermute(x, "mp", [(0, 1), (1, 0)])


def moved(x, by):
    count, sides = lax.axis_size("blk"), lax.axis_size("mp")
    pairs = [
        (i * sides + m, (i + 2 * by) % count * sides + (m ^ (i % 2)))
        for i in range(count)
        for m in range(sides)
    ]
    return lax.ppermute(x, ("blk", "mp"), pairs)


def blend(blocks, batch_count):
    whole, part = blocks.shape[1:], (batch_count * STRIDE + PACKED, LAT)
    got = partner(blocks)
    here, first, second = call(sum_chip, (blocks, got), [(part, F32), (whole, F32), (whole, F32)])
    first = moved(first, 1)
    second = moved(second, 2)
    other_side = across(here)
    mine, other = call(sum_far, (here, other_side, first, second), [(part, F32)] * 2)
    return pl.pallas_call(
        finish,
        out_shape=jax.ShapeDtypeStruct((batch_count, STRIDE, LAT), F32),
        compiler_params=pltpu.CompilerParams(vmem_limit_bytes=1 << 20),
        name="finish",
    )(mine, partner(other))


def shards(features, w_query, w_key, w_value, w_out, w_head, offsets, blend_mask):
    batch_count, passes, tokens, half = features.shape[1:]
    width = w_query.shape[1]
    sequences = batch_count * passes
    columns = 3 * width + 2 * OUTW
    windows = [(s, 0, half) for s in range(sequences - 1)]
    split = max(half - LAST_COLUMNS, 0)
    if split:
        windows.append((sequences - 1, 0, split))
    windows.append((sequences - 1, split, half))
    arrived = []
    for group in (windows[:1], windows[1:]):
        parts = call(
            functools.partial(cut, group),
            ((features, pltpu.HBM),),
            [((tokens, stop - start), features.dtype) for _, start, stop in group],
            [pltpu.SemaphoreType.DMA((len(group),))],
        )
        for part in parts:
            arrived.append(across(part))
    outs = [
        ((sequences, tokens, columns), F32),
        ((sequences, tokens, 1), F32),
        ((sequences, tokens, 1), F32),
        ((sequences, tokens, TAIL), BF16),
        ((8, columns), F32),
        ((TAIL + half, columns), BF16),
        ((width, 2 * OUTW), BF16),
        ((4 * OUTW, PATCH * LAT), BF16),
        ((GRID, PATCH * LAT), F32),
        ((BLOCKS, PACKED, LAT), F32),
    ]
    weights = [(w, pltpu.HBM) for w in (w_query, w_key, w_value, w_out)]
    frame = [pltpu.VMEM((FRAME, LANES), F32)]
    prepared = call(
        prepare,
        (offsets, (features, pltpu.HBM), *weights, w_head.T, blend_mask),
        outs,
        frame
        + [
            pltpu.VMEM(features.shape[1:], features.dtype),
            pltpu.VMEM((half, columns), BF16),
            pltpu.VMEM(w_out.shape, BF16),
            pltpu.SemaphoreType.DMA((2 + 6 * (width // PAIR),)),
        ],
        2 * sequences * tokens * half * 3 * width,
        24 << 20,
        1,
    )
    acc, mean, square, tail, sums, far_weights, out_weights = prepared[:7]
    spread_map, mask_tile, mask_blocks = prepared[7:]
    own = (acc, mean, square)
    flops = 2 * tokens * (half * 3 * width + 2 * tokens * width)
    blocks = []
    token = mask_blocks
    at = 0
    for s in range(sequences):
        near, near_count = own, half
        if arrived[at].shape[1] < half:
            near = tuple(
                call(
                    functools.partial(extend, s),
                    (arrived[at], *own, tail, far_weights, (token, pl.ANY)),
                    [((1, tokens, columns), F32), ((1, tokens, 1), F32), ((1, tokens, 1), F32)],
                    (),
                    2 * tokens * arrived[at].shape[1] * 3 * width,
                    8 << 20,
                )
            )
            near_count = half + arrived[at].shape[1]
            at += 1
        args = (offsets, arrived[at], *near, tail, sums, far_weights, out_weights)
        at += 1
        scratch = ()
        if s % passes == 0:
            args += ((token, pl.ANY),)
            results = [((tokens, 2 * OUTW), F32)]
            if s == 0:
                results.append(((8, columns), F32))
        else:
            args += (spread_map, mask_tile, token)
            rows = BLOCK
            if s == sequences - 1:
                args += (*blocks, mask_blocks)
                rows = batch_count * BLOCK + PACKED
            results = [((BLOCKS, rows, LAT), F32)]
            scratch = frame
        token, *more = call(
            functools.partial(attend, s, near_count, width),
            args,
            results,
            scratch,
            flops,
            16 << 20,
            1,
        )
        if more:
            (sums,) = more
        if s % passes:
            blocks.append(token)
    return blend(blocks[-1], batch_count)


def solution(mesh):
    return jax.shard_map(
        shards,
        mesh=mesh,
        in_specs=(
            P("blk", None, None, None, "mp"),
            P(None, "mp"),
            P(None, "mp"),
            P(None, "mp"),
            P("mp", None),
            P(),
            P("blk"),
            P("blk", None, None),
        ),
        out_specs=P(None, "blk", None),
        check_vma=False,
    )
```

time: 161 us -> 51.7 us (0.32)
  waiting for transfers between devices: 63.8 us -> 16.8 us
  local copies, waits for them, and re-layouts: 33 us -> 0.01 us
  matrix products: 27.3 us -> 0 us
  Pallas kernels: 0 us -> 21.4 us
  between operations: 14.4 us -> 0.78 us
  other arithmetic: 12.4 us -> 0 us
  starting transfers between devices: 9.98 us -> 12.6 us
    all_gather x1 -> x0, waiting for transfers between devices: 41.4 us -> none  [shards(): gathered = lax.all_gather(features, 'mp', axis=4, tiled=True)]
    dot_general x8 -> x0, matrix products: 27.3 us -> none  [the longest x1 5.62 us: shards(): jnp.dot(normed, w_query, preferred_element_type=jnp.float32)]
    pallas_call x0 -> x11, Pallas kernels: none -> 21.4 us  [the longest x10 20.5 us: call(): pl.pallas_call(kernel, out_shape=[pltpu.VMEM(shape, dtype) for shape, dty...]
    psum x1 -> x0, waiting for transfers between devices: 16.8 us -> none  [shards(): lax.psum(head_part.astype(jnp.bfloat16), 'mp').astype(jnp.float32)]
    reshape x5 -> x0, local copies, waits for them, and re-layouts: 14.3 us -> none  [the longest x1 3.78 us: shards(): value_rows = jnp.dot(normed, w_value, preferred_element_type=jnp.float32)...]
    ppermute x8 -> x10, waiting for transfers between devices: 4.95 us -> 16.8 us  [the longest x6 14.3 us: across(): return lax.ppermute(x, 'mp', [(0, 1), (1, 0)])]
    convert_element_type x5 -> x0, local copies, waits for them, and re-layouts: 7.57 us -> none  [the longest x1 2.49 us: shards(): queries = jnp.dot(normed, w_query, preferred_element_type=jnp.float32).as...]
    sub x1 -> x0, other arithmetic: 5.44 us -> none  [shards(): scores = scores - jnp.max(scores, axis=3, keepdims=True)]
  transfers between devices with their start and end apart: 10 -> 10, of which waited for: 5 -> 6; matrix products, arithmetic and copies ran while one was open for 11% -> 0% of each run, Pallas kernels for 0% -> 32%
where the time goes in v2:
time: 51.7 us; the launch traced here: 51.5 us
  Pallas kernels  21.4 us (41%)
  waiting for transfers between devices  16.8 us (32%)
  starting transfers between devices  12.6 us (24%)
  between operations  0.78 us (2%)
    pallas_call x10, Pallas kernels, call(): pl.pallas_call(kernel, out_shape=[pltpu.VMEM(shape, dtype) for shape, dty...  20.5 us
    ppermute x6, waiting for transfers between devices, across(): return lax.ppermute(x, 'mp', [(0, 1), (1, 0)])  14.3 us
    ppermute x6, starting transfers between devices, across(): return lax.ppermute(x, 'mp', [(0, 1), (1, 0)])  8.7 us
    ppermute x2, starting transfers between devices, moved(): return lax.ppermute(x, ('blk', 'mp'), pairs)  3.34 us
    ppermute x2, waiting for transfers between devices, partner(): return lax.ppermute(x, 'blk', [(i, i ^ 1) for i in range(count)])  2.33 us
  transfers between devices with their start and end apart: 10, of which 6 were waited for; matrix products, arithmetic and copies ran while one was open for 0% of the time, Pallas kernels for 32%

profile of v2, /device:TPU:0, one launch (start us, length us, event | category | flops | bytes accessed | tf_op | source)
XLA Modules:
  0.0 51.5 jit_solution(838928551528936186)
XLA Ops:
  0.0 0.0 copy-start.1
  0.0 1.0 %shard_map.84 = bf16[256,640]{1,0:T(8,128)(2,1)S(1)} custom-call(bf16[1,2,2,256,640]{4,3,2,1,0:T(8,128)(2,1)} %features.5), custom_call_target="tpu_custom_call" | custom-call | bytes 1048576 | tf_op jit(solution)/shard_map/pallas_call | solution.py:381
  1.0 3.1 %collective-permute-start.3 = (bf16[256,640]{1,0:T(8,128)(2,1)S(1)}, bf16[256,640]{1,0:T(8,128)(2,1)S(1)}, u32[]{:S(2)}, u32[]{:S(2)}) collective-permute-start(bf16[256,640]{1,0:T(8,128)(2,1)S(1)} %shard_map.84), channel_id=1, source_target_pairs={{0,1},{1,0},{2,3},{3,2},{4,5},{5,4},{6,7},{7,6},{8,9},{9,8},{10,11... | collective-permute-start | bytes 983048 | tf_op jit(solution)/shard_map/ppermute | solution.py:398
  4.1 1.2 %shard_map.82 = (bf16[256,640]{1,0:T(8,128)(2,1)S(1)}, bf16[256,640]{1,0:T(8,128)(2,1)S(1)}, bf16[256,384]{1,0:T(8,128)(2,1)S(1)}, bf16[256,256]{1,0:T(8,128)(2,1)S(1)}) custom-call(bf16[1,2,2,256,640]{4,3,2,1,0:T(8,128)(2,1)} %features.5), custom_call_target="tpu_custom_call" | custom-call | bytes 1048576 | tf_op jit(solution)/shard_map/pallas_call | solution.py:381
  5.3 0.1 collective-permute-start.4
  5.4 2.0 %collective-permute-start = (bf16[256,256]{1,0:T(8,128)(2,1)S(1)}, bf16[256,256]{1,0:T(8,128)(2,1)S(1)}, u32[]{:S(2)}, u32[]{:S(2)}) collective-permute-start(bf16[256,256]{1,0:T(8,128)(2,1)S(1)} %get-tuple-element.29), channel_id=1, source_target_pairs={{0,1},{1,0},{2,3},{3,2},{4,5},{5,4},{6,7},{7,6},{8,9},{9,8},{10,11... | collective-permute-start | bytes 393224 | tf_op jit(solution)/shard_map/ppermute | solution.py:398
  7.4 0.1 collective-permute-start.1
  7.5 1.9 %collective-permute-start.2 = (bf16[256,640]{1,0:T(8,128)(2,1)S(1)}, bf16[256,640]{1,0:T(8,128)(2,1)S(1)}, u32[]{:S(2)}, u32[]{:S(2)}) collective-permute-start(bf16[256,640]{1,0:T(8,128)(2,1)S(1)} %get-tuple-element.36), channel_id=1, source_target_pairs={{0,1},{1,0},{2,3},{3,2},{4,5},{5,4},{6,7},{7,6},{8,9},{9,8},{10,11... | collective-permute-start | bytes 983048 | tf_op jit(solution)/shard_map/ppermute | solution.py:398
  10.1 0.0 copy-done.1
  10.1 0.0 copy-done
  10.1 6.0 %shard_map.83 = (f32[4,256,2048]{2,1,0:T(8,128)S(1)}, f32[4,256,1]{2,1,0:T(8,128)S(1)}, f32[4,256,1]{2,1,0:T(8,128)S(1)}, bf16[4,256,128]{2,1,0:T(8,128)(2,1)S(1...) custom-call(s32[1]{0:T(128)S(6)} %copy.9.offsets, ...), custom_call_target="tpu_custom_call" | custom-call | flops 2516582400 | bytes 1048576 | tf_op jit(solution)/shard_map/pallas_call | solution.py:381
  16.1 0.0 collective-permute-done.3.arrived
  16.1 3.0 %shard_map.85 = (f32[256,128]{1,0:T(8,128)S(1)}, f32[8,2048]{1,0:T(8,128)S(1)}) custom-call(s32[1]{0:T(128)S(6)} %copy.9.offsets, bf16[256,640]{1,0:T(8,128)(2,1)S(1)} %collective-permute-done.3.arrived, f32[4,256,2048]{2,1,0:T(8,128)S(1)} %get-tuple-element.31.own_acc, f32[4,256,1]{2,1,0:T(8,128)S(1)} %get-tuple-element.32.own_mean, ...), custom_call_target="tpu_custom_call" | custom-call | flops 796917760 | bytes 1048576 | tf_op jit(solution)/shard_map/pallas_call | solution.py:381
  19.1 0.6 %collective-permute-done.4.arrived = bf16[256,640]{1,0:T(8,128)(2,1)S(1)} collective-permute-done((bf16[256,640]{1,0:T(8,128)(2,1)S(1)}, bf16[256,640]{1,0:T(8,128)(2,1)S(1)}, u32[]{:S(2)}, u32[]{:S(2)}) %collective-permute-start.4) | collective-permute-done | bytes 327712 | tf_op jit(solution)/shard_map/ppermute | solution.py:398
  19.7 3.0 %shard_map.86.rest_0_.rest_3_ = f32[3,32,256]{2,1,0:T(8,128)S(1)} custom-call(s32[1]{0:T(128)S(6)} %copy.9.offsets, bf16[256,640]{1,0:T(8,128)(2,1)S(1)} %collective-permute-done.4.arrived, f32[4,256,2048]{2,1,0:T(8,128)S(1)} %get-tuple-element.31.own_acc, f32[4,256,1]{2,1,0:T(8,128)S(1)} %get-tuple-element.32.own_mean, ...), custom_call_target="tpu_custom_call" | custom-call | flops 796917760 | bytes 1048576 | tf_op jit(solution)/shard_map/pallas_call | solution.py:381
  22.7 10.1 %collective-permute-done.2.arrived = bf16[256,640]{1,0:T(8,128)(2,1)S(1)} collective-permute-done((bf16[256,640]{1,0:T(8,128)(2,1)S(1)}, bf16[256,640]{1,0:T(8,128)(2,1)S(1)}, u32[]{:S(2)}, u32[]{:S(2)}) %collective-permute-start.2) | collective-permute-done | bytes 327712 | tf_op jit(solution)/shard_map/ppermute | solution.py:398
  32.9 2.7 %shard_map.87.token.rest_2_ = f32[256,128]{1,0:T(8,128)S(1)} custom-call(s32[1]{0:T(128)S(6)} %copy.9.offsets, bf16[256,640]{1,0:T(8,128)(2,1)S(1)} %collective-permute-done.2.arrived, f32[4,256,2048]{2,1,0:T(8,128)S(1)} %get-tuple-element.31.own_acc, f32[4,256,1]{2,1,0:T(8,128)S(1)} %get-tuple-element.32.own_mean, ...), custom_call_target="tpu_custom_call" | custom-call | flops 796917760 | bytes 1048576 | tf_op jit(solution)/shard_map/pallas_call | solution.py:381
  35.6 0.0 collective-permute-done.1.arrived
  35.6 0.8 %shard_map.88 = (f32[1,256,2048]{2,1,0:T(8,128)S(1)}, f32[1,256,1]{2,1,0:T(8,128)S(1)}, f32[1,256,1]{2,1,0:T(8,128)S(1)}) custom-call(bf16[256,384]{1,0:T(8,128)(2,1)S(1)} %collective-permute-done.1.arrived, f32[4,256,2048]{2,1,0:T(8,128)S(1)} %get-tuple-element.31.own_acc, f32[4,256,1]{2,1,0:T(8,128)S(1)} %get-tuple-element.32.own_mean, ...), custom_call_target="tpu_custom_call" | custom-call | flops 377487360 | bytes 1048576 | tf_op jit(solution)/shard_map/pallas_call | solution.py:381
  36.4 0.0 collective-permute-done.arrived
  36.4 2.7 %shard_map.89.own = f32[3,72,256]{2,1,0:T(8,128)S(1)} custom-call(s32[1]{0:T(128)S(6)} %copy.9.offsets, bf16[256,256]{1,0:T(8,128)(2,1)S(1)} %collective-permute-done.arrived, f32[1,256,2048]{2,1,0:T(8,128)S(1)} %get-tuple-element.45.own_acc, f32[1,256,1]{2,1,0:T(8,128)S(1)} %get-tuple-element.46.own_mean, f32[1,256,1]{2,1,0:T(8,128)S(1)} %get-tuple-element.47.own_square, ...), custom_call_target="tpu_custom_call" | custom-call | flops 796917760 | bytes 1048576 | tf_op jit(solution)/shard_map/pallas_call | solution.py:381
  39.1 0.1 collective-permute-start.5
  39.2 1.5 %collective-permute-done.5.got = f32[3,72,256]{2,1,0:T(8,128)S(1)} collective-permute-done((f32[3,72,256]{2,1,0:T(8,128)S(1)}, f32[3,72,256]{2,1,0:T(8,128)S(1)}, u32[]{:S(2)}, u32[]{:S(2)}) %collective-permute-start.5) | collective-permute-done | bytes 221216 | tf_op jit(solution)/shard_map/ppermute | solution.py:394
  40.7 1.8 %collective-permute-start.7 = (f32[72,256]{1,0:T(8,128)S(1)}, f32[72,256]{1,0:T(8,128)S(1)}, u32[]{:S(2)}, u32[]{:S(2)}) collective-permute-start(f32[72,256]{1,0:T(8,128)S(1)} %get-tuple-element.49), channel_id=1, source_target_pairs={{0,4},{1,5},{2,7},{3,6},{4,8},{5,9},{6,11},{7,10},{8,12},{9,13},{1... | collective-permute-start | bytes 221192 | tf_op jit(solution)/shard_map/ppermute | solution.py:408
  42.5 1.6 %collective-permute-start.8 = (f32[72,256]{1,0:T(8,128)S(1)}, f32[72,256]{1,0:T(8,128)S(1)}, u32[]{:S(2)}, u32[]{:S(2)}) collective-permute-start(f32[72,256]{1,0:T(8,128)S(1)} %get-tuple-element.50), channel_id=1, source_target_pairs={{0,8},{1,9},{2,11},{3,10},{4,12},{5,13},{6,15},{7,14},{8,16},{9,17... | collective-permute-start | bytes 221192 | tf_op jit(solution)/shard_map/ppermute | solution.py:408
  44.1 1.5 %collective-permute-start.6 = (f32[40,256]{1,0:T(8,128)S(1)}, f32[40,256]{1,0:T(8,128)S(1)}, u32[]{:S(2)}, u32[]{:S(2)}) collective-permute-start(f32[40,256]{1,0:T(8,128)S(1)} %get-tuple-element.48.here), channel_id=1, source_target_pairs={{0,1},{1,0},{2,3},{3,2},{4,5},{5,4},{6,7},{7,6},{8,9},{9,8},{10,11... | collective-permute-start | bytes 122888 | tf_op jit(solution)/shard_map/ppermute | solution.py:398
  45.6 3.6 %collective-permute-done.6.across = f32[40,256]{1,0:T(8,128)S(1)} collective-permute-done((f32[40,256]{1,0:T(8,128)S(1)}, f32[40,256]{1,0:T(8,128)S(1)}, u32[]{:S(2)}, u32[]{:S(2)}) %collective-permute-start.6) | collective-permute-done | bytes 40992 | tf_op jit(solution)/shard_map/ppermute | solution.py:398
  49.2 0.0 collective-permute-done.7.first
  49.2 0.1 collective-permute-done.8.second
  49.3 0.5 collective-permute-start.9
  49.9 0.9 %collective-permute-done.9.got = f32[40,256]{1,0:T(8,128)S(1)} collective-permute-done((f32[40,256]{1,0:T(8,128)S(1)}, f32[40,256]{1,0:T(8,128)S(1)}, u32[]{:S(2)}, u32[]{:S(2)}) %collective-permute-start.9) | collective-permute-done | bytes 40992 | tf_op jit(solution)/shard_map/ppermute | solution.py:394
  50.7 0.8 %finish.1 = f32[2,16,256]{2,1,0:T(8,128)} custom-call(f32[40,256]{1,0:T(8,128)S(1)} %get-tuple-element.51.mine, f32[40,256]{1,0:T(8,128)S(1)} %collective-permute-done.9.got), custom_call_target="tpu_custom_call" | custom-call | tf_op jit(solution)/shard_map/finish/pallas_call | solution.py:419
  (3 shorter events, 0.1 us)
Async XLA Ops:
  0.0 10.1 %copy-start.1 = (s32[1,64,64]{2,1,0:T(8,128)S(1)}, s32[1,64,64]{2,1,0:T(8,128)}, u32[]{:S(2)}) copy-start(s32[1,64,64]{2,1,0:T(8,128)} %mask.1) | copy-start | bytes 49156
  0.0 10.1 %copy-start = (bf16[1280,64]{0,1:T(8,128)(2,1)S(1)}, bf16[1280,64]{0,1:T(8,128)(2,1)}, u32[]{:S(2)}) copy-start(bf16[1280,64]{0,1:T(8,128)(2,1)} %param.13) | copy-start | bytes 491524
  1.0 15.1 %collective-permute-start.3 = (bf16[256,640]{1,0:T(8,128)(2,1)S(1)}, bf16[256,640]{1,0:T(8,128)(2,1)S(1)}, u32[]{:S(2)}, u32[]{:S(2)}) collective-permute-start(bf16[256,640]{1,0:T(8,128)(2,1)S(1)} %shard_map.84), channel_id=1, source_target_pairs={{0,1},{1,0},{2,3},{3,2},{4,5},{5,4},{6,7},{7,6},{8,9},{9,8},{10,11... | collective-permute-start | bytes 983048 | tf_op jit(solution)/shard_map/ppermute | solution.py:398
  5.3 14.4 %collective-permute-start.4 = (bf16[256,640]{1,0:T(8,128)(2,1)S(1)}, bf16[256,640]{1,0:T(8,128)(2,1)S(1)}, u32[]{:S(2)}, u32[]{:S(2)}) collective-permute-start(bf16[256,640]{1,0:T(8,128)(2,1)S(1)} %get-tuple-element.41), channel_id=1, source_target_pairs={{0,1},{1,0},{2,3},{3,2},{4,5},{5,4},{6,7},{7,6},{8,9},{9,8},{10,11... | collective-permute-start | bytes 983048 | tf_op jit(solution)/shard_map/ppermute | solution.py:398
  5.4 31.0 %collective-permute-start = (bf16[256,256]{1,0:T(8,128)(2,1)S(1)}, bf16[256,256]{1,0:T(8,128)(2,1)S(1)}, u32[]{:S(2)}, u32[]{:S(2)}) collective-permute-start(bf16[256,256]{1,0:T(8,128)(2,1)S(1)} %get-tuple-element.29), channel_id=1, source_target_pairs={{0,1},{1,0},{2,3},{3,2},{4,5},{5,4},{6,7},{7,6},{8,9},{9,8},{10,11... | collective-permute-start | bytes 393224 | tf_op jit(solution)/shard_map/ppermute | solution.py:398
  7.4 28.2 %collective-permute-start.1 = (bf16[256,384]{1,0:T(8,128)(2,1)S(1)}, bf16[256,384]{1,0:T(8,128)(2,1)S(1)}, u32[]{:S(2)}, u32[]{:S(2)}) collective-permute-start(bf16[256,384]{1,0:T(8,128)(2,1)S(1)} %get-tuple-element.30), channel_id=1, source_target_pairs={{0,1},{1,0},{2,3},{3,2},{4,5},{5,4},{6,7},{7,6},{8,9},{9,8},{10,11... | collective-permute-start | bytes 589832 | tf_op jit(solution)/shard_map/ppermute | solution.py:398
  7.5 25.4 %collective-permute-start.2 = (bf16[256,640]{1,0:T(8,128)(2,1)S(1)}, bf16[256,640]{1,0:T(8,128)(2,1)S(1)}, u32[]{:S(2)}, u32[]{:S(2)}) collective-permute-start(bf16[256,640]{1,0:T(8,128)(2,1)S(1)} %get-tuple-element.36), channel_id=1, source_target_pairs={{0,1},{1,0},{2,3},{3,2},{4,5},{5,4},{6,7},{7,6},{8,9},{9,8},{10,11... | collective-permute-start | bytes 983048 | tf_op jit(solution)/shard_map/ppermute | solution.py:398
  39.1 1.5 %collective-permute-start.5 = (f32[3,72,256]{2,1,0:T(8,128)S(1)}, f32[3,72,256]{2,1,0:T(8,128)S(1)}, u32[]{:S(2)}, u32[]{:S(2)}) collective-permute-start(f32[3,72,256]{2,1,0:T(8,128)S(1)} %shard_map.89.own), channel_id=1, source_target_pairs={{0,2},{2,0},{4,6},{6,4},{8,10},{10,8},{12,14},{14,12},{16,18},{18,... | collective-permute-start | bytes 663560 | tf_op jit(solution)/shard_map/ppermute | solution.py:394
  40.7 8.5 %collective-permute-start.7 = (f32[72,256]{1,0:T(8,128)S(1)}, f32[72,256]{1,0:T(8,128)S(1)}, u32[]{:S(2)}, u32[]{:S(2)}) collective-permute-start(f32[72,256]{1,0:T(8,128)S(1)} %get-tuple-element.49), channel_id=1, source_target_pairs={{0,4},{1,5},{2,7},{3,6},{4,8},{5,9},{6,11},{7,10},{8,12},{9,13},{1... | collective-permute-start | bytes 221192 | tf_op jit(solution)/shard_map/ppermute | solution.py:408
  42.5 6.8 %collective-permute-start.8 = (f32[72,256]{1,0:T(8,128)S(1)}, f32[72,256]{1,0:T(8,128)S(1)}, u32[]{:S(2)}, u32[]{:S(2)}) collective-permute-start(f32[72,256]{1,0:T(8,128)S(1)} %get-tuple-element.50), channel_id=1, source_target_pairs={{0,8},{1,9},{2,11},{3,10},{4,12},{5,13},{6,15},{7,14},{8,16},{9,17... | collective-permute-start | bytes 221192 | tf_op jit(solution)/shard_map/ppermute | solution.py:408
  44.1 5.2 %collective-permute-start.6 = (f32[40,256]{1,0:T(8,128)S(1)}, f32[40,256]{1,0:T(8,128)S(1)}, u32[]{:S(2)}, u32[]{:S(2)}) collective-permute-start(f32[40,256]{1,0:T(8,128)S(1)} %get-tuple-element.48.here), channel_id=1, source_target_pairs={{0,1},{1,0},{2,3},{3,2},{4,5},{5,4},{6,7},{7,6},{8,9},{9,8},{10,11... | collective-permute-start | bytes 122888 | tf_op jit(solution)/shard_map/ppermute | solution.py:398
  49.3 1.4 %collective-permute-start.9 = (f32[40,256]{1,0:T(8,128)S(1)}, f32[40,256]{1,0:T(8,128)S(1)}, u32[]{:S(2)}, u32[]{:S(2)}) collective-permute-start(f32[40,256]{1,0:T(8,128)S(1)} %get-tuple-element.52), channel_id=1, source_target_pairs={{0,2},{2,0},{4,6},{6,4},{8,10},{10,8},{12,14},{14,12},{16,18},{18,... | collective-permute-start | bytes 122888 | tf_op jit(solution)/shard_map/ppermute | solution.py:394

commit v3 on v2

--- a/solution.py
+++ b/solution.py
@@ -49,11 +49,13 @@
     return mean, jnp.sum(centred * centred, axis=1, keepdims=True)
 
 
-def merged(a, b, a_count, b_count):
-    count = a_count + b_count
-    gap = b[0] - a[0]
-    mean = a[0] + gap * (b_count / count)
-    return mean, a[1] + b[1] + gap * gap * (a_count * b_count / count)
+def merged(near, near_count, x):
+    mean, square = near
+    count = near_count + x.shape[1]
+    gap = x - mean
+    total = jnp.sum(gap, axis=1, keepdims=True)
+    square = square + jnp.sum(gap * gap, axis=1, keepdims=True)
+    return mean + total * (1.0 / count), square - total * total * (1.0 / count)
 
 
 def split2(x):
@@ -200,37 +202,52 @@
 
 def halves(x):
     odd = lax.axis_index("blk") % 2 == 1
-    own, other = [], []
-    for b in range(x.shape[0] // BLOCK):
-        low = x[b * BLOCK : b * BLOCK + STRIDE]
-        high = x[b * BLOCK + STRIDE : (b + 1) * BLOCK]
-        own.append(jnp.where(odd, high, low))
-        other.append(jnp.where(odd, low, high))
-    weights = x[-PACKED:]
-    return jnp.concatenate(own + [weights], axis=0), jnp.concatenate(other + [weights], axis=0)
-
-
-def sum_chip(own, got, here, next_chip, second_chip):
-    here[...] = halves(own[0] + got[0])[0]
+    low, high, weights = x[:STRIDE], x[STRIDE:BLOCK], x[BLOCK:]
+    own, other = jnp.where(odd, high, low), jnp.where(odd, low, high)
+    if weights.shape[0]:
+        own = jnp.concatenate([own, weights], axis=0)
+        other = jnp.concatenate([other, weights], axis=0)
+    return own, other
+
+
+def sum_early(own, got, here, next_chip, second_chip):
+    for t, out in enumerate((here, next_chip, second_chip)):
+        out[...] = halves(own[t] + got[t])[0]
+
+
+def sum_chip(own, got, *refs):
+    here, next_chip, second_chip = refs[-3:]
     next_chip[...] = own[1] + got[1]
     second_chip[...] = own[2] + got[2]
+    at = 0
+    for i in range(0, len(refs) - 3, 3):
+        a, b, c = refs[i : i + 3]
+        here[at : at + a.shape[0]] = a[...] + b[...] + c[...]
+        at += a.shape[0]
+    here[at:] = halves(own[0] + got[0])[0]
 
 
 def sum_far(here, across, first, second, mine, other):
     kept, passed = halves(first[...] + second[...])
-    mine[...] = here[...] + across[...] + kept
+    before = here.shape[0] - kept.shape[0]
+    mine[:before] = here[:before] + across[:before]
+    mine[before:] = here[before:] + across[before:] + kept
     other[...] = passed
 
 
 def finish(mine, got, out):
     odd = lax.axis_index("blk") % 2 == 1
-    total = mine[...] + got[...]
-    packed = total[-PACKED:]
+    packed = mine[STRIDE : STRIDE + PACKED]
     packed = jnp.where(odd, packed[:, LAT // 2 :], packed[:, : LAT // 2])
-    weights = [packed[:, k * WINDOW : (k + 1) * WINDOW] for k in range(STRIDE // PACKED)]
-    weights = dot(jnp.concatenate(weights, axis=0).astype(BF16), repeat_map())
-    for b in range(out.shape[0]):
-        out[b] = total[b * STRIDE : (b + 1) * STRIDE] / weights
+    plain = [packed[:, k * WINDOW : (k + 1) * WINDOW] for k in range(STRIDE // PACKED)]
+    weights = dot(jnp.concatenate(plain, axis=0).astype(BF16), repeat_map())
+    batch_count = out.shape[0]
+    for b in range(batch_count):
+        at = b * STRIDE + PACKED * (b > 0)
+        total = mine[at : at + STRIDE]
+        if b == batch_count - 1:
+            total = total + got[...]
+        out[b] = total / weights
 
 
 def extend(
@@ -250,7 +267,7 @@
     x = arrived[...]
     near = own_mean[s], own_square[s]
     half = far_weights.shape[0] - TAIL
-    mean[0], square[0] = merged(near, moments(x.astype(F32)), half, x.shape[1])
+    mean[0], square[0] = merged(near, half, x.astype(F32))
     x = jnp.concatenate([own_tail[s], x], axis=1)
     for first, last in column_groups(own_acc.shape[2]):
         w = far_weights[: x.shape[1], first:last]
@@ -273,12 +290,14 @@
     *rest,
 ):
     first_pass = s % 2 == 0
+    q_even, q_odd, keys, values, context = rest[-5:]
+    rest = rest[:-5]
     if first_pass:
         _, guided_out = rest[:2]
         sums_out = rest[2:]
     else:
         spread_map, mask_tile, guided_in = rest[:3]
-        before = rest[3:-2]
+        mask_blocks = rest[3:-2]
         blocks, frame = rest[-2:]
     tokens, far_count = arrived.shape
     columns = own_acc.shape[2]
@@ -286,7 +305,7 @@
     slab = s if own_acc.shape[0] > 1 else 0
     x = arrived[...]
     near = own_mean[slab], own_square[slab]
-    mean, square = merged(near, moments(x.astype(F32)), near_count, far_count)
+    mean, square = merged(near, near_count, x.astype(F32))
     scale = lax.rsqrt(square / (near_count + far_count) + 1e-05)
     offset = mean * scale
     if near_count == half:
@@ -298,12 +317,11 @@
     factor = math.log2(math.e) / HEAD**0.5
     query_scale, query_offset = scale * factor, offset * factor
     first_head = iota((1, PAIR), 1) < HEAD
-    ones = jnp.ones((tokens, PAIR), BF16)
     none = jnp.zeros((tokens, PAIR), BF16)
-    ones_even = jnp.where(first_head, ones, none)
-    ones_odd = jnp.where(first_head, none, ones)
-    out = None
-    for first, last in column_groups(columns):
+    groups = column_groups(columns)
+    direct = []
+
+    def project(first, last):
         total = dot(x, far_weights[rows, first:last])
         sums = sums_in[0:8, first:last]
         if start:
@@ -312,35 +330,59 @@
             total = total[:tokens]
         total = total + own_acc[slab, :, first:last]
         sums = sums[0:1]
-        contexts = []
         for p in range((min(last, 3 * width) - first) // TRIPLE):
+            place = slice(first // 3 + p * PAIR, first // 3 + (p + 1) * PAIR)
 
             def part(j, by, less):
                 places = slice(p * TRIPLE + j * PAIR, p * TRIPLE + (j + 1) * PAIR)
                 return total[:, places] * by - less * sums[:, places]
 
-            query = part(0, query_scale, query_offset)
-            k = part(1, scale, offset).astype(BF16)
-            v = part(2, scale, offset).astype(BF16)
-            probs = []
-            for q in (jnp.where(first_head, query, 0.0), jnp.where(first_head, 0.0, query)):
-                scores = dot_nt(q.astype(BF16), k)
-                top = jnp.max(scores, axis=1, keepdims=True)
-                probs.append(jnp.exp2(scores - top).astype(BF16))
-            stacked = jnp.concatenate(
-                [
-                    jnp.concatenate([jnp.where(first_head, v, none), ones_even], axis=1),
-                    jnp.concatenate([jnp.where(first_head, none, v), ones_odd], axis=1),
-                ],
-                axis=0,
-            )
-            both = dot(jnp.concatenate(probs, axis=1), stacked)
-            contexts.append((both[:, :PAIR] / both[:, PAIR:]).astype(BF16))
-        here = slice(first // 3, first // 3 + len(contexts) * PAIR)
-        more = dot(jnp.concatenate(contexts, axis=1), out_weights[here])
-        out = more if out is None else out + more
+            query = part(0, query_scale, query_offset).astype(BF16)
+            q_even[:, place] = jnp.where(first_head, query, none)
+            q_odd[:, place] = jnp.where(first_head, none, query)
+            keys[:, place] = part(1, scale, offset).astype(BF16)
+            values[:, place] = part(2, scale, offset).astype(BF16)
         if last > 3 * width:
-            out = out + total[:, 3 * width - first :]
+            direct.append(total[:, 3 * width - first :])
+
+    ones = jnp.ones((tokens, PAIR), BF16)
+    ones_even = jnp.where(first_head, ones, none)
+    ones_odd = jnp.where(first_head, none, ones)
+
+    probs = {}
+
+    def score(p):
+        place = slice(p * PAIR, (p + 1) * PAIR)
+        k = keys[:, place]
+        both = []
+        for q in (q_even, q_odd):
+            scores = dot_nt(q[:, place], k)
+            top = jnp.max(scores, axis=1, keepdims=True)
+            both.append(jnp.exp2(scores - top).astype(BF16))
+        probs[p] = jnp.concatenate(both, axis=1)
+
+    def attention(p):
+        place = slice(p * PAIR, (p + 1) * PAIR)
+        v = values[:, place]
+        stacked = jnp.concatenate(
+            [
+                jnp.concatenate([jnp.where(first_head, v, none), ones_even], axis=1),
+                jnp.concatenate([jnp.where(first_head, none, v), ones_odd], axis=1),
+            ],
+            axis=0,
+        )
+        both = dot(probs.pop(p), stacked)
+        context[:, place] = (both[:, :PAIR] / both[:, PAIR:]).astype(BF16)
+
+    pairs = width // PAIR
+    for g in groups:
+        project(*g)
+    score(0)
+    for p in range(pairs):
+        if p + 1 < pairs:
+            score(p + 1)
+        attention(p)
+    out = dot(context[...], out_weights[...]) + direct[0]
     if first_pass:
         guided_out[...] = (1.0 - guidance) * out
         return
@@ -358,15 +400,10 @@
             places = slice(a * LAT + h * LANES, a * LAT + (h + 1) * LANES)
             frame[pl.ds(a, GRID, stride=PATCH), :] = spread[:, places]
         rolled = to_frame(frame, shift)
-        at = sum(x.shape[1] for x in before[:-1])
         for t in range(BLOCKS):
-            blocks[t, at : at + BLOCK, lanes] = rolled[t * BLOCK : (t + 1) * BLOCK]
-    at = 0
-    for i, x in enumerate(before):
-        if i == len(before) - 1:
-            at += BLOCK
-        blocks[:, at : at + x.shape[1]] = x[...]
-        at += x.shape[1]
+            blocks[t, :BLOCK, lanes] = rolled[t * BLOCK : (t + 1) * BLOCK]
+    for x in mask_blocks:
+        blocks[:, BLOCK:] = x[...]
 
 
 def call(kernel, args, outs, scratch=(), flops=0, limit=1 << 20, smem=0):
@@ -408,14 +445,28 @@
     return lax.ppermute(x, ("blk", "mp"), pairs)
 
 
-def blend(blocks, batch_count):
+def blend_early(blocks):
+    part = (blocks.shape[1] - STRIDE, LAT)
+    got = partner(blocks)
+    here, first, second = call(sum_early, (blocks, got), [(part, F32)] * 3)
+    count = lax.axis_size("blk")
+    first = lax.ppermute(first, "blk", [(i, (i + 2) % count) for i in range(count)])
+    second = lax.ppermute(second, "blk", [(i, (i + 4) % count) for i in range(count)])
+    return here, first, second
+
+
+def blend_last(blocks, early, batch_count):
     whole, part = blocks.shape[1:], (batch_count * STRIDE + PACKED, LAT)
     got = partner(blocks)
-    here, first, second = call(sum_chip, (blocks, got), [(part, F32), (whole, F32), (whole, F32)])
+    here, first, second = call(
+        sum_chip, (blocks, got, *early), [(part, F32), (whole, F32), (whole, F32)]
+    )
     first = moved(first, 1)
     second = moved(second, 2)
     other_side = across(here)
-    mine, other = call(sum_far, (here, other_side, first, second), [(part, F32)] * 2)
+    mine, other = call(
+        sum_far, (here, other_side, first, second), [(part, F32), ((STRIDE, LAT), F32)]
+    )
     return pl.pallas_call(
         finish,
         out_shape=jax.ShapeDtypeStruct((batch_count, STRIDE, LAT), F32),
@@ -476,8 +527,9 @@
     acc, mean, square, tail, sums, far_weights, out_weights = prepared[:7]
     spread_map, mask_tile, mask_blocks = prepared[7:]
     own = (acc, mean, square)
+    work = [pltpu.VMEM((tokens, width), BF16)] * 5
     flops = 2 * tokens * (half * 3 * width + 2 * tokens * width)
-    blocks = []
+    early = []
     token = mask_blocks
     at = 0
     for s in range(sequences):
@@ -497,7 +549,7 @@
             at += 1
         args = (offsets, arrived[at], *near, tail, sums, far_weights, out_weights)
         at += 1
-        scratch = ()
+        scratch = work
         if s % passes == 0:
             args += ((token, pl.ANY),)
             results = [((tokens, 2 * OUTW), F32)]
@@ -506,11 +558,11 @@
         else:
             args += (spread_map, mask_tile, token)
             rows = BLOCK
-            if s == sequences - 1:
-                args += (*blocks, mask_blocks)
-                rows = batch_count * BLOCK + PACKED
+            if s < passes:
+                args += (mask_blocks,)
+                rows += PACKED
             results = [((BLOCKS, rows, LAT), F32)]
-            scratch = frame
+            scratch = frame + work
         token, *more = call(
             functools.partial(attend, s, near_count, width),
             args,
@@ -523,8 +575,9 @@
         if more:
             (sums,) = more
         if s % passes:
-            blocks.append(token)
-    return blend(blocks[-1], batch_count)
+            if s < sequences - 1:
+                early += blend_early(token)
+    return blend_last(token, early, batch_count)
 
 
 def solution(mesh):

time: 51.7 us -> 53.5 us (1.035)
  waiting for transfers between devices: 16.8 us -> 19.8 us
  Pallas kernels: 21.4 us -> 18.9 us
  starting transfers between devices: 12.6 us -> 13.9 us
    ppermute x2, waiting for transfers between devices: 0.11 us -> 5.71 us  [moved(): return lax.ppermute(x, ('blk', 'mp'), pairs)]
    ppermute x6, waiting for transfers between devices: 14.3 us -> 8.85 us  [across(): return lax.ppermute(x, 'mp', [(0, 1), (1, 0)])]
    ppermute x0 -> x2, waiting for transfers between devices: none -> 4.04 us  [the longest x1 3.33 us: blend_early(): lax.ppermute(first, 'blk', [(i, (i + 2) % count) for i in range(count)])]
    ppermute x0 -> x2, starting transfers between devices: none -> 3.33 us  [the longest x1 1.75 us: blend_early(): lax.ppermute(first, 'blk', [(i, (i + 2) % count) for i in range(count)])]
    pallas_call x10 -> x11, Pallas kernels: 20.5 us -> 18.1 us  [call(): pl.pallas_call(kernel, out_shape=[pltpu.VMEM(shape, dtype) for shape, dty...]
    ppermute x2, starting transfers between devices: 3.34 us -> 1.56 us  [moved(): return lax.ppermute(x, ('blk', 'mp'), pairs)]
    ppermute x2 -> x3, waiting for transfers between devices: 2.33 us -> 1.18 us  [partner(): return lax.ppermute(x, 'blk', [(i, i ^ 1) for i in range(count)])]
  transfers between devices with their start and end apart: 10 -> 13, of which waited for: 6 -> 9; matrix products, arithmetic and copies ran while one was open for 0% -> 0% of each run, Pallas kernels for 32% -> 32%
where the time goes in v3:
time: 53.5 us; the launch traced here: 53.4 us
  waiting for transfers between devices  19.8 us (37%)
  Pallas kernels  18.9 us (35%)
  starting transfers between devices  13.9 us (26%)
  between operations  0.8 us (1%)
    pallas_call x11, Pallas kernels, call(): pl.pallas_call(kernel, out_shape=[pltpu.VMEM(shape, dtype) for shape, dty...  18.1 us
    ppermute x6, waiting for transfers between devices, across(): return lax.ppermute(x, 'mp', [(0, 1), (1, 0)])  8.85 us
    ppermute x6, starting transfers between devices, across(): return lax.ppermute(x, 'mp', [(0, 1), (1, 0)])  8.76 us
    ppermute x2, waiting for transfers between devices, moved(): return lax.ppermute(x, ('blk', 'mp'), pairs)  5.71 us
    ppermute x1, waiting for transfers between devices, blend_early(): lax.ppermute(first, 'blk', [(i, (i + 2) % count) for i in range(count)])  3.33 us
    ppermute x1, starting transfers between devices, blend_early(): lax.ppermute(first, 'blk', [(i, (i + 2) % count) for i in range(count)])  1.75 us
    ppermute x1, starting transfers between devices, blend_early(): lax.ppermute(second, 'blk', [(i, (i + 4) % count) for i in range(count)])  1.58 us
    ppermute x2, starting transfers between devices, moved(): return lax.ppermute(x, ('blk', 'mp'), pairs)  1.56 us
  transfers between devices with their start and end apart: 13, of which 9 were waited for; matrix products, arithmetic and copies ran while one was open for 0% of the time, Pallas kernels for 32%

profile of v3, /device:TPU:0, one launch (start us, length us, event | category | flops | bytes accessed | tf_op | source)
XLA Modules:
  0.0 53.4 jit_solution(6281068724417849788)
XLA Ops:
  0.0 1.0 %shard_map.84 = bf16[256,640]{1,0:T(8,128)(2,1)S(1)} custom-call(bf16[1,2,2,256,640]{4,3,2,1,0:T(8,128)(2,1)} %features.5), custom_call_target="tpu_custom_call" | custom-call | bytes 1048576 | tf_op jit(solution)/shard_map/pallas_call | solution.py:418
  1.0 3.1 %collective-permute-start.3 = (bf16[256,640]{1,0:T(8,128)(2,1)S(1)}, bf16[256,640]{1,0:T(8,128)(2,1)S(1)}, u32[]{:S(2)}, u32[]{:S(2)}) collective-permute-start(bf16[256,640]{1,0:T(8,128)(2,1)S(1)} %shard_map.84), channel_id=1, source_target_pairs={{0,1},{1,0},{2,3},{3,2},{4,5},{5,4},{6,7},{7,6},{8,9},{9,8},{10,11... | collective-permute-start | bytes 983048 | tf_op jit(solution)/shard_map/ppermute | solution.py:435
  4.1 1.2 %shard_map.82 = (bf16[256,640]{1,0:T(8,128)(2,1)S(1)}, bf16[256,640]{1,0:T(8,128)(2,1)S(1)}, bf16[256,384]{1,0:T(8,128)(2,1)S(1)}, bf16[256,256]{1,0:T(8,128)(2,1)S(1)}) custom-call(bf16[1,2,2,256,640]{4,3,2,1,0:T(8,128)(2,1)} %features.5), custom_call_target="tpu_custom_call" | custom-call | bytes 1048576 | tf_op jit(solution)/shard_map/pallas_call | solution.py:418
  5.3 0.1 collective-permute-start.4
  5.4 2.0 %collective-permute-start.2 = (bf16[256,640]{1,0:T(8,128)(2,1)S(1)}, bf16[256,640]{1,0:T(8,128)(2,1)S(1)}, u32[]{:S(2)}, u32[]{:S(2)}) collective-permute-start(bf16[256,640]{1,0:T(8,128)(2,1)S(1)} %get-tuple-element.39), channel_id=1, source_target_pairs={{0,1},{1,0},{2,3},{3,2},{4,5},{5,4},{6,7},{7,6},{8,9},{9,8},{10,11... | collective-permute-start | bytes 983048 | tf_op jit(solution)/shard_map/ppermute | solution.py:435
  7.4 0.1 collective-permute-start.1
  7.5 1.9 %collective-permute-start = (bf16[256,256]{1,0:T(8,128)(2,1)S(1)}, bf16[256,256]{1,0:T(8,128)(2,1)S(1)}, u32[]{:S(2)}, u32[]{:S(2)}) collective-permute-start(bf16[256,256]{1,0:T(8,128)(2,1)S(1)} %get-tuple-element.32), channel_id=1, source_target_pairs={{0,1},{1,0},{2,3},{3,2},{4,5},{5,4},{6,7},{7,6},{8,9},{9,8},{10,11... | collective-permute-start | bytes 393224 | tf_op jit(solution)/shard_map/ppermute | solution.py:435
  10.1 6.0 %shard_map.83 = (f32[4,256,2048]{2,1,0:T(8,128)S(1)}, f32[4,256,1]{2,1,0:T(8,128)S(1)}, f32[4,256,1]{2,1,0:T(8,128)S(1)}, bf16[4,256,128]{2,1,0:T(8,128)(2,1)S(1...) custom-call(s32[1]{0:T(128)S(6)} %copy.9.offsets, ...), custom_call_target="tpu_custom_call" | custom-call | flops 2516582400 | bytes 1048576 | tf_op jit(solution)/shard_map/pallas_call | solution.py:418
  16.1 0.0 collective-permute-done.3.arrived
  16.1 2.5 %shard_map.85 = (f32[256,128]{1,0:T(8,128)S(1)}, f32[8,2048]{1,0:T(8,128)S(1)}) custom-call(s32[1]{0:T(128)S(6)} %copy.9.offsets, bf16[256,640]{1,0:T(8,128)(2,1)S(1)} %collective-permute-done.3.arrived, f32[4,256,2048]{2,1,0:T(8,128)S(1)} %get-tuple-element.34.own_acc, f32[4,256,1]{2,1,0:T(8,128)S(1)} %get-tuple-element.35.own_mean, ...), custom_call_target="tpu_custom_call" | custom-call | flops 796917760 | bytes 1048576 | tf_op jit(solution)/shard_map/pallas_call | solution.py:418
  18.6 1.1 %collective-permute-done.4.arrived = bf16[256,640]{1,0:T(8,128)(2,1)S(1)} collective-permute-done((bf16[256,640]{1,0:T(8,128)(2,1)S(1)}, bf16[256,640]{1,0:T(8,128)(2,1)S(1)}, u32[]{:S(2)}, u32[]{:S(2)}) %collective-permute-start.4) | collective-permute-done | bytes 327712 | tf_op jit(solution)/shard_map/ppermute | solution.py:435
  19.7 2.4 %shard_map.86.rest_0_.own = f32[3,40,256]{2,1,0:T(8,128)S(1)} custom-call(s32[1]{0:T(128)S(6)} %copy.9.offsets, bf16[256,640]{1,0:T(8,128)(2,1)S(1)} %collective-permute-done.4.arrived, f32[4,256,2048]{2,1,0:T(8,128)S(1)} %get-tuple-element.34.own_acc, f32[4,256,1]{2,1,0:T(8,128)S(1)} %get-tuple-element.35.own_mean, ...), custom_call_target="tpu_custom_call" | custom-call | flops 796917760 | bytes 1048576 | tf_op jit(solution)/shard_map/pallas_call | solution.py:418
  22.1 0.1 collective-permute-start.6
  22.2 4.5 %collective-permute-done.2.arrived = bf16[256,640]{1,0:T(8,128)(2,1)S(1)} collective-permute-done((bf16[256,640]{1,0:T(8,128)(2,1)S(1)}, bf16[256,640]{1,0:T(8,128)(2,1)S(1)}, u32[]{:S(2)}, u32[]{:S(2)}) %collective-permute-start.2) | collective-permute-done | bytes 327712 | tf_op jit(solution)/shard_map/ppermute | solution.py:435
  26.7 2.2 %shard_map.87.token.rest_2_ = f32[256,128]{1,0:T(8,128)S(1)} custom-call(s32[1]{0:T(128)S(6)} %copy.9.offsets, bf16[256,640]{1,0:T(8,128)(2,1)S(1)} %collective-permute-done.2.arrived, f32[4,256,2048]{2,1,0:T(8,128)S(1)} %get-tuple-element.34.own_acc, f32[4,256,1]{2,1,0:T(8,128)S(1)} %get-tuple-element.35.own_mean, ...), custom_call_target="tpu_custom_call" | custom-call | flops 796917760 | bytes 1048576 | tf_op jit(solution)/shard_map/pallas_call | solution.py:418
  28.9 2.0 %collective-permute-done.1.arrived = bf16[256,384]{1,0:T(8,128)(2,1)S(1)} collective-permute-done((bf16[256,384]{1,0:T(8,128)(2,1)S(1)}, bf16[256,384]{1,0:T(8,128)(2,1)S(1)}, u32[]{:S(2)}, u32[]{:S(2)}) %collective-permute-start.1) | collective-permute-done | bytes 196640 | tf_op jit(solution)/shard_map/ppermute | solution.py:435
  30.9 0.8 %shard_map.88 = (f32[1,256,2048]{2,1,0:T(8,128)S(1)}, f32[1,256,1]{2,1,0:T(8,128)S(1)}, f32[1,256,1]{2,1,0:T(8,128)S(1)}) custom-call(bf16[256,384]{1,0:T(8,128)(2,1)S(1)} %collective-permute-done.1.arrived, f32[4,256,2048]{2,1,0:T(8,128)S(1)} %get-tuple-element.34.own_acc, f32[4,256,1]{2,1,0:T(8,128)S(1)} %get-tuple-element.35.own_mean, ...), custom_call_target="tpu_custom_call" | custom-call | flops 377487360 | bytes 1048576 | tf_op jit(solution)/shard_map/pallas_call | solution.py:418
  31.7 1.2 %collective-permute-done.arrived = bf16[256,256]{1,0:T(8,128)(2,1)S(1)} collective-permute-done((bf16[256,256]{1,0:T(8,128)(2,1)S(1)}, bf16[256,256]{1,0:T(8,128)(2,1)S(1)}, u32[]{:S(2)}, u32[]{:S(2)}) %collective-permute-start) | collective-permute-done | bytes 131104 | tf_op jit(solution)/shard_map/ppermute | solution.py:435
  32.9 2.0 %shard_map.89.own = f32[3,32,256]{2,1,0:T(8,128)S(1)} custom-call(s32[1]{0:T(128)S(6)} %copy.9.offsets, bf16[256,256]{1,0:T(8,128)(2,1)S(1)} %collective-permute-done.arrived, f32[1,256,2048]{2,1,0:T(8,128)S(1)} %get-tuple-element.48.own_acc, f32[1,256,1]{2,1,0:T(8,128)S(1)} %get-tuple-element.49.own_mean, f32[1,256,1]{2,1,0:T(8,128)S(1)} %get-tuple-element.50.own_square, ...), custom_call_target="tpu_custom_call" | custom-call | flops 796917760 | bytes 1048576 | tf_op jit(solution)/shard_map/pallas_call | solution.py:418
  34.9 0.1 collective-permute-start.5
  35.0 0.0 collective-permute-done.6.got
  35.0 1.7 %collective-permute-start.7 = (f32[24,256]{1,0:T(8,128)S(1)}, f32[24,256]{1,0:T(8,128)S(1)}, u32[]{:S(2)}, u32[]{:S(2)}) collective-permute-start(f32[24,256]{1,0:T(8,128)S(1)} %get-tuple-element.52), channel_id=1, source_target_pairs={{0,4},{2,6},{4,8},{6,10},{8,12},{10,14},{12,16},{14,18},{16,20},{1... | collective-permute-start | bytes 73736 | tf_op jit(solution)/shard_map/ppermute | solution.py:453
  36.8 1.6 %collective-permute-start.8 = (f32[24,256]{1,0:T(8,128)S(1)}, f32[24,256]{1,0:T(8,128)S(1)}, u32[]{:S(2)}, u32[]{:S(2)}) collective-permute-start(f32[24,256]{1,0:T(8,128)S(1)} %get-tuple-element.53), channel_id=1, source_target_pairs={{0,8},{2,10},{4,12},{6,14},{8,16},{10,18},{12,20},{14,22},{16,24},... | collective-permute-start | bytes 73736 | tf_op jit(solution)/shard_map/ppermute | solution.py:454
  38.4 3.3 %collective-permute-done.7.refs_1_ = f32[24,256]{1,0:T(8,128)S(1)} collective-permute-done((f32[24,256]{1,0:T(8,128)S(1)}, f32[24,256]{1,0:T(8,128)S(1)}, u32[]{:S(2)}, u32[]{:S(2)}) %collective-permute-start.7) | collective-permute-done | bytes 24608 | tf_op jit(solution)/shard_map/ppermute | solution.py:453
  41.7 0.7 %collective-permute-done.8.refs_2_ = f32[24,256]{1,0:T(8,128)S(1)} collective-permute-done((f32[24,256]{1,0:T(8,128)S(1)}, f32[24,256]{1,0:T(8,128)S(1)}, u32[]{:S(2)}, u32[]{:S(2)}) %collective-permute-start.8) | collective-permute-done | bytes 24608 | tf_op jit(solution)/shard_map/ppermute | solution.py:454
  42.4 1.6 %collective-permute-start.9 = (f32[40,256]{1,0:T(8,128)S(1)}, f32[40,256]{1,0:T(8,128)S(1)}, u32[]{:S(2)}, u32[]{:S(2)}) collective-permute-start(f32[40,256]{1,0:T(8,128)S(1)} %get-tuple-element.54.here), channel_id=1, source_target_pairs={{0,1},{1,0},{2,3},{3,2},{4,5},{5,4},{6,7},{7,6},{8,9},{9,8},{10,11... | collective-permute-start | bytes 122888 | tf_op jit(solution)/shard_map/ppermute | solution.py:435
  44.0 1.6 %collective-permute-start.10 = (f32[32,256]{1,0:T(8,128)S(1)}, f32[32,256]{1,0:T(8,128)S(1)}, u32[]{:S(2)}, u32[]{:S(2)}) collective-permute-start(f32[32,256]{1,0:T(8,128)S(1)} %get-tuple-element.55), channel_id=1, source_target_pairs={{0,4},{1,5},{2,7},{3,6},{4,8},{5,9},{6,11},{7,10},{8,12},{9,13},{1... | collective-permute-start | bytes 98312 | tf_op jit(solution)/shard_map/ppermute | solution.py:445
  45.6 5.0 %collective-permute-done.10.first = f32[32,256]{1,0:T(8,128)S(1)} collective-permute-done((f32[32,256]{1,0:T(8,128)S(1)}, f32[32,256]{1,0:T(8,128)S(1)}, u32[]{:S(2)}, u32[]{:S(2)}) %collective-permute-start.10) | collective-permute-done | bytes 32800 | tf_op jit(solution)/shard_map/ppermute | solution.py:445
  50.6 0.7 %collective-permute-done.11.second = f32[32,256]{1,0:T(8,128)S(1)} collective-permute-done((f32[32,256]{1,0:T(8,128)S(1)}, f32[32,256]{1,0:T(8,128)S(1)}, u32[]{:S(2)}, u32[]{:S(2)}) %collective-permute-start.11) | collective-permute-done | bytes 32800 | tf_op jit(solution)/shard_map/ppermute | solution.py:445
  51.3 0.1 collective-permute-start.12
  51.4 1.2 %collective-permute-done.12.got = f32[16,256]{1,0:T(8,128)S(1)} collective-permute-done((f32[16,256]{1,0:T(8,128)S(1)}, f32[16,256]{1,0:T(8,128)S(1)}, u32[]{:S(2)}, u32[]{:S(2)}) %collective-permute-start.12) | collective-permute-done | bytes 16416 | tf_op jit(solution)/shard_map/ppermute | solution.py:431
  52.6 0.8 %finish.1 = f32[2,16,256]{2,1,0:T(8,128)} custom-call(f32[40,256]{1,0:T(8,128)S(1)} %get-tuple-element.57.mine, f32[16,256]{1,0:T(8,128)S(1)} %collective-permute-done.12.got), custom_call_target="tpu_custom_call" | custom-call | tf_op jit(solution)/shard_map/finish/pallas_call | solution.py:470
  (10 shorter events, 0.1 us)
Async XLA Ops:
  0.0 10.1 %copy-start = (bf16[1280,64]{0,1:T(8,128)(2,1)S(1)}, bf16[1280,64]{0,1:T(8,128)(2,1)}, u32[]{:S(2)}) copy-start(bf16[1280,64]{0,1:T(8,128)(2,1)} %param.13) | copy-start | bytes 491524
  0.0 10.1 %copy-start.1 = (s32[1,64,64]{2,1,0:T(8,128)S(1)}, s32[1,64,64]{2,1,0:T(8,128)}, u32[]{:S(2)}) copy-start(s32[1,64,64]{2,1,0:T(8,128)} %mask.1) | copy-start | bytes 49156
  1.0 15.1 %collective-permute-start.3 = (bf16[256,640]{1,0:T(8,128)(2,1)S(1)}, bf16[256,640]{1,0:T(8,128)(2,1)S(1)}, u32[]{:S(2)}, u32[]{:S(2)}) collective-permute-start(bf16[256,640]{1,0:T(8,128)(2,1)S(1)} %shard_map.84), channel_id=1, source_target_pairs={{0,1},{1,0},{2,3},{3,2},{4,5},{5,4},{6,7},{7,6},{8,9},{9,8},{10,11... | collective-permute-start | bytes 983048 | tf_op jit(solution)/shard_map/ppermute | solution.py:435
  5.3 14.4 %collective-permute-start.4 = (bf16[256,640]{1,0:T(8,128)(2,1)S(1)}, bf16[256,640]{1,0:T(8,128)(2,1)S(1)}, u32[]{:S(2)}, u32[]{:S(2)}) collective-permute-start(bf16[256,640]{1,0:T(8,128)(2,1)S(1)} %get-tuple-element.44), channel_id=1, source_target_pairs={{0,1},{1,0},{2,3},{3,2},{4,5},{5,4},{6,7},{7,6},{8,9},{9,8},{10,11... | collective-permute-start | bytes 983048 | tf_op jit(solution)/shard_map/ppermute | solution.py:435
  5.4 21.3 %collective-permute-start.2 = (bf16[256,640]{1,0:T(8,128)(2,1)S(1)}, bf16[256,640]{1,0:T(8,128)(2,1)S(1)}, u32[]{:S(2)}, u32[]{:S(2)}) collective-permute-start(bf16[256,640]{1,0:T(8,128)(2,1)S(1)} %get-tuple-element.39), channel_id=1, source_target_pairs={{0,1},{1,0},{2,3},{3,2},{4,5},{5,4},{6,7},{7,6},{8,9},{9,8},{10,11... | collective-permute-start | bytes 983048 | tf_op jit(solution)/shard_map/ppermute | solution.py:435
  7.4 23.5 %collective-permute-start.1 = (bf16[256,384]{1,0:T(8,128)(2,1)S(1)}, bf16[256,384]{1,0:T(8,128)(2,1)S(1)}, u32[]{:S(2)}, u32[]{:S(2)}) collective-permute-start(bf16[256,384]{1,0:T(8,128)(2,1)S(1)} %get-tuple-element.33), channel_id=1, source_target_pairs={{0,1},{1,0},{2,3},{3,2},{4,5},{5,4},{6,7},{7,6},{8,9},{9,8},{10,11... | collective-permute-start | bytes 589832 | tf_op jit(solution)/shard_map/ppermute | solution.py:435
  7.5 25.4 %collective-permute-start = (bf16[256,256]{1,0:T(8,128)(2,1)S(1)}, bf16[256,256]{1,0:T(8,128)(2,1)S(1)}, u32[]{:S(2)}, u32[]{:S(2)}) collective-permute-start(bf16[256,256]{1,0:T(8,128)(2,1)S(1)} %get-tuple-element.32), channel_id=1, source_target_pairs={{0,1},{1,0},{2,3},{3,2},{4,5},{5,4},{6,7},{7,6},{8,9},{9,8},{10,11... | collective-permute-start | bytes 393224 | tf_op jit(solution)/shard_map/ppermute | solution.py:435
  22.1 12.9 %collective-permute-start.6 = (f32[3,40,256]{2,1,0:T(8,128)S(1)}, f32[3,40,256]{2,1,0:T(8,128)S(1)}, u32[]{:S(2)}, u32[]{:S(2)}) collective-permute-start(f32[3,40,256]{2,1,0:T(8,128)S(1)} %shard_map.86.rest_0_.own), channel_id=1, source_target_pairs={{0,2},{2,0},{4,6},{6,4},{8,10},{10,8},{12,14},{14,12},{16,18},{18,... | collective-permute-start | bytes 368648 | tf_op jit(solution)/shard_map/ppermute | solution.py:431
  34.9 3.5 %collective-permute-start.5 = (f32[3,32,256]{2,1,0:T(8,128)S(1)}, f32[3,32,256]{2,1,0:T(8,128)S(1)}, u32[]{:S(2)}, u32[]{:S(2)}) collective-permute-start(f32[3,32,256]{2,1,0:T(8,128)S(1)} %shard_map.89.own), channel_id=1, source_target_pairs={{0,2},{2,0},{4,6},{6,4},{8,10},{10,8},{12,14},{14,12},{16,18},{18,... | collective-permute-start | bytes 294920 | tf_op jit(solution)/shard_map/ppermute | solution.py:431
  35.0 6.7 %collective-permute-start.7 = (f32[24,256]{1,0:T(8,128)S(1)}, f32[24,256]{1,0:T(8,128)S(1)}, u32[]{:S(2)}, u32[]{:S(2)}) collective-permute-start(f32[24,256]{1,0:T(8,128)S(1)} %get-tuple-element.52), channel_id=1, source_target_pairs={{0,4},{2,6},{4,8},{6,10},{8,12},{10,14},{12,16},{14,18},{16,20},{1... | collective-permute-start | bytes 73736 | tf_op jit(solution)/shard_map/ppermute | solution.py:453
  36.8 5.6 %collective-permute-start.8 = (f32[24,256]{1,0:T(8,128)S(1)}, f32[24,256]{1,0:T(8,128)S(1)}, u32[]{:S(2)}, u32[]{:S(2)}) collective-permute-start(f32[24,256]{1,0:T(8,128)S(1)} %get-tuple-element.53), channel_id=1, source_target_pairs={{0,8},{2,10},{4,12},{6,14},{8,16},{10,18},{12,20},{14,22},{16,24},... | collective-permute-start | bytes 73736 | tf_op jit(solution)/shard_map/ppermute | solution.py:454
  42.4 8.9 %collective-permute-start.9 = (f32[40,256]{1,0:T(8,128)S(1)}, f32[40,256]{1,0:T(8,128)S(1)}, u32[]{:S(2)}, u32[]{:S(2)}) collective-permute-start(f32[40,256]{1,0:T(8,128)S(1)} %get-tuple-element.54.here), channel_id=1, source_target_pairs={{0,1},{1,0},{2,3},{3,2},{4,5},{5,4},{6,7},{7,6},{8,9},{9,8},{10,11... | collective-permute-start | bytes 122888 | tf_op jit(solution)/shard_map/ppermute | solution.py:435
  44.0 6.6 %collective-permute-start.10 = (f32[32,256]{1,0:T(8,128)S(1)}, f32[32,256]{1,0:T(8,128)S(1)}, u32[]{:S(2)}, u32[]{:S(2)}) collective-permute-start(f32[32,256]{1,0:T(8,128)S(1)} %get-tuple-element.55), channel_id=1, source_target_pairs={{0,4},{1,5},{2,7},{3,6},{4,8},{5,9},{6,11},{7,10},{8,12},{9,13},{1... | collective-permute-start | bytes 98312 | tf_op jit(solution)/shard_map/ppermute | solution.py:445
  45.6 5.7 %collective-permute-start.11 = (f32[32,256]{1,0:T(8,128)S(1)}, f32[32,256]{1,0:T(8,128)S(1)}, u32[]{:S(2)}, u32[]{:S(2)}) collective-permute-start(f32[32,256]{1,0:T(8,128)S(1)} %get-tuple-element.56), channel_id=1, source_target_pairs={{0,8},{1,9},{2,11},{3,10},{4,12},{5,13},{6,15},{7,14},{8,16},{9,17... | collective-permute-start | bytes 98312 | tf_op jit(solution)/shard_map/ppermute | solution.py:445
  51.3 1.2 %collective-permute-start.12 = (f32[16,256]{1,0:T(8,128)S(1)}, f32[16,256]{1,0:T(8,128)S(1)}, u32[]{:S(2)}, u32[]{:S(2)}) collective-permute-start(f32[16,256]{1,0:T(8,128)S(1)} %get-tuple-element.58), channel_id=1, source_target_pairs={{0,2},{2,0},{4,6},{6,4},{8,10},{10,8},{12,14},{14,12},{16,18},{18,... | collective-permute-start | bytes 49160 | tf_op jit(solution)/shard_map/ppermute | solution.py:431

commit v4 on v3

--- a/solution.py
+++ b/solution.py
@@ -103,7 +103,6 @@
     near_sum,
     far_weights,
     out_weights,
-    spread_map,
     mask_tile,
     mask_blocks,
     frame,
@@ -151,9 +150,6 @@
         for k in range(LAT // WINDOW):
             rows = slice(t * BLOCK + k * PACKED, t * BLOCK + (k + 1) * PACKED)
             mask_blocks[t, :, k * WINDOW : (k + 1) * WINDOW] = rolled[rows, :WINDOW]
-    part = OUTW // PATCH
-    rows, places = iota(spread_map.shape, 0) % OUTW, iota(spread_map.shape, 1)
-    spread_map[...] = ((rows // part == places // LAT) & (rows % part == places % part)).astype(BF16)
     near_weights[:, 3 * width : 3 * width + OUTW] = w_head[:, near].T
     near_weights[:, 3 * width + OUTW :] = jnp.zeros((half, columns - 3 * width - OUTW), BF16)
     far_weights[TAIL:, 3 * width :] = jnp.zeros((half, columns - 3 * width), BF16)
@@ -235,19 +231,22 @@
     other[...] = passed
 
 
-def finish(mine, got, out):
+def settle(mine, weights, *blended):
     odd = lax.axis_index("blk") % 2 == 1
     packed = mine[STRIDE : STRIDE + PACKED]
     packed = jnp.where(odd, packed[:, LAT // 2 :], packed[:, : LAT // 2])
     plain = [packed[:, k * WINDOW : (k + 1) * WINDOW] for k in range(STRIDE // PACKED)]
-    weights = dot(jnp.concatenate(plain, axis=0).astype(BF16), repeat_map())
-    batch_count = out.shape[0]
-    for b in range(batch_count):
+    weights[...] = dot(jnp.concatenate(plain, axis=0).astype(BF16), repeat_map())
+    for b, out in enumerate(blended):
         at = b * STRIDE + PACKED * (b > 0)
-        total = mine[at : at + STRIDE]
-        if b == batch_count - 1:
-            total = total + got[...]
-        out[b] = total / weights
+        out[...] = mine[at : at + STRIDE] / weights[...]
+
+
+def finish(mine, got, weights, *rest):
+    blended, out = rest[:-1], rest[-1]
+    for b, x in enumerate(blended):
+        out[b] = x[...]
+    out[len(blended)] = (mine[-STRIDE:] + got[...]) / weights[...]
 
 
 def extend(
@@ -296,8 +295,8 @@
         _, guided_out = rest[:2]
         sums_out = rest[2:]
     else:
-        spread_map, mask_tile, guided_in = rest[:3]
-        mask_blocks = rest[3:-2]
+        mask_tile, guided_in = rest[:2]
+        mask_blocks = rest[2:-2]
         blocks, frame = rest[-2:]
     tokens, far_count = arrived.shape
     columns = own_acc.shape[2]
@@ -387,18 +386,26 @@
         guided_out[...] = (1.0 - guidance) * out
         return
     guided = guidance * out + guided_in[...]
-    tiled = dot(jnp.concatenate(split2(guided), axis=1), spread_map[...])
-    lane_row = iota((1, PATCH * LAT), 1) % LAT // (LAT // GRID)
-    spread = tiled[:GRID]
-    for r in range(1, GRID):
-        spread = jnp.where(lane_row == r, tiled[r * GRID : (r + 1) * GRID], spread)
-    spread = spread * mask_tile[...]
+    guided = guided + pltpu.roll(guided, OUTW, 1)
+    part = OUTW // PATCH
+    per_half = LANES // part
+    group = iota((1, LANES), 1) // part
+    spread = [[None] * HALVES for _ in range(PATCH)]
+    for r in range(GRID):
+        token_row = guided[r * GRID : (r + 1) * GRID]
+        turned = [token_row]
+        turned += [pltpu.roll(token_row, part * d, 1) for d in range(1, PATCH)]
+        h, place = divmod(r, per_half)
+        for a in range(PATCH):
+            value = turned[(r - a) % PATCH]
+            before = spread[a][h]
+            spread[a][h] = value if before is None else jnp.where(group == place, value, before)
     shift = window_shift(offsets)
     for h in range(HALVES):
         lanes = slice(h * LANES, (h + 1) * LANES)
         for a in range(PATCH):
             places = slice(a * LAT + h * LANES, a * LAT + (h + 1) * LANES)
-            frame[pl.ds(a, GRID, stride=PATCH), :] = spread[:, places]
+            frame[pl.ds(a, GRID, stride=PATCH), :] = spread[a][h] * mask_tile[:, places]
         rolled = to_frame(frame, shift)
         for t in range(BLOCKS):
             blocks[t, :BLOCK, lanes] = rolled[t * BLOCK : (t + 1) * BLOCK]
@@ -467,12 +474,14 @@
     mine, other = call(
         sum_far, (here, other_side, first, second), [(part, F32), ((STRIDE, LAT), F32)]
     )
+    got = partner(other)
+    settled = call(settle, (mine,), [((STRIDE, LAT), F32)] * batch_count)
     return pl.pallas_call(
         finish,
         out_shape=jax.ShapeDtypeStruct((batch_count, STRIDE, LAT), F32),
         compiler_params=pltpu.CompilerParams(vmem_limit_bytes=1 << 20),
         name="finish",
-    )(mine, partner(other))
+    )(mine, got, *settled)
 
 
 def shards(features, w_query, w_key, w_value, w_out, w_head, offsets, blend_mask):
@@ -503,7 +512,6 @@
         ((8, columns), F32),
         ((TAIL + half, columns), BF16),
         ((width, 2 * OUTW), BF16),
-        ((4 * OUTW, PATCH * LAT), BF16),
         ((GRID, PATCH * LAT), F32),
         ((BLOCKS, PACKED, LAT), F32),
     ]
@@ -525,7 +533,7 @@
         1,
     )
     acc, mean, square, tail, sums, far_weights, out_weights = prepared[:7]
-    spread_map, mask_tile, mask_blocks = prepared[7:]
+    mask_tile, mask_blocks = prepared[7:]
     own = (acc, mean, square)
     work = [pltpu.VMEM((tokens, width), BF16)] * 5
     flops = 2 * tokens * (half * 3 * width + 2 * tokens * width)
@@ -556,7 +564,7 @@
             if s == 0:
                 results.append(((8, columns), F32))
         else:
-            args += (spread_map, mask_tile, token)
+            args += (mask_tile, token)
             rows = BLOCK
             if s < passes:
                 args += (mask_blocks,)

time: 53.5 us -> 53.3 us (level)
    pallas_call x11 -> x12, Pallas kernels: 18.1 us -> 18.1 us  [call(): pl.pallas_call(kernel, out_shape=[pltpu.VMEM(shape, dtype) for shape, dty...]
where the time goes in v4:
time: 53.3 us; the launch traced here: 53.1 us
  waiting for transfers between devices  19.7 us (37%)
  Pallas kernels  18.7 us (35%)
  starting transfers between devices  13.9 us (26%)
  between operations  0.8 us (2%)
    pallas_call x12, Pallas kernels, call(): pl.pallas_call(kernel, out_shape=[pltpu.VMEM(shape, dtype) for shape, dty...  18.1 us
    ppermute x6, waiting for transfers between devices, across(): return lax.ppermute(x, 'mp', [(0, 1), (1, 0)])  9 us
    ppermute x6, starting transfers between devices, across(): return lax.ppermute(x, 'mp', [(0, 1), (1, 0)])  8.76 us
    ppermute x2, waiting for transfers between devices, moved(): return lax.ppermute(x, ('blk', 'mp'), pairs)  5.71 us
    ppermute x1, waiting for transfers between devices, blend_early(): lax.ppermute(first, 'blk', [(i, (i + 2) % count) for i in range(count)])  3.33 us
    ppermute x1, starting transfers between devices, blend_early(): lax.ppermute(first, 'blk', [(i, (i + 2) % count) for i in range(count)])  1.76 us
    ppermute x1, starting transfers between devices, blend_early(): lax.ppermute(second, 'blk', [(i, (i + 4) % count) for i in range(count)])  1.58 us
    ppermute x2, starting transfers between devices, moved(): return lax.ppermute(x, ('blk', 'mp'), pairs)  1.56 us
  transfers between devices with their start and end apart: 13, of which 9 were waited for; matrix products, arithmetic and copies ran while one was open for 0% of the time, Pallas kernels for 32%

profile of v4, /device:TPU:0, one launch (start us, length us, event | category | flops | bytes accessed | tf_op | source)
XLA Modules:
  0.0 53.1 jit_solution(13077604657358205189)
XLA Ops:
  0.0 1.0 %shard_map.84 = bf16[256,640]{1,0:T(8,128)(2,1)S(1)} custom-call(bf16[1,2,2,256,640]{4,3,2,1,0:T(8,128)(2,1)} %features.5), custom_call_target="tpu_custom_call" | custom-call | bytes 1048576 | tf_op jit(solution)/shard_map/pallas_call | solution.py:425
  1.0 3.1 %collective-permute-start.3 = (bf16[256,640]{1,0:T(8,128)(2,1)S(1)}, bf16[256,640]{1,0:T(8,128)(2,1)S(1)}, u32[]{:S(2)}, u32[]{:S(2)}) collective-permute-start(bf16[256,640]{1,0:T(8,128)(2,1)S(1)} %shard_map.84), channel_id=1, source_target_pairs={{0,1},{1,0},{2,3},{3,2},{4,5},{5,4},{6,7},{7,6},{8,9},{9,8},{10,11... | collective-permute-start | bytes 983048 | tf_op jit(solution)/shard_map/ppermute | solution.py:442
  4.1 1.2 %shard_map.82 = (bf16[256,640]{1,0:T(8,128)(2,1)S(1)}, bf16[256,640]{1,0:T(8,128)(2,1)S(1)}, bf16[256,384]{1,0:T(8,128)(2,1)S(1)}, bf16[256,256]{1,0:T(8,128)(2,1)S(1)}) custom-call(bf16[1,2,2,256,640]{4,3,2,1,0:T(8,128)(2,1)} %features.5), custom_call_target="tpu_custom_call" | custom-call | bytes 1048576 | tf_op jit(solution)/shard_map/pallas_call | solution.py:425
  5.3 0.1 collective-permute-start.4
  5.4 2.0 %collective-permute-start.2 = (bf16[256,640]{1,0:T(8,128)(2,1)S(1)}, bf16[256,640]{1,0:T(8,128)(2,1)S(1)}, u32[]{:S(2)}, u32[]{:S(2)}) collective-permute-start(bf16[256,640]{1,0:T(8,128)(2,1)S(1)} %get-tuple-element.40), channel_id=1, source_target_pairs={{0,1},{1,0},{2,3},{3,2},{4,5},{5,4},{6,7},{7,6},{8,9},{9,8},{10,11... | collective-permute-start | bytes 983048 | tf_op jit(solution)/shard_map/ppermute | solution.py:442
  7.4 0.1 collective-permute-start.1
  7.5 1.9 %collective-permute-start = (bf16[256,256]{1,0:T(8,128)(2,1)S(1)}, bf16[256,256]{1,0:T(8,128)(2,1)S(1)}, u32[]{:S(2)}, u32[]{:S(2)}) collective-permute-start(bf16[256,256]{1,0:T(8,128)(2,1)S(1)} %get-tuple-element.33), channel_id=1, source_target_pairs={{0,1},{1,0},{2,3},{3,2},{4,5},{5,4},{6,7},{7,6},{8,9},{9,8},{10,11... | collective-permute-start | bytes 393224 | tf_op jit(solution)/shard_map/ppermute | solution.py:442
  10.1 5.9 %shard_map.83 = (f32[4,256,2048]{2,1,0:T(8,128)S(1)}, f32[4,256,1]{2,1,0:T(8,128)S(1)}, f32[4,256,1]{2,1,0:T(8,128)S(1)}, bf16[4,256,128]{2,1,0:T(8,128)(2,1)S(1...) custom-call(s32[1]{0:T(128)S(6)} %copy.9.offsets, ...), custom_call_target="tpu_custom_call" | custom-call | flops 2516582400 | bytes 1048576 | tf_op jit(solution)/shard_map/pallas_call | solution.py:425
  16.0 0.0 collective-permute-done.3.arrived
  16.0 2.5 %shard_map.85 = (f32[256,128]{1,0:T(8,128)S(1)}, f32[8,2048]{1,0:T(8,128)S(1)}) custom-call(s32[1]{0:T(128)S(6)} %copy.9.offsets, bf16[256,640]{1,0:T(8,128)(2,1)S(1)} %collective-permute-done.3.arrived, f32[4,256,2048]{2,1,0:T(8,128)S(1)} %get-tuple-element.35.own_acc, f32[4,256,1]{2,1,0:T(8,128)S(1)} %get-tuple-element.36.own_mean, ...), custom_call_target="tpu_custom_call" | custom-call | flops 796917760 | bytes 1048576 | tf_op jit(solution)/shard_map/pallas_call | solution.py:425
  18.5 1.2 %collective-permute-done.4.arrived = bf16[256,640]{1,0:T(8,128)(2,1)S(1)} collective-permute-done((bf16[256,640]{1,0:T(8,128)(2,1)S(1)}, bf16[256,640]{1,0:T(8,128)(2,1)S(1)}, u32[]{:S(2)}, u32[]{:S(2)}) %collective-permute-start.4) | collective-permute-done | bytes 327712 | tf_op jit(solution)/shard_map/ppermute | solution.py:442
  19.7 2.3 %shard_map.86.rest_0_.own = f32[3,40,256]{2,1,0:T(8,128)S(1)} custom-call(s32[1]{0:T(128)S(6)} %copy.9.offsets, bf16[256,640]{1,0:T(8,128)(2,1)S(1)} %collective-permute-done.4.arrived, f32[4,256,2048]{2,1,0:T(8,128)S(1)} %get-tuple-element.35.own_acc, f32[4,256,1]{2,1,0:T(8,128)S(1)} %get-tuple-element.36.own_mean, ...), custom_call_target="tpu_custom_call" | custom-call | flops 796917760 | bytes 1048576 | tf_op jit(solution)/shard_map/pallas_call | solution.py:425
  22.0 0.1 collective-permute-start.6
  22.1 4.6 %collective-permute-done.2.arrived = bf16[256,640]{1,0:T(8,128)(2,1)S(1)} collective-permute-done((bf16[256,640]{1,0:T(8,128)(2,1)S(1)}, bf16[256,640]{1,0:T(8,128)(2,1)S(1)}, u32[]{:S(2)}, u32[]{:S(2)}) %collective-permute-start.2) | collective-permute-done | bytes 327712 | tf_op jit(solution)/shard_map/ppermute | solution.py:442
  26.7 2.2 %shard_map.87.token.rest_1_ = f32[256,128]{1,0:T(8,128)S(1)} custom-call(s32[1]{0:T(128)S(6)} %copy.9.offsets, bf16[256,640]{1,0:T(8,128)(2,1)S(1)} %collective-permute-done.2.arrived, f32[4,256,2048]{2,1,0:T(8,128)S(1)} %get-tuple-element.35.own_acc, f32[4,256,1]{2,1,0:T(8,128)S(1)} %get-tuple-element.36.own_mean, ...), custom_call_target="tpu_custom_call" | custom-call | flops 796917760 | bytes 1048576 | tf_op jit(solution)/shard_map/pallas_call | solution.py:425
  28.9 2.1 %collective-permute-done.1.arrived = bf16[256,384]{1,0:T(8,128)(2,1)S(1)} collective-permute-done((bf16[256,384]{1,0:T(8,128)(2,1)S(1)}, bf16[256,384]{1,0:T(8,128)(2,1)S(1)}, u32[]{:S(2)}, u32[]{:S(2)}) %collective-permute-start.1) | collective-permute-done | bytes 196640 | tf_op jit(solution)/shard_map/ppermute | solution.py:442
  30.9 0.8 %shard_map.88 = (f32[1,256,2048]{2,1,0:T(8,128)S(1)}, f32[1,256,1]{2,1,0:T(8,128)S(1)}, f32[1,256,1]{2,1,0:T(8,128)S(1)}) custom-call(bf16[256,384]{1,0:T(8,128)(2,1)S(1)} %collective-permute-done.1.arrived, f32[4,256,2048]{2,1,0:T(8,128)S(1)} %get-tuple-element.35.own_acc, f32[4,256,1]{2,1,0:T(8,128)S(1)} %get-tuple-element.36.own_mean, ...), custom_call_target="tpu_custom_call" | custom-call | flops 377487360 | bytes 1048576 | tf_op jit(solution)/shard_map/pallas_call | solution.py:425
  31.7 1.2 %collective-permute-done.arrived = bf16[256,256]{1,0:T(8,128)(2,1)S(1)} collective-permute-done((bf16[256,256]{1,0:T(8,128)(2,1)S(1)}, bf16[256,256]{1,0:T(8,128)(2,1)S(1)}, u32[]{:S(2)}, u32[]{:S(2)}) %collective-permute-start) | collective-permute-done | bytes 131104 | tf_op jit(solution)/shard_map/ppermute | solution.py:442
  32.9 2.0 %shard_map.89.own = f32[3,32,256]{2,1,0:T(8,128)S(1)} custom-call(s32[1]{0:T(128)S(6)} %copy.9.offsets, bf16[256,256]{1,0:T(8,128)(2,1)S(1)} %collective-permute-done.arrived, f32[1,256,2048]{2,1,0:T(8,128)S(1)} %get-tuple-element.48.own_acc, f32[1,256,1]{2,1,0:T(8,128)S(1)} %get-tuple-element.49.own_mean, f32[1,256,1]{2,1,0:T(8,128)S(1)} %get-tuple-element.50.own_square, ...), custom_call_target="tpu_custom_call" | custom-call | flops 796917760 | bytes 1048576 | tf_op jit(solution)/shard_map/pallas_call | solution.py:425
  34.8 0.1 collective-permute-start.5
  35.0 1.8 %collective-permute-start.7 = (f32[24,256]{1,0:T(8,128)S(1)}, f32[24,256]{1,0:T(8,128)S(1)}, u32[]{:S(2)}, u32[]{:S(2)}) collective-permute-start(f32[24,256]{1,0:T(8,128)S(1)} %get-tuple-element.52), channel_id=1, source_target_pairs={{0,4},{2,6},{4,8},{6,10},{8,12},{10,14},{12,16},{14,18},{16,20},{1... | collective-permute-start | bytes 73736 | tf_op jit(solution)/shard_map/ppermute | solution.py:460
  36.7 1.6 %collective-permute-start.8 = (f32[24,256]{1,0:T(8,128)S(1)}, f32[24,256]{1,0:T(8,128)S(1)}, u32[]{:S(2)}, u32[]{:S(2)}) collective-permute-start(f32[24,256]{1,0:T(8,128)S(1)} %get-tuple-element.53), channel_id=1, source_target_pairs={{0,8},{2,10},{4,12},{6,14},{8,16},{10,18},{12,20},{14,22},{16,24},... | collective-permute-start | bytes 73736 | tf_op jit(solution)/shard_map/ppermute | solution.py:461
  38.3 3.3 %collective-permute-done.7.refs_1_ = f32[24,256]{1,0:T(8,128)S(1)} collective-permute-done((f32[24,256]{1,0:T(8,128)S(1)}, f32[24,256]{1,0:T(8,128)S(1)}, u32[]{:S(2)}, u32[]{:S(2)}) %collective-permute-start.7) | collective-permute-done | bytes 24608 | tf_op jit(solution)/shard_map/ppermute | solution.py:460
  41.6 0.7 %collective-permute-done.8.refs_2_ = f32[24,256]{1,0:T(8,128)S(1)} collective-permute-done((f32[24,256]{1,0:T(8,128)S(1)}, f32[24,256]{1,0:T(8,128)S(1)}, u32[]{:S(2)}, u32[]{:S(2)}) %collective-permute-start.8) | collective-permute-done | bytes 24608 | tf_op jit(solution)/shard_map/ppermute | solution.py:461
  42.4 1.6 %collective-permute-start.9 = (f32[40,256]{1,0:T(8,128)S(1)}, f32[40,256]{1,0:T(8,128)S(1)}, u32[]{:S(2)}, u32[]{:S(2)}) collective-permute-start(f32[40,256]{1,0:T(8,128)S(1)} %get-tuple-element.54.here), channel_id=1, source_target_pairs={{0,1},{1,0},{2,3},{3,2},{4,5},{5,4},{6,7},{7,6},{8,9},{9,8},{10,11... | collective-permute-start | bytes 122888 | tf_op jit(solution)/shard_map/ppermute | solution.py:442
  43.9 1.6 %collective-permute-start.10 = (f32[32,256]{1,0:T(8,128)S(1)}, f32[32,256]{1,0:T(8,128)S(1)}, u32[]{:S(2)}, u32[]{:S(2)}) collective-permute-start(f32[32,256]{1,0:T(8,128)S(1)} %get-tuple-element.55), channel_id=1, source_target_pairs={{0,4},{1,5},{2,7},{3,6},{4,8},{5,9},{6,11},{7,10},{8,12},{9,13},{1... | collective-permute-start | bytes 98312 | tf_op jit(solution)/shard_map/ppermute | solution.py:452
  45.5 5.1 %collective-permute-done.10.first = f32[32,256]{1,0:T(8,128)S(1)} collective-permute-done((f32[32,256]{1,0:T(8,128)S(1)}, f32[32,256]{1,0:T(8,128)S(1)}, u32[]{:S(2)}, u32[]{:S(2)}) %collective-permute-start.10) | collective-permute-done | bytes 32800 | tf_op jit(solution)/shard_map/ppermute | solution.py:452
  50.6 0.7 %collective-permute-done.11.second = f32[32,256]{1,0:T(8,128)S(1)} collective-permute-done((f32[32,256]{1,0:T(8,128)S(1)}, f32[32,256]{1,0:T(8,128)S(1)}, u32[]{:S(2)}, u32[]{:S(2)}) %collective-permute-start.11) | collective-permute-done | bytes 32800 | tf_op jit(solution)/shard_map/ppermute | solution.py:452
  51.2 0.1 collective-permute-start.12
  51.3 0.2 shard_map.93
  51.5 1.0 %collective-permute-done.12.got = f32[16,256]{1,0:T(8,128)S(1)} collective-permute-done((f32[16,256]{1,0:T(8,128)S(1)}, f32[16,256]{1,0:T(8,128)S(1)}, u32[]{:S(2)}, u32[]{:S(2)}) %collective-permute-start.12) | collective-permute-done | bytes 16416 | tf_op jit(solution)/shard_map/ppermute | solution.py:438
  52.5 0.6 %finish.1 = f32[2,16,256]{2,1,0:T(8,128)} custom-call(f32[40,256]{1,0:T(8,128)S(1)} %get-tuple-element.57.mine, f32[16,256]{1,0:T(8,128)S(1)} %collective-permute-done.12.got, f32[16,256]{1,0:T(8,128)S(1)} %get-tuple-element.59.weights, f32[16,256]{1,0:T(8,128)S(1)} %get-tuple-element.60.rest_0_), custom_call_target="tpu_custom_call" | custom-call | tf_op jit(solution)/shard_map/finish/pallas_call | solution.py:479
  (11 shorter events, 0.1 us)
Async XLA Ops:
  0.0 10.1 %copy-start = (bf16[1280,64]{0,1:T(8,128)(2,1)S(1)}, bf16[1280,64]{0,1:T(8,128)(2,1)}, u32[]{:S(2)}) copy-start(bf16[1280,64]{0,1:T(8,128)(2,1)} %param.13) | copy-start | bytes 491524
  0.0 10.1 %copy-start.1 = (s32[1,64,64]{2,1,0:T(8,128)S(1)}, s32[1,64,64]{2,1,0:T(8,128)}, u32[]{:S(2)}) copy-start(s32[1,64,64]{2,1,0:T(8,128)} %mask.1) | copy-start | bytes 49156
  1.0 15.0 %collective-permute-start.3 = (bf16[256,640]{1,0:T(8,128)(2,1)S(1)}, bf16[256,640]{1,0:T(8,128)(2,1)S(1)}, u32[]{:S(2)}, u32[]{:S(2)}) collective-permute-start(bf16[256,640]{1,0:T(8,128)(2,1)S(1)} %shard_map.84), channel_id=1, source_target_pairs={{0,1},{1,0},{2,3},{3,2},{4,5},{5,4},{6,7},{7,6},{8,9},{9,8},{10,11... | collective-permute-start | bytes 983048 | tf_op jit(solution)/shard_map/ppermute | solution.py:442
  5.3 14.4 %collective-permute-start.4 = (bf16[256,640]{1,0:T(8,128)(2,1)S(1)}, bf16[256,640]{1,0:T(8,128)(2,1)S(1)}, u32[]{:S(2)}, u32[]{:S(2)}) collective-permute-start(bf16[256,640]{1,0:T(8,128)(2,1)S(1)} %get-tuple-element.45), channel_id=1, source_target_pairs={{0,1},{1,0},{2,3},{3,2},{4,5},{5,4},{6,7},{7,6},{8,9},{9,8},{10,11... | collective-permute-start | bytes 983048 | tf_op jit(solution)/shard_map/ppermute | solution.py:442
  5.4 21.3 %collective-permute-start.2 = (bf16[256,640]{1,0:T(8,128)(2,1)S(1)}, bf16[256,640]{1,0:T(8,128)(2,1)S(1)}, u32[]{:S(2)}, u32[]{:S(2)}) collective-permute-start(bf16[256,640]{1,0:T(8,128)(2,1)S(1)} %get-tuple-element.40), channel_id=1, source_target_pairs={{0,1},{1,0},{2,3},{3,2},{4,5},{5,4},{6,7},{7,6},{8,9},{9,8},{10,11... | collective-permute-start | bytes 983048 | tf_op jit(solution)/shard_map/ppermute | solution.py:442
  7.4 23.5 %collective-permute-start.1 = (bf16[256,384]{1,0:T(8,128)(2,1)S(1)}, bf16[256,384]{1,0:T(8,128)(2,1)S(1)}, u32[]{:S(2)}, u32[]{:S(2)}) collective-permute-start(bf16[256,384]{1,0:T(8,128)(2,1)S(1)} %get-tuple-element.34), channel_id=1, source_target_pairs={{0,1},{1,0},{2,3},{3,2},{4,5},{5,4},{6,7},{7,6},{8,9},{9,8},{10,11... | collective-permute-start | bytes 589832 | tf_op jit(solution)/shard_map/ppermute | solution.py:442
  7.5 25.4 %collective-permute-start = (bf16[256,256]{1,0:T(8,128)(2,1)S(1)}, bf16[256,256]{1,0:T(8,128)(2,1)S(1)}, u32[]{:S(2)}, u32[]{:S(2)}) collective-permute-start(bf16[256,256]{1,0:T(8,128)(2,1)S(1)} %get-tuple-element.33), channel_id=1, source_target_pairs={{0,1},{1,0},{2,3},{3,2},{4,5},{5,4},{6,7},{7,6},{8,9},{9,8},{10,11... | collective-permute-start | bytes 393224 | tf_op jit(solution)/shard_map/ppermute | solution.py:442
  22.0 12.9 %collective-permute-start.6 = (f32[3,40,256]{2,1,0:T(8,128)S(1)}, f32[3,40,256]{2,1,0:T(8,128)S(1)}, u32[]{:S(2)}, u32[]{:S(2)}) collective-permute-start(f32[3,40,256]{2,1,0:T(8,128)S(1)} %shard_map.86.rest_0_.own), channel_id=1, source_target_pairs={{0,2},{2,0},{4,6},{6,4},{8,10},{10,8},{12,14},{14,12},{16,18},{18,... | collective-permute-start | bytes 368648 | tf_op jit(solution)/shard_map/ppermute | solution.py:438
  34.8 3.5 %collective-permute-start.5 = (f32[3,32,256]{2,1,0:T(8,128)S(1)}, f32[3,32,256]{2,1,0:T(8,128)S(1)}, u32[]{:S(2)}, u32[]{:S(2)}) collective-permute-start(f32[3,32,256]{2,1,0:T(8,128)S(1)} %shard_map.89.own), channel_id=1, source_target_pairs={{0,2},{2,0},{4,6},{6,4},{8,10},{10,8},{12,14},{14,12},{16,18},{18,... | collective-permute-start | bytes 294920 | tf_op jit(solution)/shard_map/ppermute | solution.py:438
  35.0 6.7 %collective-permute-start.7 = (f32[24,256]{1,0:T(8,128)S(1)}, f32[24,256]{1,0:T(8,128)S(1)}, u32[]{:S(2)}, u32[]{:S(2)}) collective-permute-start(f32[24,256]{1,0:T(8,128)S(1)} %get-tuple-element.52), channel_id=1, source_target_pairs={{0,4},{2,6},{4,8},{6,10},{8,12},{10,14},{12,16},{14,18},{16,20},{1... | collective-permute-start | bytes 73736 | tf_op jit(solution)/shard_map/ppermute | solution.py:460
  36.7 5.6 %collective-permute-start.8 = (f32[24,256]{1,0:T(8,128)S(1)}, f32[24,256]{1,0:T(8,128)S(1)}, u32[]{:S(2)}, u32[]{:S(2)}) collective-permute-start(f32[24,256]{1,0:T(8,128)S(1)} %get-tuple-element.53), channel_id=1, source_target_pairs={{0,8},{2,10},{4,12},{6,14},{8,16},{10,18},{12,20},{14,22},{16,24},... | collective-permute-start | bytes 73736 | tf_op jit(solution)/shard_map/ppermute | solution.py:461
  42.4 8.9 %collective-permute-start.9 = (f32[40,256]{1,0:T(8,128)S(1)}, f32[40,256]{1,0:T(8,128)S(1)}, u32[]{:S(2)}, u32[]{:S(2)}) collective-permute-start(f32[40,256]{1,0:T(8,128)S(1)} %get-tuple-element.54.here), channel_id=1, source_target_pairs={{0,1},{1,0},{2,3},{3,2},{4,5},{5,4},{6,7},{7,6},{8,9},{9,8},{10,11... | collective-permute-start | bytes 122888 | tf_op jit(solution)/shard_map/ppermute | solution.py:442
  43.9 6.6 %collective-permute-start.10 = (f32[32,256]{1,0:T(8,128)S(1)}, f32[32,256]{1,0:T(8,128)S(1)}, u32[]{:S(2)}, u32[]{:S(2)}) collective-permute-start(f32[32,256]{1,0:T(8,128)S(1)} %get-tuple-element.55), channel_id=1, source_target_pairs={{0,4},{1,5},{2,7},{3,6},{4,8},{5,9},{6,11},{7,10},{8,12},{9,13},{1... | collective-permute-start | bytes 98312 | tf_op jit(solution)/shard_map/ppermute | solution.py:452
  45.5 5.7 %collective-permute-start.11 = (f32[32,256]{1,0:T(8,128)S(1)}, f32[32,256]{1,0:T(8,128)S(1)}, u32[]{:S(2)}, u32[]{:S(2)}) collective-permute-start(f32[32,256]{1,0:T(8,128)S(1)} %get-tuple-element.56), channel_id=1, source_target_pairs={{0,8},{1,9},{2,11},{3,10},{4,12},{5,13},{6,15},{7,14},{8,16},{9,17... | collective-permute-start | bytes 98312 | tf_op jit(solution)/shard_map/ppermute | solution.py:452
  51.2 1.2 %collective-permute-start.12 = (f32[16,256]{1,0:T(8,128)S(1)}, f32[16,256]{1,0:T(8,128)S(1)}, u32[]{:S(2)}, u32[]{:S(2)}) collective-permute-start(f32[16,256]{1,0:T(8,128)S(1)} %get-tuple-element.58), channel_id=1, source_target_pairs={{0,2},{2,0},{4,6},{6,4},{8,10},{10,8},{12,14},{14,12},{16,18},{18,... | collective-permute-start | bytes 49160 | tf_op jit(solution)/shard_map/ppermute | solution.py:438

commit v5 on v4

--- a/solution.py
+++ b/solution.py
@@ -179,8 +179,8 @@
         load.wait()
 
 
-def cut(windows, features, *refs):
-    outs, sem = refs[:-1], refs[-1]
+def cut(windows, with_moments, features, *refs):
+    outs, sem = refs[: len(windows)], refs[-1]
     passes = features.shape[2]
     loads = [
         pltpu.make_async_copy(
@@ -194,6 +194,11 @@
         load.start()
     for load in loads:
         load.wait()
+    if with_moments:
+        last = windows[-1][0]
+        parts = [out[...].astype(F32) for (s, *_), out in zip(windows, outs) if s == last]
+        both = jnp.concatenate(moments(jnp.concatenate(parts, axis=1)), axis=1)
+        refs[-2][...] = jnp.concatenate([both] + [jnp.zeros_like(both)] * 3, axis=1).T
 
 
 def halves(x):
@@ -249,33 +254,49 @@
     out[len(blended)] = (mine[-STRIDE:] + got[...]) / weights[...]
 
 
+def query_factor():
+    return math.log2(math.e) / HEAD**0.5
+
+
 def extend(
     s,
+    width,
     arrived,
+    far_moments,
     own_acc,
     own_mean,
     own_square,
     own_tail,
+    sums,
     far_weights,
     token,
     acc,
-    mean,
-    square,
+    scales,
 ):
     del token
-    x = arrived[...]
-    near = own_mean[s], own_square[s]
     half = far_weights.shape[0] - TAIL
-    mean[0], square[0] = merged(near, half, x.astype(F32))
-    x = jnp.concatenate([own_tail[s], x], axis=1)
+    moments_far = far_moments[...].T
+    gap = moments_far[:, 0:1] - own_mean[s]
+    mean = own_mean[s] + 0.5 * gap
+    square = own_square[s] + moments_far[:, 1:2] + gap * gap * (0.5 * half)
+    scale = lax.rsqrt(square / (2 * half) + 1e-05)
+    scales[...] = scale
+    offset = mean * scale
+    factor = query_factor()
+    x = jnp.concatenate([own_tail[s], arrived[...]], axis=1)
     for first, last in column_groups(own_acc.shape[2]):
         w = far_weights[: x.shape[1], first:last]
-        acc[0, :, first:last] = own_acc[s, :, first:last] + dot(x, w)
+        total = own_acc[s, :, first:last] + dot(x, w)
+        for at in range(first, last, PAIR):
+            here = total[:, at - first : at - first + PAIR]
+            if at < 3 * width:
+                by = factor if at % TRIPLE == 0 else 1.0
+                here = here * (scale * by) - (offset * by) * sums[0:1, at : at + PAIR]
+            acc[:, at : at + PAIR] = here
 
 
 def attend(
     s,
-    near_count,
     width,
     offsets,
     arrived,
@@ -289,6 +310,7 @@
     *rest,
 ):
     first_pass = s % 2 == 0
+    normalized = len(own_acc.shape) == 2
     q_even, q_odd, keys, values, context = rest[-5:]
     rest = rest[:-5]
     if first_pass:
@@ -298,23 +320,25 @@
         mask_tile, guided_in = rest[:2]
         mask_blocks = rest[2:-2]
         blocks, frame = rest[-2:]
-    tokens, far_count = arrived.shape
-    columns = own_acc.shape[2]
+    tokens, _ = arrived.shape
+    columns = own_acc.shape[-1]
     half = far_weights.shape[0] - TAIL
-    slab = s if own_acc.shape[0] > 1 else 0
     x = arrived[...]
-    near = own_mean[slab], own_square[slab]
-    mean, square = merged(near, near_count, x.astype(F32))
-    scale = lax.rsqrt(square / (near_count + far_count) + 1e-05)
-    offset = mean * scale
-    if near_count == half:
+    if normalized:
+        scale = own_mean[...]
+    else:
+        near = own_mean[s], own_square[s]
+        mean, square = merged(near, half, x.astype(F32))
+        scale = lax.rsqrt(square / (2 * half) + 1e-05)
+        offset = mean * scale
         x = jnp.concatenate([own_tail[s], x], axis=1)
     rows = slice(TAIL + half - x.shape[1], TAIL + half)
     start = s == 0
     if start:
         x = jnp.concatenate([x, jnp.ones((16, x.shape[1]), BF16)], axis=0)
-    factor = math.log2(math.e) / HEAD**0.5
-    query_scale, query_offset = scale * factor, offset * factor
+    factor = query_factor()
+    query_scale = scale * factor
+    query_offset = None if normalized else offset * factor
     first_head = iota((1, PAIR), 1) < HEAD
     none = jnp.zeros((tokens, PAIR), BF16)
     groups = column_groups(columns)
@@ -322,27 +346,34 @@
 
     def project(first, last):
         total = dot(x, far_weights[rows, first:last])
-        sums = sums_in[0:8, first:last]
-        if start:
-            sums = sums + total[tokens : tokens + 8]
-            sums_out[0][:, first:last] = sums
-            total = total[:tokens]
-        total = total + own_acc[slab, :, first:last]
-        sums = sums[0:1]
+        sums = None
+        if normalized:
+            before = own_acc[:, first:last]
+        else:
+            sums = sums_in[0:8, first:last]
+            if start:
+                sums = sums + total[tokens : tokens + 8]
+                sums_out[0][:, first:last] = sums
+                total = total[:tokens]
+            total = total + own_acc[s, :, first:last]
+            sums = sums[0:1]
         for p in range((min(last, 3 * width) - first) // TRIPLE):
             place = slice(first // 3 + p * PAIR, first // 3 + (p + 1) * PAIR)
 
             def part(j, by, less):
                 places = slice(p * TRIPLE + j * PAIR, p * TRIPLE + (j + 1) * PAIR)
+                if normalized:
+                    return before[:, places] + total[:, places] * by
                 return total[:, places] * by - less * sums[:, places]
 
             query = part(0, query_scale, query_offset).astype(BF16)
             q_even[:, place] = jnp.where(first_head, query, none)
             q_odd[:, place] = jnp.where(first_head, none, query)
-            keys[:, place] = part(1, scale, offset).astype(BF16)
-            values[:, place] = part(2, scale, offset).astype(BF16)
+            keys[:, place] = part(1, scale, None if normalized else offset).astype(BF16)
+            values[:, place] = part(2, scale, None if normalized else offset).astype(BF16)
         if last > 3 * width:
-            direct.append(total[:, 3 * width - first :])
+            plain = before if normalized else total
+            direct.append(plain[:, 3 * width - first :])
 
     ones = jnp.ones((tokens, PAIR), BF16)
     ones_even = jnp.where(first_head, ones, none)
@@ -496,13 +527,21 @@
     windows.append((sequences - 1, split, half))
     arrived = []
     for group in (windows[:1], windows[1:]):
+        shapes = [((tokens, stop - start), features.dtype) for _, start, stop in group]
+        with_moments = len(group) > 1
+        if with_moments:
+            shapes.append(((8, tokens), F32))
         parts = call(
-            functools.partial(cut, group),
+            functools.partial(cut, group, with_moments),
             ((features, pltpu.HBM),),
-            [((tokens, stop - start), features.dtype) for _, start, stop in group],
+            shapes,
             [pltpu.SemaphoreType.DMA((len(group),))],
+            0,
+            4 << 20,
         )
-        for part in parts:
+        if with_moments:
+            far_moments = across(parts[-1])
+        for part in parts[: len(group)]:
             arrived.append(across(part))
     outs = [
         ((sequences, tokens, columns), F32),
@@ -541,19 +580,17 @@
     token = mask_blocks
     at = 0
     for s in range(sequences):
-        near, near_count = own, half
+        near = own
         if arrived[at].shape[1] < half:
-            near = tuple(
-                call(
-                    functools.partial(extend, s),
-                    (arrived[at], *own, tail, far_weights, (token, pl.ANY)),
-                    [((1, tokens, columns), F32), ((1, tokens, 1), F32), ((1, tokens, 1), F32)],
-                    (),
-                    2 * tokens * arrived[at].shape[1] * 3 * width,
-                    8 << 20,
-                )
+            normed, scales = call(
+                functools.partial(extend, s, width),
+                (arrived[at], far_moments, *own, tail, sums, far_weights, (token, pl.ANY)),
+                [((tokens, columns), F32), ((tokens, 1), F32)],
+                (),
+                2 * tokens * arrived[at].shape[1] * 3 * width,
+                8 << 20,
             )
-            near_count = half + arrived[at].shape[1]
+            near = (normed, scales, scales)
             at += 1
         args = (offsets, arrived[at], *near, tail, sums, far_weights, out_weights)
         at += 1
@@ -572,13 +609,7 @@
             results = [((BLOCKS, rows, LAT), F32)]
             scratch = frame + work
         token, *more = call(
-            functools.partial(attend, s, near_count, width),
-            args,
-            results,
-            scratch,
-            flops,
-            16 << 20,
-            1,
+            functools.partial(attend, s, width), args, results, scratch, flops, 16 << 20, 1
         )
         if more:
             (sums,) = more

time: 53.3 us -> 53.1 us (level)
    ppermute x6 -> x7, waiting for transfers between devices: 9 us -> 8.64 us  [across(): return lax.ppermute(x, 'mp', [(0, 1), (1, 0)])]
    ppermute x6 -> x7, starting transfers between devices: 8.76 us -> 8.91 us  [across(): return lax.ppermute(x, 'mp', [(0, 1), (1, 0)])]
  transfers between devices with their start and end apart: 13 -> 14, of which waited for: 9 -> 9; matrix products, arithmetic and copies ran while one was open for 0% -> 0% of each run, Pallas kernels for 32% -> 32%
where the time goes in v5:
time: 53.1 us; the launch traced here: 53 us
  waiting for transfers between devices  19.4 us (37%)
  Pallas kernels  18.8 us (35%)
  starting transfers between devices  14 us (26%)
  between operations  0.8 us (2%)
    pallas_call x12, Pallas kernels, call(): pl.pallas_call(kernel, out_shape=[pltpu.VMEM(shape, dtype) for shape, dty...  18.2 us
    ppermute x7, starting transfers between devices, across(): return lax.ppermute(x, 'mp', [(0, 1), (1, 0)])  8.91 us
    ppermute x7, waiting for transfers between devices, across(): return lax.ppermute(x, 'mp', [(0, 1), (1, 0)])  8.64 us
    ppermute x2, waiting for transfers between devices, moved(): return lax.ppermute(x, ('blk', 'mp'), pairs)  5.71 us
    ppermute x1, waiting for transfers between devices, blend_early(): lax.ppermute(first, 'blk', [(i, (i + 2) % count) for i in range(count)])  3.32 us
    ppermute x1, starting transfers between devices, blend_early(): lax.ppermute(first, 'blk', [(i, (i + 2) % count) for i in range(count)])  1.76 us
    ppermute x1, starting transfers between devices, blend_early(): lax.ppermute(second, 'blk', [(i, (i + 4) % count) for i in range(count)])  1.58 us
    ppermute x2, starting transfers between devices, moved(): return lax.ppermute(x, ('blk', 'mp'), pairs)  1.55 us
  transfers between devices with their start and end apart: 14, of which 9 were waited for; matrix products, arithmetic and copies ran while one was open for 0% of the time, Pallas kernels for 32%

profile of v5, /device:TPU:0, one launch (start us, length us, event | category | flops | bytes accessed | tf_op | source)
XLA Modules:
  0.0 53.0 jit_solution(5155657527794404136)
XLA Ops:
  0.0 1.0 %shard_map.84 = bf16[256,640]{1,0:T(8,128)(2,1)S(1)} custom-call(bf16[1,2,2,256,640]{4,3,2,1,0:T(8,128)(2,1)} %features.5), custom_call_target="tpu_custom_call" | custom-call | bytes 1048576 | tf_op jit(solution)/shard_map/pallas_call | solution.py:456
  1.0 3.1 %collective-permute-start.3 = (bf16[256,640]{1,0:T(8,128)(2,1)S(1)}, bf16[256,640]{1,0:T(8,128)(2,1)S(1)}, u32[]{:S(2)}, u32[]{:S(2)}) collective-permute-start(bf16[256,640]{1,0:T(8,128)(2,1)S(1)} %shard_map.84), channel_id=1, source_target_pairs={{0,1},{1,0},{2,3},{3,2},{4,5},{5,4},{6,7},{7,6},{8,9},{9,8},{10,11... | collective-permute-start | bytes 983048 | tf_op jit(solution)/shard_map/ppermute | solution.py:473
  4.1 1.5 %shard_map.82 = (bf16[256,640]{1,0:T(8,128)(2,1)S(1)}, bf16[256,640]{1,0:T(8,128)(2,1)S(1)}, bf16[256,384]{1,0:T(8,128)(2,1)S(1)}, bf16[256,256]{1,0:T(8,128)(2,1)S(1)}, f32[8,256]{1,0:T(8,128)S(1)}) custom-call(bf16[1,2,2,256,640]{4,3,2,1,0:T(8,128)(2,1)} %features.5), custom_call_target="tpu_custom_call" | custom-call | bytes 1048576 | tf_op jit(solution)/shard_map/pallas_call | solution.py:456
  5.6 0.1 collective-permute-start.5
  5.7 2.0 %collective-permute-start.4 = (bf16[256,640]{1,0:T(8,128)(2,1)S(1)}, bf16[256,640]{1,0:T(8,128)(2,1)S(1)}, u32[]{:S(2)}, u32[]{:S(2)}) collective-permute-start(bf16[256,640]{1,0:T(8,128)(2,1)S(1)} %get-tuple-element.45), channel_id=1, source_target_pairs={{0,1},{1,0},{2,3},{3,2},{4,5},{5,4},{6,7},{7,6},{8,9},{9,8},{10,11... | collective-permute-start | bytes 983048 | tf_op jit(solution)/shard_map/ppermute | solution.py:473
  7.7 0.1 collective-permute-start.1
  7.7 1.9 %collective-permute-start.2 = (f32[8,256]{1,0:T(8,128)S(1)}, f32[8,256]{1,0:T(8,128)S(1)}, u32[]{:S(2)}, u32[]{:S(2)}) collective-permute-start(f32[8,256]{1,0:T(8,128)S(1)} %get-tuple-element.35), channel_id=1, source_target_pairs={{0,1},{1,0},{2,3},{3,2},{4,5},{5,4},{6,7},{7,6},{8,9},{9,8},{10,11... | collective-permute-start | bytes 24584 | tf_op jit(solution)/shard_map/ppermute | solution.py:473
  10.4 5.9 %shard_map.83 = (f32[4,256,2048]{2,1,0:T(8,128)S(1)}, f32[4,256,1]{2,1,0:T(8,128)S(1)}, f32[4,256,1]{2,1,0:T(8,128)S(1)}, bf16[4,256,128]{2,1,0:T(8,128)(2,1)S(1...) custom-call(s32[1]{0:T(128)S(6)} %copy.9.offsets, ...), custom_call_target="tpu_custom_call" | custom-call | flops 2516582400 | bytes 1048576 | tf_op jit(solution)/shard_map/pallas_call | solution.py:456
  16.3 0.1 collective-permute-start
  16.5 2.5 %shard_map.85 = (f32[256,128]{1,0:T(8,128)S(1)}, f32[8,2048]{1,0:T(8,128)S(1)}) custom-call(s32[1]{0:T(128)S(6)} %copy.9.offsets, bf16[256,640]{1,0:T(8,128)(2,1)S(1)} %collective-permute-done.3.arrived, f32[4,256,2048]{2,1,0:T(8,128)S(1)} %get-tuple-element.36.own_acc, f32[4,256,1]{2,1,0:T(8,128)S(1)} %get-tuple-element.37.own_mean, ...), custom_call_target="tpu_custom_call" | custom-call | flops 796917760 | bytes 1048576 | tf_op jit(solution)/shard_map/pallas_call | solution.py:456
  18.9 0.7 %collective-permute-done.5.arrived = bf16[256,640]{1,0:T(8,128)(2,1)S(1)} collective-permute-done((bf16[256,640]{1,0:T(8,128)(2,1)S(1)}, bf16[256,640]{1,0:T(8,128)(2,1)S(1)}, u32[]{:S(2)}, u32[]{:S(2)}) %collective-permute-start.5) | collective-permute-done | bytes 327712 | tf_op jit(solution)/shard_map/ppermute | solution.py:473
  19.7 2.3 %shard_map.86.rest_0_.own = f32[3,40,256]{2,1,0:T(8,128)S(1)} custom-call(s32[1]{0:T(128)S(6)} %copy.9.offsets, bf16[256,640]{1,0:T(8,128)(2,1)S(1)} %collective-permute-done.5.arrived, f32[4,256,2048]{2,1,0:T(8,128)S(1)} %get-tuple-element.36.own_acc, f32[4,256,1]{2,1,0:T(8,128)S(1)} %get-tuple-element.37.own_mean, ...), custom_call_target="tpu_custom_call" | custom-call | flops 796917760 | bytes 1048576 | tf_op jit(solution)/shard_map/pallas_call | solution.py:456
  22.0 0.1 collective-permute-start.7
  22.1 4.6 %collective-permute-done.4.arrived = bf16[256,640]{1,0:T(8,128)(2,1)S(1)} collective-permute-done((bf16[256,640]{1,0:T(8,128)(2,1)S(1)}, bf16[256,640]{1,0:T(8,128)(2,1)S(1)}, u32[]{:S(2)}, u32[]{:S(2)}) %collective-permute-start.4) | collective-permute-done | bytes 327712 | tf_op jit(solution)/shard_map/ppermute | solution.py:473
  26.7 2.2 %shard_map.87.token.rest_1_ = f32[256,128]{1,0:T(8,128)S(1)} custom-call(s32[1]{0:T(128)S(6)} %copy.9.offsets, bf16[256,640]{1,0:T(8,128)(2,1)S(1)} %collective-permute-done.4.arrived, f32[4,256,2048]{2,1,0:T(8,128)S(1)} %get-tuple-element.36.own_acc, f32[4,256,1]{2,1,0:T(8,128)S(1)} %get-tuple-element.37.own_mean, ...), custom_call_target="tpu_custom_call" | custom-call | flops 796917760 | bytes 1048576 | tf_op jit(solution)/shard_map/pallas_call | solution.py:456
  28.9 2.2 %collective-permute-done.2.far_moments = f32[8,256]{1,0:T(8,128)S(1)} collective-permute-done((f32[8,256]{1,0:T(8,128)S(1)}, f32[8,256]{1,0:T(8,128)S(1)}, u32[]{:S(2)}, u32[]{:S(2)}) %collective-permute-start.2) | collective-permute-done | bytes 8224 | tf_op jit(solution)/shard_map/ppermute | solution.py:473
  31.1 0.9 %shard_map.88 = (f32[256,2048]{1,0:T(8,128)S(1)}, f32[256,1]{1,0:T(8,128)S(1)}) custom-call(bf16[256,384]{1,0:T(8,128)(2,1)S(1)} %collective-permute-done.1.arrived, f32[8,256]{1,0:T(8,128)S(1)} %collective-permute-done.2.far_moments, f32[4,256,2048]{2,1,0:T(8,128)S(1)} %get-tuple-element.36.own_acc, f32[4,256,1]{2,1,0:T(8,128)S(1)} %get-tuple-element.37.own_mean, ...), custom_call_target="tpu_custom_call" | custom-call | flops 377487360 | bytes 1048576 | tf_op jit(solution)/shard_map/pallas_call | solution.py:456
  32.0 1.1 %collective-permute-done.arrived = bf16[256,256]{1,0:T(8,128)(2,1)S(1)} collective-permute-done((bf16[256,256]{1,0:T(8,128)(2,1)S(1)}, bf16[256,256]{1,0:T(8,128)(2,1)S(1)}, u32[]{:S(2)}, u32[]{:S(2)}) %collective-permute-start) | collective-permute-done | bytes 131104 | tf_op jit(solution)/shard_map/ppermute | solution.py:473
  33.0 1.6 %shard_map.89.own = f32[3,32,256]{2,1,0:T(8,128)S(1)} custom-call(s32[1]{0:T(128)S(6)} %copy.9.offsets, bf16[256,256]{1,0:T(8,128)(2,1)S(1)} %collective-permute-done.arrived, f32[256,2048]{1,0:T(8,128)S(1)} %get-tuple-element.49.own_acc, f32[256,1]{1,0:T(8,128)S(1)} %get-tuple-element.50.own_mean.own_square, ...), custom_call_target="tpu_custom_call" | custom-call | flops 796917760 | bytes 1048576 | tf_op jit(solution)/shard_map/pallas_call | solution.py:456
  34.7 0.1 collective-permute-start.6
  34.8 1.8 %collective-permute-start.8 = (f32[24,256]{1,0:T(8,128)S(1)}, f32[24,256]{1,0:T(8,128)S(1)}, u32[]{:S(2)}, u32[]{:S(2)}) collective-permute-start(f32[24,256]{1,0:T(8,128)S(1)} %get-tuple-element.52), channel_id=1, source_target_pairs={{0,4},{2,6},{4,8},{6,10},{8,12},{10,14},{12,16},{14,18},{16,20},{1... | collective-permute-start | bytes 73736 | tf_op jit(solution)/shard_map/ppermute | solution.py:491
  36.6 1.6 %collective-permute-start.9 = (f32[24,256]{1,0:T(8,128)S(1)}, f32[24,256]{1,0:T(8,128)S(1)}, u32[]{:S(2)}, u32[]{:S(2)}) collective-permute-start(f32[24,256]{1,0:T(8,128)S(1)} %get-tuple-element.53), channel_id=1, source_target_pairs={{0,8},{2,10},{4,12},{6,14},{8,16},{10,18},{12,20},{14,22},{16,24},... | collective-permute-start | bytes 73736 | tf_op jit(solution)/shard_map/ppermute | solution.py:492
  38.1 3.3 %collective-permute-done.8.refs_1_ = f32[24,256]{1,0:T(8,128)S(1)} collective-permute-done((f32[24,256]{1,0:T(8,128)S(1)}, f32[24,256]{1,0:T(8,128)S(1)}, u32[]{:S(2)}, u32[]{:S(2)}) %collective-permute-start.8) | collective-permute-done | bytes 24608 | tf_op jit(solution)/shard_map/ppermute | solution.py:491
  41.5 0.7 %collective-permute-done.9.refs_2_ = f32[24,256]{1,0:T(8,128)S(1)} collective-permute-done((f32[24,256]{1,0:T(8,128)S(1)}, f32[24,256]{1,0:T(8,128)S(1)}, u32[]{:S(2)}, u32[]{:S(2)}) %collective-permute-start.9) | collective-permute-done | bytes 24608 | tf_op jit(solution)/shard_map/ppermute | solution.py:492
  42.2 1.6 %collective-permute-start.10 = (f32[40,256]{1,0:T(8,128)S(1)}, f32[40,256]{1,0:T(8,128)S(1)}, u32[]{:S(2)}, u32[]{:S(2)}) collective-permute-start(f32[40,256]{1,0:T(8,128)S(1)} %get-tuple-element.54.here), channel_id=1, source_target_pairs={{0,1},{1,0},{2,3},{3,2},{4,5},{5,4},{6,7},{7,6},{8,9},{9,8},{10,11... | collective-permute-start | bytes 122888 | tf_op jit(solution)/shard_map/ppermute | solution.py:473
  43.8 1.5 %collective-permute-start.11 = (f32[32,256]{1,0:T(8,128)S(1)}, f32[32,256]{1,0:T(8,128)S(1)}, u32[]{:S(2)}, u32[]{:S(2)}) collective-permute-start(f32[32,256]{1,0:T(8,128)S(1)} %get-tuple-element.55), channel_id=1, source_target_pairs={{0,4},{1,5},{2,7},{3,6},{4,8},{5,9},{6,11},{7,10},{8,12},{9,13},{1... | collective-permute-start | bytes 98312 | tf_op jit(solution)/shard_map/ppermute | solution.py:483
  45.4 5.1 %collective-permute-done.11.first = f32[32,256]{1,0:T(8,128)S(1)} collective-permute-done((f32[32,256]{1,0:T(8,128)S(1)}, f32[32,256]{1,0:T(8,128)S(1)}, u32[]{:S(2)}, u32[]{:S(2)}) %collective-permute-start.11) | collective-permute-done | bytes 32800 | tf_op jit(solution)/shard_map/ppermute | solution.py:483
  50.4 0.6 %collective-permute-done.12.second = f32[32,256]{1,0:T(8,128)S(1)} collective-permute-done((f32[32,256]{1,0:T(8,128)S(1)}, f32[32,256]{1,0:T(8,128)S(1)}, u32[]{:S(2)}, u32[]{:S(2)}) %collective-permute-start.12) | collective-permute-done | bytes 32800 | tf_op jit(solution)/shard_map/ppermute | solution.py:483
  51.1 0.1 collective-permute-start.13
  51.2 0.2 shard_map.93
  51.4 1.0 %collective-permute-done.13.got = f32[16,256]{1,0:T(8,128)S(1)} collective-permute-done((f32[16,256]{1,0:T(8,128)S(1)}, f32[16,256]{1,0:T(8,128)S(1)}, u32[]{:S(2)}, u32[]{:S(2)}) %collective-permute-start.13) | collective-permute-done | bytes 16416 | tf_op jit(solution)/shard_map/ppermute | solution.py:469
  52.3 0.6 %finish.1 = f32[2,16,256]{2,1,0:T(8,128)} custom-call(f32[40,256]{1,0:T(8,128)S(1)} %get-tuple-element.57.mine, f32[16,256]{1,0:T(8,128)S(1)} %collective-permute-done.13.got, f32[16,256]{1,0:T(8,128)S(1)} %get-tuple-element.59.weights, f32[16,256]{1,0:T(8,128)S(1)} %get-tuple-element.60.rest_0_), custom_call_target="tpu_custom_call" | custom-call | tf_op jit(solution)/shard_map/finish/pallas_call | solution.py:510
  (13 shorter events, 0.1 us)
Async XLA Ops:
  0.0 10.3 %copy-start = (bf16[1280,64]{0,1:T(8,128)(2,1)S(1)}, bf16[1280,64]{0,1:T(8,128)(2,1)}, u32[]{:S(2)}) copy-start(bf16[1280,64]{0,1:T(8,128)(2,1)} %param.13) | copy-start | bytes 491524
  0.0 10.4 %copy-start.1 = (s32[1,64,64]{2,1,0:T(8,128)S(1)}, s32[1,64,64]{2,1,0:T(8,128)}, u32[]{:S(2)}) copy-start(s32[1,64,64]{2,1,0:T(8,128)} %mask.1) | copy-start | bytes 49156
  1.0 15.3 %collective-permute-start.3 = (bf16[256,640]{1,0:T(8,128)(2,1)S(1)}, bf16[256,640]{1,0:T(8,128)(2,1)S(1)}, u32[]{:S(2)}, u32[]{:S(2)}) collective-permute-start(bf16[256,640]{1,0:T(8,128)(2,1)S(1)} %shard_map.84), channel_id=1, source_target_pairs={{0,1},{1,0},{2,3},{3,2},{4,5},{5,4},{6,7},{7,6},{8,9},{9,8},{10,11... | collective-permute-start | bytes 983048 | tf_op jit(solution)/shard_map/ppermute | solution.py:473
  5.6 14.1 %collective-permute-start.5 = (bf16[256,640]{1,0:T(8,128)(2,1)S(1)}, bf16[256,640]{1,0:T(8,128)(2,1)S(1)}, u32[]{:S(2)}, u32[]{:S(2)}) collective-permute-start(bf16[256,640]{1,0:T(8,128)(2,1)S(1)} %get-tuple-element.46), channel_id=1, source_target_pairs={{0,1},{1,0},{2,3},{3,2},{4,5},{5,4},{6,7},{7,6},{8,9},{9,8},{10,11... | collective-permute-start | bytes 983048 | tf_op jit(solution)/shard_map/ppermute | solution.py:473
  5.7 21.0 %collective-permute-start.4 = (bf16[256,640]{1,0:T(8,128)(2,1)S(1)}, bf16[256,640]{1,0:T(8,128)(2,1)S(1)}, u32[]{:S(2)}, u32[]{:S(2)}) collective-permute-start(bf16[256,640]{1,0:T(8,128)(2,1)S(1)} %get-tuple-element.45), channel_id=1, source_target_pairs={{0,1},{1,0},{2,3},{3,2},{4,5},{5,4},{6,7},{7,6},{8,9},{9,8},{10,11... | collective-permute-start | bytes 983048 | tf_op jit(solution)/shard_map/ppermute | solution.py:473
  7.7 23.4 %collective-permute-start.1 = (bf16[256,384]{1,0:T(8,128)(2,1)S(1)}, bf16[256,384]{1,0:T(8,128)(2,1)S(1)}, u32[]{:S(2)}, u32[]{:S(2)}) collective-permute-start(bf16[256,384]{1,0:T(8,128)(2,1)S(1)} %get-tuple-element.34), channel_id=1, source_target_pairs={{0,1},{1,0},{2,3},{3,2},{4,5},{5,4},{6,7},{7,6},{8,9},{9,8},{10,11... | collective-permute-start | bytes 589832 | tf_op jit(solution)/shard_map/ppermute | solution.py:473
  7.7 23.3 %collective-permute-start.2 = (f32[8,256]{1,0:T(8,128)S(1)}, f32[8,256]{1,0:T(8,128)S(1)}, u32[]{:S(2)}, u32[]{:S(2)}) collective-permute-start(f32[8,256]{1,0:T(8,128)S(1)} %get-tuple-element.35), channel_id=1, source_target_pairs={{0,1},{1,0},{2,3},{3,2},{4,5},{5,4},{6,7},{7,6},{8,9},{9,8},{10,11... | collective-permute-start | bytes 24584 | tf_op jit(solution)/shard_map/ppermute | solution.py:473
  16.3 16.7 %collective-permute-start = (bf16[256,256]{1,0:T(8,128)(2,1)S(1)}, bf16[256,256]{1,0:T(8,128)(2,1)S(1)}, u32[]{:S(2)}, u32[]{:S(2)}) collective-permute-start(bf16[256,256]{1,0:T(8,128)(2,1)S(1)} %get-tuple-element.33), channel_id=1, source_target_pairs={{0,1},{1,0},{2,3},{3,2},{4,5},{5,4},{6,7},{7,6},{8,9},{9,8},{10,11... | collective-permute-start | bytes 393224 | tf_op jit(solution)/shard_map/ppermute | solution.py:473
  22.0 12.7 %collective-permute-start.7 = (f32[3,40,256]{2,1,0:T(8,128)S(1)}, f32[3,40,256]{2,1,0:T(8,128)S(1)}, u32[]{:S(2)}, u32[]{:S(2)}) collective-permute-start(f32[3,40,256]{2,1,0:T(8,128)S(1)} %shard_map.86.rest_0_.own), channel_id=1, source_target_pairs={{0,2},{2,0},{4,6},{6,4},{8,10},{10,8},{12,14},{14,12},{16,18},{18,... | collective-permute-start | bytes 368648 | tf_op jit(solution)/shard_map/ppermute | solution.py:469
  34.7 3.5 %collective-permute-start.6 = (f32[3,32,256]{2,1,0:T(8,128)S(1)}, f32[3,32,256]{2,1,0:T(8,128)S(1)}, u32[]{:S(2)}, u32[]{:S(2)}) collective-permute-start(f32[3,32,256]{2,1,0:T(8,128)S(1)} %shard_map.89.own), channel_id=1, source_target_pairs={{0,2},{2,0},{4,6},{6,4},{8,10},{10,8},{12,14},{14,12},{16,18},{18,... | collective-permute-start | bytes 294920 | tf_op jit(solution)/shard_map/ppermute | solution.py:469
  34.8 6.7 %collective-permute-start.8 = (f32[24,256]{1,0:T(8,128)S(1)}, f32[24,256]{1,0:T(8,128)S(1)}, u32[]{:S(2)}, u32[]{:S(2)}) collective-permute-start(f32[24,256]{1,0:T(8,128)S(1)} %get-tuple-element.52), channel_id=1, source_target_pairs={{0,4},{2,6},{4,8},{6,10},{8,12},{10,14},{12,16},{14,18},{16,20},{1... | collective-permute-start | bytes 73736 | tf_op jit(solution)/shard_map/ppermute | solution.py:491
  36.6 5.6 %collective-permute-start.9 = (f32[24,256]{1,0:T(8,128)S(1)}, f32[24,256]{1,0:T(8,128)S(1)}, u32[]{:S(2)}, u32[]{:S(2)}) collective-permute-start(f32[24,256]{1,0:T(8,128)S(1)} %get-tuple-element.53), channel_id=1, source_target_pairs={{0,8},{2,10},{4,12},{6,14},{8,16},{10,18},{12,20},{14,22},{16,24},... | collective-permute-start | bytes 73736 | tf_op jit(solution)/shard_map/ppermute | solution.py:492
  42.2 8.9 %collective-permute-start.10 = (f32[40,256]{1,0:T(8,128)S(1)}, f32[40,256]{1,0:T(8,128)S(1)}, u32[]{:S(2)}, u32[]{:S(2)}) collective-permute-start(f32[40,256]{1,0:T(8,128)S(1)} %get-tuple-element.54.here), channel_id=1, source_target_pairs={{0,1},{1,0},{2,3},{3,2},{4,5},{5,4},{6,7},{7,6},{8,9},{9,8},{10,11... | collective-permute-start | bytes 122888 | tf_op jit(solution)/shard_map/ppermute | solution.py:473
  43.8 6.6 %collective-permute-start.11 = (f32[32,256]{1,0:T(8,128)S(1)}, f32[32,256]{1,0:T(8,128)S(1)}, u32[]{:S(2)}, u32[]{:S(2)}) collective-permute-start(f32[32,256]{1,0:T(8,128)S(1)} %get-tuple-element.55), channel_id=1, source_target_pairs={{0,4},{1,5},{2,7},{3,6},{4,8},{5,9},{6,11},{7,10},{8,12},{9,13},{1... | collective-permute-start | bytes 98312 | tf_op jit(solution)/shard_map/ppermute | solution.py:483
  45.3 5.7 %collective-permute-start.12 = (f32[32,256]{1,0:T(8,128)S(1)}, f32[32,256]{1,0:T(8,128)S(1)}, u32[]{:S(2)}, u32[]{:S(2)}) collective-permute-start(f32[32,256]{1,0:T(8,128)S(1)} %get-tuple-element.56), channel_id=1, source_target_pairs={{0,8},{1,9},{2,11},{3,10},{4,12},{5,13},{6,15},{7,14},{8,16},{9,17... | collective-permute-start | bytes 98312 | tf_op jit(solution)/shard_map/ppermute | solution.py:483
  51.1 1.2 %collective-permute-start.13 = (f32[16,256]{1,0:T(8,128)S(1)}, f32[16,256]{1,0:T(8,128)S(1)}, u32[]{:S(2)}, u32[]{:S(2)}) collective-permute-start(f32[16,256]{1,0:T(8,128)S(1)} %get-tuple-element.58), channel_id=1, source_target_pairs={{0,2},{2,0},{4,6},{6,4},{8,10},{10,8},{12,14},{14,12},{16,18},{18,... | collective-permute-start | bytes 49160 | tf_op jit(solution)/shard_map/ppermute | solution.py:469

commit v6 on v5

--- a/solution.py
+++ b/solution.py
@@ -219,7 +219,7 @@
 def sum_chip(own, got, *refs):
     here, next_chip, second_chip = refs[-3:]
     next_chip[...] = own[1] + got[1]
-    second_chip[...] = own[2] + got[2]
+    second_chip[...] = (own[2] + got[2]).astype(BF16)
     at = 0
     for i in range(0, len(refs) - 3, 3):
         a, b, c = refs[i : i + 3]
@@ -229,7 +229,7 @@
 
 
 def sum_far(here, across, first, second, mine, other):
-    kept, passed = halves(first[...] + second[...])
+    kept, passed = halves(first[...] + second[...].astype(F32))
     before = here.shape[0] - kept.shape[0]
     mine[:before] = here[:before] + across[:before]
     mine[before:] = here[before:] + across[before:] + kept
@@ -497,7 +497,7 @@
     whole, part = blocks.shape[1:], (batch_count * STRIDE + PACKED, LAT)
     got = partner(blocks)
     here, first, second = call(
-        sum_chip, (blocks, got, *early), [(part, F32), (whole, F32), (whole, F32)]
+        sum_chip, (blocks, got, *early), [(part, F32), (whole, F32), (whole, BF16)]
     )
     first = moved(first, 1)
     second = moved(second, 2)

time: 53.1 us -> 53 us (level)
  transfers between devices with their start and end apart: 14 -> 14, of which waited for: 9 -> 8; matrix products, arithmetic and copies ran while one was open for 0% -> 0% of each run, Pallas kernels for 32% -> 32%
where the time goes in v6:
time: 53 us; the launch traced here: 52.8 us
  waiting for transfers between devices  19.2 us (36%)
  Pallas kernels  18.8 us (35%)
  starting transfers between devices  14 us (26%)
  between operations  0.8 us (2%)
    pallas_call x12, Pallas kernels, call(): pl.pallas_call(kernel, out_shape=[pltpu.VMEM(shape, dtype) for shape, dty...  18.2 us
    ppermute x7, starting transfers between devices, across(): return lax.ppermute(x, 'mp', [(0, 1), (1, 0)])  8.91 us
    ppermute x7, waiting for transfers between devices, across(): return lax.ppermute(x, 'mp', [(0, 1), (1, 0)])  8.64 us
    ppermute x2, waiting for transfers between devices, moved(): return lax.ppermute(x, ('blk', 'mp'), pairs)  5.54 us
    ppermute x1, waiting for transfers between devices, blend_early(): lax.ppermute(first, 'blk', [(i, (i + 2) % count) for i in range(count)])  3.32 us
    ppermute x1, starting transfers between devices, blend_early(): lax.ppermute(first, 'blk', [(i, (i + 2) % count) for i in range(count)])  1.76 us
    ppermute x1, starting transfers between devices, blend_early(): lax.ppermute(second, 'blk', [(i, (i + 4) % count) for i in range(count)])  1.58 us
    ppermute x2, starting transfers between devices, moved(): return lax.ppermute(x, ('blk', 'mp'), pairs)  1.55 us
  transfers between devices with their start and end apart: 14, of which 8 were waited for; matrix products, arithmetic and copies ran while one was open for 0% of the time, Pallas kernels for 32%

profile of v6, /device:TPU:0, one launch (start us, length us, event | category | flops | bytes accessed | tf_op | source)
XLA Modules:
  0.0 52.8 jit_solution(2441668593242282210)
XLA Ops:
  0.0 1.0 %shard_map.84 = bf16[256,640]{1,0:T(8,128)(2,1)S(1)} custom-call(bf16[1,2,2,256,640]{4,3,2,1,0:T(8,128)(2,1)} %features.5), custom_call_target="tpu_custom_call" | custom-call | bytes 1048576 | tf_op jit(solution)/shard_map/pallas_call | solution.py:456
  1.0 3.1 %collective-permute-start.3 = (bf16[256,640]{1,0:T(8,128)(2,1)S(1)}, bf16[256,640]{1,0:T(8,128)(2,1)S(1)}, u32[]{:S(2)}, u32[]{:S(2)}) collective-permute-start(bf16[256,640]{1,0:T(8,128)(2,1)S(1)} %shard_map.84), channel_id=1, source_target_pairs={{0,1},{1,0},{2,3},{3,2},{4,5},{5,4},{6,7},{7,6},{8,9},{9,8},{10,11... | collective-permute-start | bytes 983048 | tf_op jit(solution)/shard_map/ppermute | solution.py:473
  4.1 1.5 %shard_map.82 = (bf16[256,640]{1,0:T(8,128)(2,1)S(1)}, bf16[256,640]{1,0:T(8,128)(2,1)S(1)}, bf16[256,384]{1,0:T(8,128)(2,1)S(1)}, bf16[256,256]{1,0:T(8,128)(2,1)S(1)}, f32[8,256]{1,0:T(8,128)S(1)}) custom-call(bf16[1,2,2,256,640]{4,3,2,1,0:T(8,128)(2,1)} %features.5), custom_call_target="tpu_custom_call" | custom-call | bytes 1048576 | tf_op jit(solution)/shard_map/pallas_call | solution.py:456
  5.6 0.1 collective-permute-start.5
  5.7 2.0 %collective-permute-start.4 = (bf16[256,640]{1,0:T(8,128)(2,1)S(1)}, bf16[256,640]{1,0:T(8,128)(2,1)S(1)}, u32[]{:S(2)}, u32[]{:S(2)}) collective-permute-start(bf16[256,640]{1,0:T(8,128)(2,1)S(1)} %get-tuple-element.45), channel_id=1, source_target_pairs={{0,1},{1,0},{2,3},{3,2},{4,5},{5,4},{6,7},{7,6},{8,9},{9,8},{10,11... | collective-permute-start | bytes 983048 | tf_op jit(solution)/shard_map/ppermute | solution.py:473
  7.7 0.1 collective-permute-start.1
  7.7 1.9 %collective-permute-start.2 = (f32[8,256]{1,0:T(8,128)S(1)}, f32[8,256]{1,0:T(8,128)S(1)}, u32[]{:S(2)}, u32[]{:S(2)}) collective-permute-start(f32[8,256]{1,0:T(8,128)S(1)} %get-tuple-element.35), channel_id=1, source_target_pairs={{0,1},{1,0},{2,3},{3,2},{4,5},{5,4},{6,7},{7,6},{8,9},{9,8},{10,11... | collective-permute-start | bytes 24584 | tf_op jit(solution)/shard_map/ppermute | solution.py:473
  10.4 5.9 %shard_map.83 = (f32[4,256,2048]{2,1,0:T(8,128)S(1)}, f32[4,256,1]{2,1,0:T(8,128)S(1)}, f32[4,256,1]{2,1,0:T(8,128)S(1)}, bf16[4,256,128]{2,1,0:T(8,128)(2,1)S(1...) custom-call(s32[1]{0:T(128)S(6)} %copy.9.offsets, ...), custom_call_target="tpu_custom_call" | custom-call | flops 2516582400 | bytes 1048576 | tf_op jit(solution)/shard_map/pallas_call | solution.py:456
  16.3 0.1 collective-permute-start
  16.5 2.5 %shard_map.85 = (f32[256,128]{1,0:T(8,128)S(1)}, f32[8,2048]{1,0:T(8,128)S(1)}) custom-call(s32[1]{0:T(128)S(6)} %copy.9.offsets, bf16[256,640]{1,0:T(8,128)(2,1)S(1)} %collective-permute-done.3.arrived, f32[4,256,2048]{2,1,0:T(8,128)S(1)} %get-tuple-element.36.own_acc, f32[4,256,1]{2,1,0:T(8,128)S(1)} %get-tuple-element.37.own_mean, ...), custom_call_target="tpu_custom_call" | custom-call | flops 796917760 | bytes 1048576 | tf_op jit(solution)/shard_map/pallas_call | solution.py:456
  18.9 0.7 %collective-permute-done.5.arrived = bf16[256,640]{1,0:T(8,128)(2,1)S(1)} collective-permute-done((bf16[256,640]{1,0:T(8,128)(2,1)S(1)}, bf16[256,640]{1,0:T(8,128)(2,1)S(1)}, u32[]{:S(2)}, u32[]{:S(2)}) %collective-permute-start.5) | collective-permute-done | bytes 327712 | tf_op jit(solution)/shard_map/ppermute | solution.py:473
  19.7 2.3 %shard_map.86.rest_0_.own = f32[3,40,256]{2,1,0:T(8,128)S(1)} custom-call(s32[1]{0:T(128)S(6)} %copy.9.offsets, bf16[256,640]{1,0:T(8,128)(2,1)S(1)} %collective-permute-done.5.arrived, f32[4,256,2048]{2,1,0:T(8,128)S(1)} %get-tuple-element.36.own_acc, f32[4,256,1]{2,1,0:T(8,128)S(1)} %get-tuple-element.37.own_mean, ...), custom_call_target="tpu_custom_call" | custom-call | flops 796917760 | bytes 1048576 | tf_op jit(solution)/shard_map/pallas_call | solution.py:456
  22.0 0.1 collective-permute-start.7
  22.1 4.6 %collective-permute-done.4.arrived = bf16[256,640]{1,0:T(8,128)(2,1)S(1)} collective-permute-done((bf16[256,640]{1,0:T(8,128)(2,1)S(1)}, bf16[256,640]{1,0:T(8,128)(2,1)S(1)}, u32[]{:S(2)}, u32[]{:S(2)}) %collective-permute-start.4) | collective-permute-done | bytes 327712 | tf_op jit(solution)/shard_map/ppermute | solution.py:473
  26.7 2.2 %shard_map.87.token.rest_1_ = f32[256,128]{1,0:T(8,128)S(1)} custom-call(s32[1]{0:T(128)S(6)} %copy.9.offsets, bf16[256,640]{1,0:T(8,128)(2,1)S(1)} %collective-permute-done.4.arrived, f32[4,256,2048]{2,1,0:T(8,128)S(1)} %get-tuple-element.36.own_acc, f32[4,256,1]{2,1,0:T(8,128)S(1)} %get-tuple-element.37.own_mean, ...), custom_call_target="tpu_custom_call" | custom-call | flops 796917760 | bytes 1048576 | tf_op jit(solution)/shard_map/pallas_call | solution.py:456
  28.9 2.2 %collective-permute-done.2.far_moments = f32[8,256]{1,0:T(8,128)S(1)} collective-permute-done((f32[8,256]{1,0:T(8,128)S(1)}, f32[8,256]{1,0:T(8,128)S(1)}, u32[]{:S(2)}, u32[]{:S(2)}) %collective-permute-start.2) | collective-permute-done | bytes 8224 | tf_op jit(solution)/shard_map/ppermute | solution.py:473
  31.1 0.0 collective-permute-done.1.arrived
  31.1 0.9 %shard_map.88 = (f32[256,2048]{1,0:T(8,128)S(1)}, f32[256,1]{1,0:T(8,128)S(1)}) custom-call(bf16[256,384]{1,0:T(8,128)(2,1)S(1)} %collective-permute-done.1.arrived, f32[8,256]{1,0:T(8,128)S(1)} %collective-permute-done.2.far_moments, f32[4,256,2048]{2,1,0:T(8,128)S(1)} %get-tuple-element.36.own_acc, f32[4,256,1]{2,1,0:T(8,128)S(1)} %get-tuple-element.37.own_mean, ...), custom_call_target="tpu_custom_call" | custom-call | flops 377487360 | bytes 1048576 | tf_op jit(solution)/shard_map/pallas_call | solution.py:456
  32.0 1.1 %collective-permute-done.arrived = bf16[256,256]{1,0:T(8,128)(2,1)S(1)} collective-permute-done((bf16[256,256]{1,0:T(8,128)(2,1)S(1)}, bf16[256,256]{1,0:T(8,128)(2,1)S(1)}, u32[]{:S(2)}, u32[]{:S(2)}) %collective-permute-start) | collective-permute-done | bytes 131104 | tf_op jit(solution)/shard_map/ppermute | solution.py:473
  33.0 1.6 %shard_map.89.own = f32[3,32,256]{2,1,0:T(8,128)S(1)} custom-call(s32[1]{0:T(128)S(6)} %copy.9.offsets, bf16[256,256]{1,0:T(8,128)(2,1)S(1)} %collective-permute-done.arrived, f32[256,2048]{1,0:T(8,128)S(1)} %get-tuple-element.49.own_acc, f32[256,1]{1,0:T(8,128)S(1)} %get-tuple-element.50.own_mean.own_square, ...), custom_call_target="tpu_custom_call" | custom-call | flops 796917760 | bytes 1048576 | tf_op jit(solution)/shard_map/pallas_call | solution.py:456
  34.7 0.1 collective-permute-start.6
  34.8 1.8 %collective-permute-start.8 = (f32[24,256]{1,0:T(8,128)S(1)}, f32[24,256]{1,0:T(8,128)S(1)}, u32[]{:S(2)}, u32[]{:S(2)}) collective-permute-start(f32[24,256]{1,0:T(8,128)S(1)} %get-tuple-element.52), channel_id=1, source_target_pairs={{0,4},{2,6},{4,8},{6,10},{8,12},{10,14},{12,16},{14,18},{16,20},{1... | collective-permute-start | bytes 73736 | tf_op jit(solution)/shard_map/ppermute | solution.py:491
  36.6 1.6 %collective-permute-start.9 = (f32[24,256]{1,0:T(8,128)S(1)}, f32[24,256]{1,0:T(8,128)S(1)}, u32[]{:S(2)}, u32[]{:S(2)}) collective-permute-start(f32[24,256]{1,0:T(8,128)S(1)} %get-tuple-element.53), channel_id=1, source_target_pairs={{0,8},{2,10},{4,12},{6,14},{8,16},{10,18},{12,20},{14,22},{16,24},... | collective-permute-start | bytes 73736 | tf_op jit(solution)/shard_map/ppermute | solution.py:492
  38.1 3.3 %collective-permute-done.8.refs_1_ = f32[24,256]{1,0:T(8,128)S(1)} collective-permute-done((f32[24,256]{1,0:T(8,128)S(1)}, f32[24,256]{1,0:T(8,128)S(1)}, u32[]{:S(2)}, u32[]{:S(2)}) %collective-permute-start.8) | collective-permute-done | bytes 24608 | tf_op jit(solution)/shard_map/ppermute | solution.py:491
  41.5 0.7 %collective-permute-done.9.refs_2_ = f32[24,256]{1,0:T(8,128)S(1)} collective-permute-done((f32[24,256]{1,0:T(8,128)S(1)}, f32[24,256]{1,0:T(8,128)S(1)}, u32[]{:S(2)}, u32[]{:S(2)}) %collective-permute-start.9) | collective-permute-done | bytes 24608 | tf_op jit(solution)/shard_map/ppermute | solution.py:492
  42.2 1.6 %collective-permute-start.10 = (f32[40,256]{1,0:T(8,128)S(1)}, f32[40,256]{1,0:T(8,128)S(1)}, u32[]{:S(2)}, u32[]{:S(2)}) collective-permute-start(f32[40,256]{1,0:T(8,128)S(1)} %get-tuple-element.54.here), channel_id=1, source_target_pairs={{0,1},{1,0},{2,3},{3,2},{4,5},{5,4},{6,7},{7,6},{8,9},{9,8},{10,11... | collective-permute-start | bytes 122888 | tf_op jit(solution)/shard_map/ppermute | solution.py:473
  43.8 1.5 %collective-permute-start.11 = (f32[32,256]{1,0:T(8,128)S(1)}, f32[32,256]{1,0:T(8,128)S(1)}, u32[]{:S(2)}, u32[]{:S(2)}) collective-permute-start(f32[32,256]{1,0:T(8,128)S(1)} %get-tuple-element.55), channel_id=1, source_target_pairs={{0,4},{1,5},{2,7},{3,6},{4,8},{5,9},{6,11},{7,10},{8,12},{9,13},{1... | collective-permute-start | bytes 98312 | tf_op jit(solution)/shard_map/ppermute | solution.py:483
  45.4 5.5 %collective-permute-done.12.second = bf16[32,256]{1,0:T(8,128)(2,1)S(1)} collective-permute-done((bf16[32,256]{1,0:T(8,128)(2,1)S(1)}, bf16[32,256]{1,0:T(8,128)(2,1)S(1)}, u32[]{:S(2)}, u32[]{:S(2)}) %collective-permute-start.12) | collective-permute-done | bytes 16416 | tf_op jit(solution)/shard_map/ppermute | solution.py:483
  50.9 0.1 collective-permute-start.13
  51.0 0.2 shard_map.93
  51.2 1.0 %collective-permute-done.13.got = f32[16,256]{1,0:T(8,128)S(1)} collective-permute-done((f32[16,256]{1,0:T(8,128)S(1)}, f32[16,256]{1,0:T(8,128)S(1)}, u32[]{:S(2)}, u32[]{:S(2)}) %collective-permute-start.13) | collective-permute-done | bytes 16416 | tf_op jit(solution)/shard_map/ppermute | solution.py:469
  52.2 0.6 %finish.1 = f32[2,16,256]{2,1,0:T(8,128)} custom-call(f32[40,256]{1,0:T(8,128)S(1)} %get-tuple-element.57.mine, f32[16,256]{1,0:T(8,128)S(1)} %collective-permute-done.13.got, f32[16,256]{1,0:T(8,128)S(1)} %get-tuple-element.59.weights, f32[16,256]{1,0:T(8,128)S(1)} %get-tuple-element.60.rest_0_), custom_call_target="tpu_custom_call" | custom-call | tf_op jit(solution)/shard_map/finish/pallas_call | solution.py:510
  (13 shorter events, 0.1 us)
Async XLA Ops:
  0.0 10.3 %copy-start = (bf16[1280,64]{0,1:T(8,128)(2,1)S(1)}, bf16[1280,64]{0,1:T(8,128)(2,1)}, u32[]{:S(2)}) copy-start(bf16[1280,64]{0,1:T(8,128)(2,1)} %param.13) | copy-start | bytes 491524
  0.0 10.4 %copy-start.1 = (s32[1,64,64]{2,1,0:T(8,128)S(1)}, s32[1,64,64]{2,1,0:T(8,128)}, u32[]{:S(2)}) copy-start(s32[1,64,64]{2,1,0:T(8,128)} %mask.1) | copy-start | bytes 49156
  1.0 15.3 %collective-permute-start.3 = (bf16[256,640]{1,0:T(8,128)(2,1)S(1)}, bf16[256,640]{1,0:T(8,128)(2,1)S(1)}, u32[]{:S(2)}, u32[]{:S(2)}) collective-permute-start(bf16[256,640]{1,0:T(8,128)(2,1)S(1)} %shard_map.84), channel_id=1, source_target_pairs={{0,1},{1,0},{2,3},{3,2},{4,5},{5,4},{6,7},{7,6},{8,9},{9,8},{10,11... | collective-permute-start | bytes 983048 | tf_op jit(solution)/shard_map/ppermute | solution.py:473
  5.6 14.1 %collective-permute-start.5 = (bf16[256,640]{1,0:T(8,128)(2,1)S(1)}, bf16[256,640]{1,0:T(8,128)(2,1)S(1)}, u32[]{:S(2)}, u32[]{:S(2)}) collective-permute-start(bf16[256,640]{1,0:T(8,128)(2,1)S(1)} %get-tuple-element.46), channel_id=1, source_target_pairs={{0,1},{1,0},{2,3},{3,2},{4,5},{5,4},{6,7},{7,6},{8,9},{9,8},{10,11... | collective-permute-start | bytes 983048 | tf_op jit(solution)/shard_map/ppermute | solution.py:473
  5.7 21.0 %collective-permute-start.4 = (bf16[256,640]{1,0:T(8,128)(2,1)S(1)}, bf16[256,640]{1,0:T(8,128)(2,1)S(1)}, u32[]{:S(2)}, u32[]{:S(2)}) collective-permute-start(bf16[256,640]{1,0:T(8,128)(2,1)S(1)} %get-tuple-element.45), channel_id=1, source_target_pairs={{0,1},{1,0},{2,3},{3,2},{4,5},{5,4},{6,7},{7,6},{8,9},{9,8},{10,11... | collective-permute-start | bytes 983048 | tf_op jit(solution)/shard_map/ppermute | solution.py:473
  7.7 23.4 %collective-permute-start.1 = (bf16[256,384]{1,0:T(8,128)(2,1)S(1)}, bf16[256,384]{1,0:T(8,128)(2,1)S(1)}, u32[]{:S(2)}, u32[]{:S(2)}) collective-permute-start(bf16[256,384]{1,0:T(8,128)(2,1)S(1)} %get-tuple-element.34), channel_id=1, source_target_pairs={{0,1},{1,0},{2,3},{3,2},{4,5},{5,4},{6,7},{7,6},{8,9},{9,8},{10,11... | collective-permute-start | bytes 589832 | tf_op jit(solution)/shard_map/ppermute | solution.py:473
  7.7 23.3 %collective-permute-start.2 = (f32[8,256]{1,0:T(8,128)S(1)}, f32[8,256]{1,0:T(8,128)S(1)}, u32[]{:S(2)}, u32[]{:S(2)}) collective-permute-start(f32[8,256]{1,0:T(8,128)S(1)} %get-tuple-element.35), channel_id=1, source_target_pairs={{0,1},{1,0},{2,3},{3,2},{4,5},{5,4},{6,7},{7,6},{8,9},{9,8},{10,11... | collective-permute-start | bytes 24584 | tf_op jit(solution)/shard_map/ppermute | solution.py:473
  16.3 16.7 %collective-permute-start = (bf16[256,256]{1,0:T(8,128)(2,1)S(1)}, bf16[256,256]{1,0:T(8,128)(2,1)S(1)}, u32[]{:S(2)}, u32[]{:S(2)}) collective-permute-start(bf16[256,256]{1,0:T(8,128)(2,1)S(1)} %get-tuple-element.33), channel_id=1, source_target_pairs={{0,1},{1,0},{2,3},{3,2},{4,5},{5,4},{6,7},{7,6},{8,9},{9,8},{10,11... | collective-permute-start | bytes 393224 | tf_op jit(solution)/shard_map/ppermute | solution.py:473
  22.0 12.7 %collective-permute-start.7 = (f32[3,40,256]{2,1,0:T(8,128)S(1)}, f32[3,40,256]{2,1,0:T(8,128)S(1)}, u32[]{:S(2)}, u32[]{:S(2)}) collective-permute-start(f32[3,40,256]{2,1,0:T(8,128)S(1)} %shard_map.86.rest_0_.own), channel_id=1, source_target_pairs={{0,2},{2,0},{4,6},{6,4},{8,10},{10,8},{12,14},{14,12},{16,18},{18,... | collective-permute-start | bytes 368648 | tf_op jit(solution)/shard_map/ppermute | solution.py:469
  34.7 3.5 %collective-permute-start.6 = (f32[3,32,256]{2,1,0:T(8,128)S(1)}, f32[3,32,256]{2,1,0:T(8,128)S(1)}, u32[]{:S(2)}, u32[]{:S(2)}) collective-permute-start(f32[3,32,256]{2,1,0:T(8,128)S(1)} %shard_map.89.own), channel_id=1, source_target_pairs={{0,2},{2,0},{4,6},{6,4},{8,10},{10,8},{12,14},{14,12},{16,18},{18,... | collective-permute-start | bytes 294920 | tf_op jit(solution)/shard_map/ppermute | solution.py:469
  34.8 6.7 %collective-permute-start.8 = (f32[24,256]{1,0:T(8,128)S(1)}, f32[24,256]{1,0:T(8,128)S(1)}, u32[]{:S(2)}, u32[]{:S(2)}) collective-permute-start(f32[24,256]{1,0:T(8,128)S(1)} %get-tuple-element.52), channel_id=1, source_target_pairs={{0,4},{2,6},{4,8},{6,10},{8,12},{10,14},{12,16},{14,18},{16,20},{1... | collective-permute-start | bytes 73736 | tf_op jit(solution)/shard_map/ppermute | solution.py:491
  36.6 5.6 %collective-permute-start.9 = (f32[24,256]{1,0:T(8,128)S(1)}, f32[24,256]{1,0:T(8,128)S(1)}, u32[]{:S(2)}, u32[]{:S(2)}) collective-permute-start(f32[24,256]{1,0:T(8,128)S(1)} %get-tuple-element.53), channel_id=1, source_target_pairs={{0,8},{2,10},{4,12},{6,14},{8,16},{10,18},{12,20},{14,22},{16,24},... | collective-permute-start | bytes 73736 | tf_op jit(solution)/shard_map/ppermute | solution.py:492
  42.2 8.7 %collective-permute-start.10 = (f32[40,256]{1,0:T(8,128)S(1)}, f32[40,256]{1,0:T(8,128)S(1)}, u32[]{:S(2)}, u32[]{:S(2)}) collective-permute-start(f32[40,256]{1,0:T(8,128)S(1)} %get-tuple-element.54.here), channel_id=1, source_target_pairs={{0,1},{1,0},{2,3},{3,2},{4,5},{5,4},{6,7},{7,6},{8,9},{9,8},{10,11... | collective-permute-start | bytes 122888 | tf_op jit(solution)/shard_map/ppermute | solution.py:473
  43.8 7.1 %collective-permute-start.11 = (f32[32,256]{1,0:T(8,128)S(1)}, f32[32,256]{1,0:T(8,128)S(1)}, u32[]{:S(2)}, u32[]{:S(2)}) collective-permute-start(f32[32,256]{1,0:T(8,128)S(1)} %get-tuple-element.55), channel_id=1, source_target_pairs={{0,4},{1,5},{2,7},{3,6},{4,8},{5,9},{6,11},{7,10},{8,12},{9,13},{1... | collective-permute-start | bytes 98312 | tf_op jit(solution)/shard_map/ppermute | solution.py:483
  45.4 5.5 %collective-permute-start.12 = (bf16[32,256]{1,0:T(8,128)(2,1)S(1)}, bf16[32,256]{1,0:T(8,128)(2,1)S(1)}, u32[]{:S(2)}, u32[]{:S(2)}) collective-permute-start(bf16[32,256]{1,0:T(8,128)(2,1)S(1)} %get-tuple-element.56), channel_id=1, source_target_pairs={{0,8},{1,9},{2,11},{3,10},{4,12},{5,13},{6,15},{7,14},{8,16},{9,17... | collective-permute-start | bytes 49160 | tf_op jit(solution)/shard_map/ppermute | solution.py:483
  50.9 1.2 %collective-permute-start.13 = (f32[16,256]{1,0:T(8,128)S(1)}, f32[16,256]{1,0:T(8,128)S(1)}, u32[]{:S(2)}, u32[]{:S(2)}) collective-permute-start(f32[16,256]{1,0:T(8,128)S(1)} %get-tuple-element.58), channel_id=1, source_target_pairs={{0,2},{2,0},{4,6},{6,4},{8,10},{10,8},{12,14},{14,12},{16,18},{18,... | collective-permute-start | bytes 49160 | tf_op jit(solution)/shard_map/ppermute | solution.py:469
